TPU v7x, 256 devices: a whole 4x4x8 slice. The times are simulated.
256 devices in a mesh: mem: 16 (over z_hi, x, core), lev: 16 (over y, z_lo).
Axes of the slice: x: 4, y: 4, z: 8 (z_hi: 2, z_lo: 4; z = z_hi * 4 + z_lo), core: 2. Of those that a mesh axis runs over, the one named last changes fastest.
Arguments:
- alpha_weights: float32 [16, 32, 384, 512], P('mem', 'lev'), may hold values from -6 to 6
- perturbations: bfloat16 [16, 32, 393216], P('mem', None, 'lev'), may hold values from -6 to 6
- coef_x: float32 [384, 512], replicated, may hold values from 0.02 to 0.24
- coef_y: float32 [384, 512], replicated, may hold values from 0.02 to 0.24
- level_scale: float32 [32], replicated, may hold values from 0.3 to 1
- level_map: int32 [32], replicated, may hold values from 0 to 31, each once
- tile_widths: int32 [16], replicated, may hold values from 1 to 24576, 196608 in all
- band_widths: int32 [32], replicated, may hold values from 1 to 4, as said below
Outputs:
- increment: float32 [32, 393216], P('mem', 'lev')
Inputs may be any that keep to these rules, and one draw needn't show every extreme that they name: `level_map`: a permutation of the levels. `tile_widths`: sum to 196608; the largest equals 24576. `band_widths`: some level has a band of exactly 4.
All inputs are finite; a program needn't handle non-finite values.
Results may differ from a plain program's by a relative error of at most 0.0035.
Values may be sent and summed in bfloat16 or wider, within the bound.
No kernel may reach another device: no remote copies, remote signals or barrier semaphores. Data moves between devices by JAX's collectives and lax.ppermute only.
A program may use at most 64 MiB of HBM per device.

v0:
```python
import jax
import jax.numpy as jnp
from jax import lax
from jax.sharding import PartitionSpec as P

STEPS = 16


def diffuse_level(layer_field, scaled_x, scaled_y):

    def step_once(index_step, state):
        flux_x = scaled_x[:-1, :] * (state[1:, :] - state[:-1, :])
        flux_y = scaled_y[:, :-1] * (state[:, 1:] - state[:, :-1])
        zero_row = jnp.zeros((1, state.shape[1]), state.dtype)
        zero_col = jnp.zeros((state.shape[0], 1), state.dtype)
        change = jnp.concatenate([flux_x, zero_row], 0) - jnp.concatenate([zero_row, flux_x], 0)
        change = (
            change + jnp.concatenate([flux_y, zero_col], 1) - jnp.concatenate([zero_col, flux_y], 1)
        )
        return state + change

    return lax.fori_loop(0, STEPS, step_once, layer_field)


def vertical_matrix(band_widths):
    level_pos = jnp.arange(band_widths.shape[0])
    distance = jnp.abs(level_pos[:, None] - level_pos[None, :]).astype(jnp.float32)
    mutual = jnp.minimum(band_widths[:, None], band_widths[None, :]).astype(jnp.float32)
    return jnp.where(distance <= mutual, jnp.exp(-distance * distance / (mutual * mutual)), 0.0)


def body(
    alpha_weights, perturbations, coef_x, coef_y, level_scale, level_map, tile_widths, band_widths
):
    mem_dev, lev_dev, rows_x, rows_y = alpha_weights.shape
    levels = perturbations.shape[1]
    capacity = perturbations.shape[2]
    tile_count = lax.axis_size("lev")
    member_devices = lax.axis_size("mem")
    level_ids = jnp.arange(levels)
    slot_ids = lax.axis_index("lev") * lev_dev + jnp.arange(lev_dev)
    owned_levels = jnp.sum(
        jnp.where(slot_ids[:, None] == level_ids[None, :], level_map[None, :], 0), axis=1
    )
    level_gain = jnp.sum(
        jnp.where(owned_levels[:, None] == level_ids[None, :], level_scale[None, :], 0.0), axis=1
    )

    def smooth_slot(member_field, strength):
        return diffuse_level(member_field, coef_x * strength, coef_y * strength)

    smoothed = jax.vmap(jax.vmap(smooth_slot, (0, 0)), (0, None))(alpha_weights, level_gain)
    rounded = smoothed.astype(jnp.bfloat16).reshape(mem_dev, lev_dev, rows_x * rows_y)
    padded = jnp.pad(rounded, ((0, 0), (0, 0), (0, capacity)))
    starts = jnp.cumsum(tile_widths) - tile_widths

    def cut_tile(first_col):
        return lax.dynamic_slice_in_dim(padded, first_col, capacity, 2)

    outgoing = jax.vmap(cut_tile, out_axes=1)(starts)
    arrived = lax.all_to_all(outgoing, "lev", split_axis=1, concat_axis=1, tiled=True).reshape(
        mem_dev, levels, capacity
    )
    own_width = jnp.sum(jnp.where(jnp.arange(tile_count) == lax.axis_index("lev"), tile_widths, 0))
    valid_cols = jnp.arange(capacity) < own_width
    localizer = vertical_matrix(band_widths).astype(jnp.bfloat16)
    perm_onehot = (level_ids[:, None] == level_map[None, :]).astype(jnp.bfloat16)
    permuted = jnp.dot(localizer, perm_onehot, preferred_element_type=jnp.float32).astype(
        jnp.bfloat16
    )
    share_rows = levels // member_devices
    spread = jnp.einsum("ks,msc->mkc", permuted, arrived, preferred_element_type=jnp.float32)
    pert_rows = perturbations.astype(jnp.float32)
    summed = lax.psum(
        jnp.where(valid_cols[None, :], jnp.sum(pert_rows * spread, axis=0), 0.0), "mem"
    )
    result = lax.dynamic_slice_in_dim(summed, lax.axis_index("mem") * share_rows, share_rows, 0)
    return result


def solution(mesh):
    placed = (P("mem", "lev", None, None), P("mem", None, "lev"), P(), P(), P(), P(), P(), P())
    return jax.shard_map(
        body, mesh=mesh, in_specs=placed, out_specs=P("mem", "lev"), check_vma=False
    )
```

profile of v0, /device:TPU:1, one launch (start us, length us, event | category | flops | bytes accessed | tf_op | source)
XLA Modules:
  0.0 338.7 jit_solution(3615929898913939918)
XLA Ops:
  7.6 3.1 broadcast_multiply_fusion
  10.7 44.0 %while.11 = (s32[]{:T(128)}, f32[1,2,384,512]{3,2,1,0:T(8,128)S(1)}, f32[2,384,512]{2,1,0:T(8,128)}, f32[2,384,512]{2,1,0:T(8,128)S(1)}, s32[]{:T(128)}) while((s32[]{:T(128)}, f32[1,2,384,512]{3,2,1,0:T(8,128)S(1)}, f32[2,384,512]{2,1,0:T(8,128)}, f32[2,384,512]{2,1,0:T(8,128)S(1)}, s32[]{:T(128)}) %tuple.39), condition=%wide.region_4.5_spmd, body=%wide.region_3.4_spmd.sunk | while | flops 3142146 | bytes 25130072 | solution.py:22
  11.2 0.9 copy-done.1
  12.5 0.9 subtract_add_fusion.2
  14.0 0.9 copy-done.1
  15.2 0.9 subtract_add_fusion.2
  16.7 0.9 copy-done.1
  18.0 0.9 subtract_add_fusion.2
  20.7 0.9 subtract_add_fusion.2
  23.5 0.9 subtract_add_fusion.2
  25.0 0.9 copy-done.1
  26.2 0.9 subtract_add_fusion.2
  29.0 0.9 subtract_add_fusion.2
  30.5 0.9 copy-done.1
  31.8 0.9 subtract_add_fusion.2
  34.5 0.9 subtract_add_fusion.2
  37.3 0.9 subtract_add_fusion.2
  38.7 0.9 copy-done.1
  40.0 0.9 subtract_add_fusion.2
  42.8 0.9 subtract_add_fusion.2
  45.5 0.9 subtract_add_fusion.2
  47.0 0.9 copy-done.1
  48.3 0.9 subtract_add_fusion.2
  51.0 0.9 subtract_add_fusion.2
  53.8 0.9 subtract_add_fusion.2
  56.3 1.4 pad.9
  57.7 33.7 %while.12 = (s32[]{:T(128)}, bf16[1,2,221184]{2,1,0:T(2,128)(2,1)S(1)}, s32[16,3]{0,1:T(4,128)S(1)}, bf16[16,1,2,24576]{3,2,1,0:T(2,128)(2,1)}, s32[]{:T(128)}) while((s32[]{:T(128)}, bf16[1,2,221184]{2,1,0:T(2,128)(2,1)S(1)}, s32[16,3]{0,1:T(4,128)S(1)}, bf16[16,1,2,24576]{3,2,1,0:T(2,128)(2,1)}, s32[]{:T(128)}) %tuple.34), condition=%wide.while_cond, body=%wide.while_body.sunk | while | flops 2 | bytes 197729 | solution.py:58
  58.4 1.4 bitcast_dynamic-update-slice_fusion.2
  60.5 1.4 bitcast_dynamic-update-slice_fusion.2
  62.6 1.4 bitcast_dynamic-update-slice_fusion.2
  64.7 1.5 bitcast_dynamic-update-slice_fusion.2
  66.8 1.4 bitcast_dynamic-update-slice_fusion.2
  68.9 1.4 bitcast_dynamic-update-slice_fusion.2
  71.0 1.4 bitcast_dynamic-update-slice_fusion.2
  73.1 1.4 bitcast_dynamic-update-slice_fusion.2
  75.2 1.4 bitcast_dynamic-update-slice_fusion.2
  77.3 1.4 bitcast_dynamic-update-slice_fusion.2
  79.4 1.4 bitcast_dynamic-update-slice_fusion.2
  81.5 1.4 bitcast_dynamic-update-slice_fusion.2
  83.6 1.4 bitcast_dynamic-update-slice_fusion.2
  85.8 1.4 bitcast_dynamic-update-slice_fusion.2
  87.8 1.4 bitcast_dynamic-update-slice_fusion.2
  90.0 1.4 bitcast_dynamic-update-slice_fusion.2
  91.4 9.2 %all-to-all-start = ((bf16[1,16,2,24576]{3,2,0,1:T(2,128)(2,1)}), bf16[1,16,2,24576]{3,2,0,1:T(2,128)(2,1)S(1)}, u32[]{:S(2)}, u32[]{:S(2)}) async-start(bf16[1,16,2,24576]{3,2,0,1:T(2,128)(2,1)} %bitcast.4), calls=%async_computation | async-start | bytes 3145728 | tf_op jit(solution)/shard_map/all_to_all | solution.py:61
  101.3 37.9 %all-to-all-done = bf16[1,16,2,24576]{3,2,0,1:T(2,128)(2,1)S(1)} async-done(((bf16[1,16,2,24576]{3,2,0,1:T(2,128)(2,1)}), bf16[1,16,2,24576]{3,2,0,1:T(2,128)(2,1)S(1)}, u32[]{:S(2)}, u32[]{:S(2)}) %all-to-all-start) | async-done | bytes 1572896 | tf_op jit(solution)/shard_map/all_to_all | solution.py:61
  139.8 3.9 %fusion.2 = f32[32,24576]{1,0:T(8,128)} fusion(bf16[32,24576]{1,0:T(8,128)(2,1)S(1)} %reshape.55, bf16[1,32,24576]{2,1,0:T(8,128)(2,1)} %param.11, pred[24576]{0:T(1024)(128)(4,1)S(1)} %iota_compare_fusion, s32[32]{0:T(128)S(1)} %copy-done.4, s32[32]{0:T(128)S(1)} %copy-done.3), kind=kOutput, calls=%fused_computation.8 | convolution fusion | flops 52770816 | bytes 6316288 | tf_op jit(solution)/shard_map/ks,msc->mkc/dot_general | solution.py:72
  143.7 186.3 %all-reduce.8.cloned.1.call-done = f32[32,24576]{1,0:T(8,128)} async-done(((f32[32,24576]{1,0:T(8,128)}), f32[32,24576]{1,0:T(8,128)}) %all-reduce.8.cloned.1.call-update) | async-done | bytes 3145744 | tf_op jit(solution)/shard_map/psum | solution.py:74
  330.0 1.9 constant_dynamic-slice_fusion.1
  (114 shorter events, 36.5 us)
Async XLA Ops:
  6.5 0.9 copy-start.5
  6.5 0.7 copy-start.4
  7.6 3.1 copy-start
  10.7 1.4 copy-start.1
  13.5 1.4 copy-start.1
  16.2 1.4 copy-start.1
  19.0 1.4 copy-start.1
  21.7 1.4 copy-start.1
  24.5 1.4 copy-start.1
  27.2 1.4 copy-start.1
  30.0 1.4 copy-start.1
  32.7 1.4 copy-start.1
  35.5 1.4 copy-start.1
  38.2 1.4 copy-start.1
  41.0 1.4 copy-start.1
  43.7 1.4 copy-start.1
  46.5 1.4 copy-start.1
  49.2 1.4 copy-start.1
  52.0 1.4 copy-start.1
  54.7 0.7 copy-start.2
  91.4 47.8 %all-to-all-start = ((bf16[1,16,2,24576]{3,2,0,1:T(2,128)(2,1)}), bf16[1,16,2,24576]{3,2,0,1:T(2,128)(2,1)S(1)}, u32[]{:S(2)}, u32[]{:S(2)}) async-start(bf16[1,16,2,24576]{3,2,0,1:T(2,128)(2,1)} %bitcast.4), calls=%async_computation | async-start | bytes 3145728 | tf_op jit(solution)/shard_map/all_to_all | solution.py:61
  100.6 229.4 %all-reduce.8.cloned.1.call-start = ((), (), s32[]{:S(2)}) async-start(), calls=%async_computation.1 | async-start | bytes 6291456 | tf_op jit(solution)/shard_map/psum | solution.py:74
  101.3 38.5 %copy-start.3 = (s32[32]{0:T(128)S(1)}, s32[32]{0:T(128)}, u32[]{:S(2)}) copy-start(s32[32]{0:T(128)} %param.17) | copy-start | bytes 388
Sparse Core Ops, SparseCore 0:
  143.8 186.1 all-reduce.7
where the time goes:
time: 340 us; the launch traced here: 339 us
  waiting for transfers between devices  224 us (66%)
  local copies, waits for them, and re-layouts  53.2 us (16%)
  other arithmetic  34.1 us (10%)
  between operations  13.5 us (4%)
  starting transfers between devices  9.22 us (3%)
  matrix products  3.87 us (1%)
    psum x1, waiting for transfers between devices, body(): lax.psum(jnp.where(valid_cols[None, :], jnp.sum(pert_rows * spread, axis=...  186 us
    all_to_all x1, waiting for transfers between devices, body(): lax.all_to_all(outgoing, 'lev', split_axis=1, concat_axis=1, tiled=True)  37.9 us
    gather x48, local copies, waits for them, and re-layouts  33.6 us
    add x16, other arithmetic, step_once(): return state + change  15.1 us
    while x32, local copies, waits for them, and re-layouts  14.3 us
    all_to_all x1, starting transfers between devices, body(): lax.all_to_all(outgoing, 'lev', split_axis=1, concat_axis=1, tiled=True)  9.17 us
    mul x16, other arithmetic, step_once(): flux_y = scaled_y[:, :-1] * (state[:, 1:] - state[:, :-1])  8.01 us
  transfers between devices with their start and end apart: 2, of which 2 were waited for; matrix products, arithmetic and copies ran while one was open for 0% of the time, Pallas kernels for 0%

commit v1 on v0

v1 whole, which is shorter than its diff:
```python
import jax
import jax.numpy as jnp
from jax import lax
from jax.experimental import pallas as pl
from jax.experimental.pallas import tpu as pltpu
from jax.sharding import PartitionSpec as P

STEPS = 16
LANES = 128
SUBS = 8
ROWS_PER_BLOCK = 8
CORES, RING, HALVES = 2, 4, 2


def split_bf16(x):
    high = x.astype(jnp.bfloat16)
    return high, (x - high.astype(jnp.float32)).astype(jnp.bfloat16)


def diffuse_kernel(
    place_ref, scale_ref, map_ref, width_ref, alpha_ref, cx_ref, cy_ref, spread_ref, gather_ref,
    out_ref, raw_scr, cx_scr, cy_scr, x_scr, f_scr, gx_scr, gy_scr, ax_scr, ay_scr, ayr_scr, o_scr,
    msg_scr, sems, out_sem,
):
    rows, cols = cx_ref.shape
    levels = alpha_ref.shape[1]
    fold = rows // SUBS
    blocks = cols // LANES
    tiles, _, length = out_ref.shape

    def part(b):
        return pl.ds(b * LANES, LANES)

    copies = []
    for b in range(blocks):
        one = [
            pltpu.make_async_copy(cx_ref.at[:, part(b)], cx_scr.at[b], sems.at[b, 0]),
            pltpu.make_async_copy(cy_ref.at[:, part(b)], cy_scr.at[b], sems.at[b, 1]),
        ]
        for v in range(levels):
            one.append(
                pltpu.make_async_copy(
                    alpha_ref.at[0, v, :, part(b)], raw_scr.at[v, b], sems.at[b, 2 + v]
                )
            )
        copies.append(one)
    for k in range(2 + levels):
        for b in range(blocks):
            copies[b][k].start()

    def spread_columns(planes):
        for r in range(fold):
            for b in range(blocks):
                x_scr[pl.ds(r * SUBS, SUBS), part(b)] = planes[b, pl.ds(r, SUBS, stride=fold), :]
        high, low = split_bf16(x_scr[...])
        return jnp.dot(high, spread_ref[...], preferred_element_type=jnp.float32) + jnp.dot(
            low, spread_ref[...], preferred_element_type=jnp.float32
        )

    lane = lax.broadcasted_iota(jnp.int32, (SUBS, LANES), 1)
    sub = lax.broadcasted_iota(jnp.int32, (SUBS, LANES), 0)
    for b in range(blocks):
        copies[b][0].wait()
    gx_scr[...] = spread_columns(cx_scr)
    for b in range(blocks):
        copies[b][1].wait()
    gy_scr[...] = spread_columns(cy_scr)

    def at(r):
        return pl.ds(r * SUBS, SUBS)

    for v in range(levels):
        gain = scale_ref[map_ref[place_ref[0] * levels + v]]
        for b in range(blocks):
            copies[b][2 + v].wait()
        f_scr[pl.ds(0, rows), :] = spread_columns(raw_scr.at[v])
        for r in range(fold):
            for b in range(blocks):
                ax = gx_scr[at(r), part(b)] * gain
                ay = gy_scr[at(r), part(b)] * gain
                if r == fold - 1:
                    ax = jnp.where(sub == SUBS - 1, 0.0, ax)
                if b == blocks - 1:
                    ay = jnp.where(lane == LANES - 1, 0.0, ay)
                    ayr_scr[at(r), :] = pltpu.roll(ay, 1, 1)
                ax_scr[at(r), part(b)] = ax
                ay_scr[at(r), part(b)] = ay

        @pl.loop(0, STEPS)
        def _(step):
            wrap = [pltpu.roll(f_scr[at(0), part(b)], SUBS - 1, 0) for b in range(blocks)]
            for b in range(blocks):
                f_scr[at(fold), part(b)] = wrap[b]
            here = [f_scr[at(fold - 1), part(b)] for b in range(blocks)]
            before = [
                pltpu.roll(ax_scr[at(fold - 1), part(b)] * (wrap[b] - here[b]), 1, 0)
                for b in range(blocks)
            ]
            here = [f_scr[at(0), part(b)] for b in range(blocks)]
            for r in range(fold):
                after = [f_scr[at(r + 1), part(b)] for b in range(blocks)]
                right = pltpu.roll(here[0], LANES - 1, 1)
                left = pltpu.roll(here[blocks - 1], 1, 1)
                last_y = ayr_scr[at(r), :] * (here[0] - left)
                flux = []
                for b in range(blocks):
                    fx = ax_scr[at(r), part(b)] * (after[b] - here[b])
                    beside = here[b + 1] if b < blocks - 1 else right
                    fy = ay_scr[at(r), part(b)] * (beside - here[b])
                    f_scr[at(r), part(b)] = here[b] + (fx - before[b]) + (fy - last_y)
                    last_y = fy
                    flux.append(fx)
                here, before = after, flux

        x_scr[...] = jnp.dot(
            f_scr[pl.ds(0, rows), :].astype(jnp.bfloat16),
            gather_ref[...],
            preferred_element_type=jnp.float32,
        )
        for r in range(fold):
            for b in range(blocks):
                o_scr[pl.ds(r * SUBS + b * levels + v, SUBS, stride=rows), :] = x_scr[at(r), part(b)]

    for i in range(rows):
        msg_scr[:, part(i)] = o_scr[at(i), :].astype(jnp.bfloat16)
    spare = msg_scr.shape[1] - rows * LANES
    msg_scr[:, pl.ds(rows * LANES, spare)] = jnp.zeros((SUBS, spare), jnp.bfloat16)
    first_col = 0
    sends = []
    for t in range(tiles):
        first = pl.multiple_of(first_col // cols * LANES, LANES)
        sends.append(
            pltpu.make_async_copy(
                msg_scr.at[:, pl.ds(first, length)], out_ref.at[t], out_sem.at[t]
            )
        )
        sends[-1].start()
        first_col = first_col + width_ref[t]
    for one in sends:
        one.wait()


def smooth_and_cut(place, level_scale, level_map, tile_widths, alpha, coef_x, coef_y, capacity):
    _, levels, rows, cols = alpha.shape
    tiles = tile_widths.shape[0]
    blocks = cols // LANES
    assert levels * blocks == SUBS and rows % SUBS == 0
    tile_rows = pl.cdiv(capacity, cols) + 1
    length = tile_rows * LANES
    natural = lax.broadcasted_iota(jnp.int32, (cols, cols), 0)
    spaced = lax.broadcasted_iota(jnp.int32, (cols, cols), 1)
    spread = (natural == spaced % LANES * blocks + spaced // LANES).astype(jnp.bfloat16)
    anywhere = pl.BlockSpec(memory_space=pl.ANY)
    scalars = pl.BlockSpec(memory_space=pltpu.SMEM)
    vector = pl.BlockSpec(memory_space=pltpu.VMEM)
    plane = pltpu.VMEM((blocks, rows, LANES), jnp.float32)
    whole = pltpu.VMEM((rows, cols), jnp.float32)
    return pl.pallas_call(
        diffuse_kernel,
        out_shape=jax.ShapeDtypeStruct((tiles, SUBS, length), jnp.bfloat16),
        in_specs=[scalars] * 4 + [anywhere] * 3 + [vector] * 2,
        out_specs=anywhere,
        scratch_shapes=[
            pltpu.VMEM((levels, blocks, rows, LANES), jnp.float32),
            plane,
            plane,
            whole,
            pltpu.VMEM((rows + SUBS, cols), jnp.float32),
            whole,
            whole,
            whole,
            whole,
            pltpu.VMEM((rows, LANES), jnp.float32),
            pltpu.VMEM((rows * SUBS, LANES), jnp.float32),
            pltpu.VMEM((SUBS, (rows + tile_rows) * LANES), jnp.bfloat16),
            pltpu.SemaphoreType.DMA((blocks, 2 + levels)),
            pltpu.SemaphoreType.DMA((tiles,)),
        ],
        name="diffuse",
    )(place, level_scale, level_map, tile_widths, alpha, coef_x, coef_y, spread, spread.T)


def localize_kernel(place_ref, width_ref, x_ref, weight_ref, order_ref, pert_ref, own_ref, send_ref, s_scr):
    step = pl.program_id(0)
    tiles = width_ref.shape[0]
    levels = order_ref.shape[0]
    blocks = weight_ref.shape[0] // levels
    cols = blocks * LANES
    chunk = pert_ref.shape[2]
    count = chunk // cols
    me = place_ref[0]
    first_col = 0
    for t in range(tiles):
        first_col = first_col + jnp.where(t < me, width_ref[t], 0)
    shift = first_col % cols
    shift_blocks = shift // LANES
    shift_lanes = shift % LANES
    width = width_ref[me] - step * chunk
    begin = pl.multiple_of(step * (count * LANES), LANES)
    spread = jnp.dot(
        weight_ref[...],
        x_ref[:, pl.ds(begin, (count + 1) * LANES)],
        preferred_element_type=jnp.float32,
    )
    for r in range(count + 1):
        for b in range(blocks):
            s_scr[:, pl.ds((r * blocks + b) * LANES, LANES)] = spread[
                b * levels : (b + 1) * levels, r * LANES : (r + 1) * LANES
            ]
    ordered = jnp.dot(order_ref[...], pert_ref[0], preferred_element_type=jnp.float32)
    lane = lax.broadcasted_iota(jnp.int32, (levels, LANES), 1)
    keep = lane < LANES - shift_lanes
    half = levels // 2

    def rolled(k):
        block = s_scr[:, pl.ds(pl.multiple_of((k + shift_blocks) * LANES, LANES), LANES)]
        return pltpu.roll(block, lax.rem(LANES - shift_lanes, LANES), 1)

    here = rolled(0)
    for k in range(count * blocks):
        after = rolled(k + 1)
        at = jnp.where(keep, here, after)
        part = pl.ds(k * LANES, LANES)
        value = ordered[:, k * LANES : (k + 1) * LANES] * at
        value = jnp.where(lane < width - k * LANES, value, 0.0).astype(jnp.bfloat16)
        own_ref[:, part] = value[:half]
        send_ref[:, part] = value[half:]
        here = after


def localize(place, tile_widths, arrived, weight, order, perturbations):
    _, levels, capacity = perturbations.shape
    blocks = weight.shape[0] // levels
    cols = blocks * LANES
    chunk = ROWS_PER_BLOCK * cols
    assert capacity % chunk == 0
    scalars = pl.BlockSpec(memory_space=pltpu.SMEM)
    vector = pl.BlockSpec(memory_space=pltpu.VMEM)
    half = jax.ShapeDtypeStruct((levels // 2, capacity), jnp.bfloat16)
    half_spec = pl.BlockSpec((levels // 2, chunk), lambda i: (0, i))
    return pl.pallas_call(
        localize_kernel,
        grid=(capacity // chunk,),
        out_shape=(half, half),
        in_specs=[scalars, scalars, vector, vector, vector,
                  pl.BlockSpec((1, levels, chunk), lambda i: (0, 0, i))],
        out_specs=(half_spec, half_spec),
        scratch_shapes=[pltpu.VMEM((levels, chunk + 2 * cols), jnp.float32)],
        name="localize",
    )(place, tile_widths, arrived, weight, order, perturbations)


def body(
    alpha_weights, perturbations, coef_x, coef_y, level_scale, level_map, tile_widths, band_widths
):
    _, lev_dev, rows, cols = alpha_weights.shape
    _, levels, capacity = perturbations.shape
    blocks = cols // LANES
    tiles = tile_widths.shape[0]
    mem = lax.axis_index("mem")
    place = lax.axis_index("lev").astype(jnp.int32).reshape(1)

    outgoing = smooth_and_cut(
        place, level_scale, level_map, tile_widths, alpha_weights, coef_x, coef_y, capacity
    )
    arrived = lax.all_to_all(outgoing, "lev", split_axis=0, concat_axis=0, tiled=True)
    arrived = arrived.reshape(tiles * SUBS, -1)

    slot = jnp.arange(levels)
    core = (mem + slot // 16) % CORES
    ring = (mem // CORES + slot // 4) % RING
    half = (mem // (CORES * RING) + slot // 2) % HALVES
    row_level = half * 16 + ring * 4 + core * 2 + slot % 2
    order = (row_level[:, None] == slot[None, :]).astype(jnp.bfloat16)
    row_band = jnp.sum(jnp.where(row_level[:, None] == slot[None, :], band_widths[None, :], 0), 1)
    col_band = jnp.sum(jnp.where(level_map[:, None] == slot[None, :], band_widths[None, :], 0), 1)
    distance = jnp.abs(row_level[:, None] - level_map[None, :]).astype(jnp.float32)
    mutual = jnp.minimum(row_band[:, None], col_band[None, :]).astype(jnp.float32)
    local = jnp.where(distance <= mutual, jnp.exp(-distance * distance / (mutual * mutual)), 0.0)
    same_block = (jnp.arange(blocks)[:, None] == jnp.arange(blocks)[None, :])[:, None, None, :, None]
    weight = jnp.where(same_block, local.reshape(1, levels, tiles, 1, lev_dev), 0.0)
    weight = weight.astype(jnp.bfloat16).reshape(blocks * levels, tiles * SUBS)

    own, other = localize(place, tile_widths, arrived, weight, order, perturbations)

    def wide(x):
        return x.astype(jnp.float32)

    members = CORES * RING * HALVES
    came = lax.ppermute(other, "mem", [(i, i ^ 1) for i in range(members)])
    pair = (wide(own) + wide(came)).astype(jnp.bfloat16).reshape(RING, 4, capacity)
    total = wide(pair[0])
    for d in range(1, RING):
        ring_perm = [
            (z * 8 + x * 2 + c, z * 8 + (x + d) % RING * 2 + c)
            for z in range(HALVES)
            for x in range(RING)
            for c in range(CORES)
        ]
        total = total + wide(lax.ppermute(pair[d], "mem", ring_perm))
    came = lax.ppermute(
        total[2:].astype(jnp.bfloat16), "mem", [(i, (i + 8) % members) for i in range(members)]
    )
    return total[:2] + wide(came)


def solution(mesh):
    placed = (P("mem", "lev", None, None), P("mem", None, "lev"), P(), P(), P(), P(), P(), P())
    return jax.shard_map(
        body, mesh=mesh, in_specs=placed, out_specs=P("mem", "lev"), check_vma=False
    )
```

time: 340 us -> 105 us (0.31)
  waiting for transfers between devices: 224 us -> 56.3 us
  local copies, waits for them, and re-layouts: 53.2 us -> 2.53 us
  other arithmetic: 34.1 us -> 4.92 us
  Pallas kernels: 0 us -> 22.1 us
  between operations: 13.5 us -> 0.13 us
  starting transfers between devices: 9.22 us -> 18.6 us
  matrix products: 3.87 us -> 0 us
    psum x1 -> x0, waiting for transfers between devices: 186 us -> none  [body(): lax.psum(jnp.where(valid_cols[None, :], jnp.sum(pert_rows * spread, axis=...]
    gather x48 -> x0, local copies, waits for them, and re-layouts: 33.6 us -> none
    pallas_call x0 -> x2, Pallas kernels: none -> 22.1 us  [the longest x1 15.8 us: smooth_and_cut(): pl.pallas_call(diffuse_kernel, out_shape=jax.ShapeDtypeStruct((tiles, SUB...]
    ppermute x0 -> x5, waiting for transfers between devices: none -> 19.2 us  [the longest x3 11.4 us: body(): total = total + wide(lax.ppermute(pair[d], 'mem', ring_perm))]
    mul x33 -> x0, other arithmetic: 17.1 us -> none  [the longest x16 8.01 us: step_once(): flux_y = scaled_y[:, :-1] * (state[:, 1:] - state[:, :-1])]
    while x32 -> x0, local copies, waits for them, and re-layouts: 14.3 us -> none
    add x17 -> x4, other arithmetic: 15.1 us -> 1 us  [the longest x1 0.79 us: body(): return total[:2] + wide(came)]
    ppermute x0 -> x5, starting transfers between devices: none -> 9.38 us  [the longest x1 4.3 us: body(): lax.ppermute(total[2:].astype(jnp.bfloat16), 'mem', [(i, (i + 8) % member...]
  transfers between devices with their start and end apart: 2 -> 6, of which waited for: 2 -> 5; matrix products, arithmetic and copies ran while one was open for 0% -> 2% of each run, Pallas kernels for 0% -> 0%
where the time goes in v1:
time: 105 us; the launch traced here: 104 us
  waiting for transfers between devices  56.3 us (54%)
  Pallas kernels  22.1 us (21%)
  starting transfers between devices  18.6 us (18%)
  other arithmetic  4.92 us (5%)
  local copies, waits for them, and re-layouts  2.53 us (2%)
    all_to_all x1, waiting for transfers between devices, body(): lax.all_to_all(outgoing, 'lev', split_axis=0, concat_axis=0, tiled=True)  37.1 us
    pallas_call x1, Pallas kernels, smooth_and_cut(): pl.pallas_call(diffuse_kernel, out_shape=jax.ShapeDtypeStruct((tiles, SUB...  15.8 us
    ppermute x3, waiting for transfers between devices, body(): total = total + wide(lax.ppermute(pair[d], 'mem', ring_perm))  11.4 us
    all_to_all x1, starting transfers between devices, body(): lax.all_to_all(outgoing, 'lev', split_axis=0, concat_axis=0, tiled=True)  9.19 us
    pallas_call x1, Pallas kernels, localize(): pl.pallas_call(localize_kernel, grid=(capacity // chunk,), out_shape=(hal...  6.32 us
    ppermute x1, waiting for transfers between devices, body(): lax.ppermute(total[2:].astype(jnp.bfloat16), 'mem', [(i, (i + 8) % member...  5.62 us
    ppermute x1, starting transfers between devices, body(): lax.ppermute(total[2:].astype(jnp.bfloat16), 'mem', [(i, (i + 8) % member...  4.3 us
    ppermute x3, starting transfers between devices, body(): total = total + wide(lax.ppermute(pair[d], 'mem', ring_perm))  3.69 us
  transfers between devices with their start and end apart: 6, of which 5 were waited for; matrix products, arithmetic and copies ran while one was open for 2% of the time, Pallas kernels for 0%

profile of v1, /device:TPU:1, one launch (start us, length us, event | category | flops | bytes accessed | tf_op | source)
XLA Modules:
  0.0 104.5 jit_solution(17095313186897204483)
XLA Ops:
  0.0 1.5 %fusion.1 = (bf16[512,512]{1,0:T(8,128)(2,1)}, bf16[512,512]{1,0:T(8,128)(2,1)}) fusion(s32[512]{0:T(512)S(1)} %get-tuple-element.16, s32[512]{0:T(512)S(1)} %get-tuple-element.19, s32[512]{0:T(512)S(1)} %get-tuple-element.17, s32[512]{0:T(512)S(1)} %get-tuple-element.18, pred[512]{0:T(512)(128)(4,1)S(1)} %get-tuple-element.20, ...), kind=kLoop, calls=%fused_computation.4 | loop fusion | flops 3145728 | bytes 1057792 | tf_op jit(solution)/shard_map/convert_element_type | solution.py:152
  1.5 15.8 %diffuse.1 = bf16[16,8,6272]{2,1,0:T(8,128)(2,1)} custom-call(s32[1]{0:T(128)} %bitcast.place_ref, f32[32]{0:T(128)} %scale_ref.1, s32[32]{0:T(128)} %map_ref.1, s32[16]{0:T(128)} %width_ref.3, f32[1,2,384,512]{3,2,1,0:T(8,128)} %alpha_ref.1, f32[384,512]{1,0:T(8,128)} %cx_ref.1, f32[384,512]{1,0:T(8,128)} %cy_ref.1, ...), custom_call_target="tpu_custom_call" | custom-call | tf_op jit(solution)/shard_map/diffuse/pallas_call | solution.py:158
  17.3 0.0 copy-start.1
  17.3 0.0 copy-start.2
  17.3 9.2 %all-to-all-start = ((bf16[16,8,6272]{2,1,0:T(8,128)(2,1)}), bf16[16,8,6272]{2,1,0:T(8,128)(2,1)S(1)}, u32[]{:S(2)}, u32[]{:S(2)}) async-start(bf16[16,8,6272]{2,1,0:T(8,128)(2,1)} %diffuse.1), calls=%async_computation | async-start | bytes 3211264 | tf_op jit(solution)/shard_map/all_to_all | solution.py:266
  26.5 0.0 copy-done.1
  26.5 0.1 sub.58
  26.6 0.0 copy-done.2
  26.7 0.2 select_reduce_fusion.1
  26.8 0.1 min.20
  26.9 0.1 compare_select_fusion
  27.1 0.1 select_convert_fusion
  27.2 0.1 convert_element_type.59
  27.3 0.7 copy.9.weight_ref
  28.0 0.7 fusion.3.order_ref
  28.7 37.1 %all-to-all-done = bf16[16,8,6272]{2,1,0:T(8,128)(2,1)S(1)} async-done(((bf16[16,8,6272]{2,1,0:T(8,128)(2,1)}), bf16[16,8,6272]{2,1,0:T(8,128)(2,1)S(1)}, u32[]{:S(2)}, u32[]{:S(2)}) %all-to-all-start) | async-done | bytes 1605664 | tf_op jit(solution)/shard_map/all_to_all | solution.py:266
  65.8 0.0 copy-start
  65.8 1.2 %copy-done = bf16[16,8,6272]{2,1,0:T(8,128)(2,1)} copy-done((bf16[16,8,6272]{2,1,0:T(8,128)(2,1)}, bf16[16,8,6272]{2,1,0:T(8,128)(2,1)S(1)}, u32[]{:S(2)}) %copy-start) | copy-done | bytes 1605656
  67.0 6.3 %localize.1 = (bf16[16,24576]{1,0:T(8,128)(2,1)}, bf16[16,24576]{1,0:T(8,128)(2,1)}) custom-call(s32[1]{0:T(128)} %bitcast.place_ref, s32[16]{0:T(128)} %width_ref.3, bf16[128,6272]{1,0:T(8,128)(2,1)} %bitcast.4, bf16[128,128]{1,0:T(8,128)(2,1)} %copy.9.weight_ref, bf16[32,32]{1,0:T(8,128)(2,1)} %fusion.3.order_ref, bf16[1,32,24576]{2,1,0:T(8,128)(2,1)} %pert_ref.1), custom_call_target="tpu_custom_call" | custom-call | tf_op jit(solution)/shard_map/localize/pallas_call | solution.py:241
  73.3 1.4 %collective-permute-start = (bf16[16,24576]{1,0:T(8,128)(2,1)}, bf16[16,24576]{1,0:T(8,128)(2,1)S(1)}, u32[]{:S(2)}, u32[]{:S(2)}) collective-permute-start(bf16[16,24576]{1,0:T(8,128)(2,1)} %get-tuple-element.8), channel_id=1, source_target_pairs={{0,16},{16,0},{32,48},{48,32},{64,80},{80,64},{96,112},{112,96},{1... | collective-permute-start | bytes 2359304 | tf_op jit(solution)/shard_map/ppermute | solution.py:290
  74.7 2.1 %collective-permute-done = bf16[16,24576]{1,0:T(8,128)(2,1)S(1)} collective-permute-done((bf16[16,24576]{1,0:T(8,128)(2,1)}, bf16[16,24576]{1,0:T(8,128)(2,1)S(1)}, u32[]{:S(2)}, u32[]{:S(2)}) %collective-permute-start) | collective-permute-done | bytes 786464 | tf_op jit(solution)/shard_map/ppermute | solution.py:290
  76.8 1.3 %add_convert_fusion = bf16[16,24576]{1,0:T(8,128)(2,1)S(1)} fusion(bf16[16,24576]{1,0:T(8,128)(2,1)S(1)} %collective-permute-done, bf16[16,24576]{1,0:T(8,128)(2,1)} %get-tuple-element.7), kind=kLoop, calls=%fused_computation | loop fusion | flops 1572864 | bytes 2359296 | tf_op jit(solution)/shard_map/convert_element_type | solution.py:291
  78.1 0.2 fusion.23
  78.4 2.6 %collective-permute-start.3 = (bf16[4,24576]{1,0:T(4,128)(2,1)S(1)}, bf16[4,24576]{1,0:T(4,128)(2,1)S(1)}, u32[]{:S(2)}, u32[]{:S(2)}) collective-permute-start(bf16[4,24576]{1,0:T(4,128)(2,1)S(1)} %get-tuple-element.12), channel_id=1, source_target_pairs={{0,96},{16,112},{32,0},{48,16},{64,32},{80,48},{96,64},{112,80},{1... | collective-permute-start | bytes 589832 | tf_op jit(solution)/shard_map/ppermute | solution.py:300
  80.9 0.5 collective-permute-start.2
  81.4 0.6 collective-permute-start.1
  82.1 6.8 %collective-permute-done.3 = bf16[4,24576]{1,0:T(4,128)(2,1)S(1)} collective-permute-done((bf16[4,24576]{1,0:T(4,128)(2,1)S(1)}, bf16[4,24576]{1,0:T(4,128)(2,1)S(1)}, u32[]{:S(2)}, u32[]{:S(2)}) %collective-permute-start.3) | collective-permute-done | bytes 196640 | tf_op jit(solution)/shard_map/ppermute | solution.py:300
  88.9 0.0 collective-permute-done.2
  88.9 4.6 %collective-permute-done.1 = bf16[4,24576]{1,0:T(4,128)(2,1)S(1)} collective-permute-done((bf16[4,24576]{1,0:T(4,128)(2,1)S(1)}, bf16[4,24576]{1,0:T(4,128)(2,1)S(1)}, u32[]{:S(2)}, u32[]{:S(2)}) %collective-permute-start.1) | collective-permute-done | bytes 196640 | tf_op jit(solution)/shard_map/ppermute | solution.py:300
  93.5 0.2 convert_add_fusion
  93.7 0.1 slice.38
  93.8 4.3 %collective-permute-start.4 = (bf16[2,24576]{1,0:T(2,128)(2,1)S(1)}, bf16[2,24576]{1,0:T(2,128)(2,1)S(1)}, u32[]{:S(2)}, u32[]{:S(2)}) collective-permute-start(bf16[2,24576]{1,0:T(2,128)(2,1)S(1)} %slice.38), channel_id=1, source_target_pairs={{0,128},{16,144},{32,160},{48,176},{64,192},{80,208},{96,224},{112... | collective-permute-start | bytes 294920 | tf_op jit(solution)/shard_map/ppermute | solution.py:301
  98.1 5.6 %collective-permute-done.4 = bf16[2,24576]{1,0:T(2,128)(2,1)S(1)} collective-permute-done((bf16[2,24576]{1,0:T(2,128)(2,1)S(1)}, bf16[2,24576]{1,0:T(2,128)(2,1)S(1)}, u32[]{:S(2)}, u32[]{:S(2)}) %collective-permute-start.4) | collective-permute-done | bytes 98336 | tf_op jit(solution)/shard_map/ppermute | solution.py:301
  103.7 0.8 slice_add_fusion
  (5 shorter events, 0.0 us)
Async XLA Ops:
  17.3 9.2 %copy-start.1 = (s32[32]{0:T(128)S(1)}, s32[32]{0:T(128)}, u32[]{:S(2)}) copy-start(s32[32]{0:T(128)} %map_ref.1) | copy-start | bytes 388
  17.3 9.3 %copy-start.2 = (s32[32]{0:T(128)S(1)}, s32[32]{0:T(128)}, u32[]{:S(2)}) copy-start(s32[32]{0:T(128)} %param.15) | copy-start | bytes 388
  17.3 48.5 %all-to-all-start = ((bf16[16,8,6272]{2,1,0:T(8,128)(2,1)}), bf16[16,8,6272]{2,1,0:T(8,128)(2,1)S(1)}, u32[]{:S(2)}, u32[]{:S(2)}) async-start(bf16[16,8,6272]{2,1,0:T(8,128)(2,1)} %diffuse.1), calls=%async_computation | async-start | bytes 3211264 | tf_op jit(solution)/shard_map/all_to_all | solution.py:266
  65.8 1.2 %copy-start = (bf16[16,8,6272]{2,1,0:T(8,128)(2,1)}, bf16[16,8,6272]{2,1,0:T(8,128)(2,1)S(1)}, u32[]{:S(2)}) copy-start(bf16[16,8,6272]{2,1,0:T(8,128)(2,1)S(1)} %all-to-all-done) | copy-start | bytes 4816900
  73.3 3.5 %collective-permute-start = (bf16[16,24576]{1,0:T(8,128)(2,1)}, bf16[16,24576]{1,0:T(8,128)(2,1)S(1)}, u32[]{:S(2)}, u32[]{:S(2)}) collective-permute-start(bf16[16,24576]{1,0:T(8,128)(2,1)} %get-tuple-element.8), channel_id=1, source_target_pairs={{0,16},{16,0},{32,48},{48,32},{64,80},{80,64},{96,112},{112,96},{1... | collective-permute-start | bytes 2359304 | tf_op jit(solution)/shard_map/ppermute | solution.py:290
  78.4 10.5 %collective-permute-start.3 = (bf16[4,24576]{1,0:T(4,128)(2,1)S(1)}, bf16[4,24576]{1,0:T(4,128)(2,1)S(1)}, u32[]{:S(2)}, u32[]{:S(2)}) collective-permute-start(bf16[4,24576]{1,0:T(4,128)(2,1)S(1)} %get-tuple-element.12), channel_id=1, source_target_pairs={{0,96},{16,112},{32,0},{48,16},{64,32},{80,48},{96,64},{112,80},{1... | collective-permute-start | bytes 589832 | tf_op jit(solution)/shard_map/ppermute | solution.py:300
  80.9 8.0 %collective-permute-start.2 = (bf16[4,24576]{1,0:T(4,128)(2,1)S(1)}, bf16[4,24576]{1,0:T(4,128)(2,1)S(1)}, u32[]{:S(2)}, u32[]{:S(2)}) collective-permute-start(bf16[4,24576]{1,0:T(4,128)(2,1)S(1)} %get-tuple-element.13), channel_id=1, source_target_pairs={{0,64},{16,80},{32,96},{48,112},{64,0},{80,16},{96,32},{112,48},{1... | collective-permute-start | bytes 589832 | tf_op jit(solution)/shard_map/ppermute | solution.py:300
  81.4 12.0 %collective-permute-start.1 = (bf16[4,24576]{1,0:T(4,128)(2,1)S(1)}, bf16[4,24576]{1,0:T(4,128)(2,1)S(1)}, u32[]{:S(2)}, u32[]{:S(2)}) collective-permute-start(bf16[4,24576]{1,0:T(4,128)(2,1)S(1)} %get-tuple-element.11), channel_id=1, source_target_pairs={{0,32},{16,48},{32,64},{48,80},{64,96},{80,112},{96,0},{112,16},{1... | collective-permute-start | bytes 589832 | tf_op jit(solution)/shard_map/ppermute | solution.py:300
  93.8 9.9 %collective-permute-start.4 = (bf16[2,24576]{1,0:T(2,128)(2,1)S(1)}, bf16[2,24576]{1,0:T(2,128)(2,1)S(1)}, u32[]{:S(2)}, u32[]{:S(2)}) collective-permute-start(bf16[2,24576]{1,0:T(2,128)(2,1)S(1)} %slice.38), channel_id=1, source_target_pairs={{0,128},{16,144},{32,160},{48,176},{64,192},{80,208},{96,224},{112... | collective-permute-start | bytes 294920 | tf_op jit(solution)/shard_map/ppermute | solution.py:301

commit v2 on v1

--- a/solution.py
+++ b/solution.py
@@ -1,3 +1,5 @@
+import functools
+
 import jax
 import jax.numpy as jnp
 from jax import lax
@@ -9,6 +11,7 @@
 LANES = 128
 SUBS = 8
 ROWS_PER_BLOCK = 8
+PIECES = (24, 24)
 CORES, RING, HALVES = 2, 4, 2
 
 
@@ -19,14 +22,18 @@
 
 def diffuse_kernel(
     place_ref, scale_ref, map_ref, width_ref, alpha_ref, cx_ref, cy_ref, spread_ref, gather_ref,
-    out_ref, raw_scr, cx_scr, cy_scr, x_scr, f_scr, gx_scr, gy_scr, ax_scr, ay_scr, ayr_scr, o_scr,
-    msg_scr, sems, out_sem,
+    *refs,
 ):
+    out_refs = refs[: len(PIECES)]
+    (
+        raw_scr, cx_scr, cy_scr, x_scr, f_scr, gx_scr, gy_scr, ax_scr, ay_scr, ayr_scr, o_scr,
+        msg_scr, sems, out_sem,
+    ) = refs[len(PIECES) :]
     rows, cols = cx_ref.shape
     levels = alpha_ref.shape[1]
     fold = rows // SUBS
     blocks = cols // LANES
-    tiles, _, length = out_ref.shape
+    tiles = width_ref.shape[0]
 
     def part(b):
         return pl.ds(b * LANES, LANES)
@@ -125,17 +132,20 @@
         msg_scr[:, part(i)] = o_scr[at(i), :].astype(jnp.bfloat16)
     spare = msg_scr.shape[1] - rows * LANES
     msg_scr[:, pl.ds(rows * LANES, spare)] = jnp.zeros((SUBS, spare), jnp.bfloat16)
-    first_col = 0
     sends = []
-    for t in range(tiles):
-        first = pl.multiple_of(first_col // cols * LANES, LANES)
-        sends.append(
-            pltpu.make_async_copy(
-                msg_scr.at[:, pl.ds(first, length)], out_ref.at[t], out_sem.at[t]
+    begin = 0
+    for p, out_ref in enumerate(out_refs):
+        first_col = 0
+        for t in range(tiles):
+            first = pl.multiple_of((first_col // cols + begin) * LANES, LANES)
+            sends.append(
+                pltpu.make_async_copy(
+                    msg_scr.at[:, pl.ds(first, out_ref.shape[2])], out_ref.at[t], out_sem.at[p, t]
+                )
             )
-        )
-        sends[-1].start()
-        first_col = first_col + width_ref[t]
+            sends[-1].start()
+            first_col = first_col + width_ref[t]
+        begin += PIECES[p]
     for one in sends:
         one.wait()
 
@@ -145,8 +155,8 @@
     tiles = tile_widths.shape[0]
     blocks = cols // LANES
     assert levels * blocks == SUBS and rows % SUBS == 0
-    tile_rows = pl.cdiv(capacity, cols) + 1
-    length = tile_rows * LANES
+    tile_rows = capacity // cols + 1
+    assert sum(PIECES) == tile_rows - 1
     natural = lax.broadcasted_iota(jnp.int32, (cols, cols), 0)
     spaced = lax.broadcasted_iota(jnp.int32, (cols, cols), 1)
     spread = (natural == spaced % LANES * blocks + spaced // LANES).astype(jnp.bfloat16)
@@ -157,9 +167,11 @@
     whole = pltpu.VMEM((rows, cols), jnp.float32)
     return pl.pallas_call(
         diffuse_kernel,
-        out_shape=jax.ShapeDtypeStruct((tiles, SUBS, length), jnp.bfloat16),
+        out_shape=[
+            jax.ShapeDtypeStruct((tiles, SUBS, (n + 1) * LANES), jnp.bfloat16) for n in PIECES
+        ],
         in_specs=[scalars] * 4 + [anywhere] * 3 + [vector] * 2,
-        out_specs=anywhere,
+        out_specs=[anywhere] * len(PIECES),
         scratch_shapes=[
             pltpu.VMEM((levels, blocks, rows, LANES), jnp.float32),
             plane,
@@ -174,13 +186,15 @@
             pltpu.VMEM((rows * SUBS, LANES), jnp.float32),
             pltpu.VMEM((SUBS, (rows + tile_rows) * LANES), jnp.bfloat16),
             pltpu.SemaphoreType.DMA((blocks, 2 + levels)),
-            pltpu.SemaphoreType.DMA((tiles,)),
+            pltpu.SemaphoreType.DMA((len(PIECES), tiles)),
         ],
         name="diffuse",
     )(place, level_scale, level_map, tile_widths, alpha, coef_x, coef_y, spread, spread.T)
 
 
-def localize_kernel(place_ref, width_ref, x_ref, weight_ref, order_ref, pert_ref, own_ref, send_ref, s_scr):
+def localize_kernel(
+    begin_row, place_ref, width_ref, x_ref, weight_ref, order_ref, pert_ref, own_ref, send_ref, s_scr
+):
     step = pl.program_id(0)
     tiles = width_ref.shape[0]
     levels = order_ref.shape[0]
@@ -195,7 +209,7 @@
     shift = first_col % cols
     shift_blocks = shift // LANES
     shift_lanes = shift % LANES
-    width = width_ref[me] - step * chunk
+    width = width_ref[me] - begin_row * cols - step * chunk
     begin = pl.multiple_of(step * (count * LANES), LANES)
     spread = jnp.dot(
         weight_ref[...],
@@ -228,22 +242,23 @@
         here = after
 
 
-def localize(place, tile_widths, arrived, weight, order, perturbations):
-    _, levels, capacity = perturbations.shape
+def localize(begin_row, rows, place, tile_widths, arrived, weight, order, perturbations):
+    levels = perturbations.shape[1]
     blocks = weight.shape[0] // levels
     cols = blocks * LANES
     chunk = ROWS_PER_BLOCK * cols
-    assert capacity % chunk == 0
+    assert rows % ROWS_PER_BLOCK == 0 and begin_row % ROWS_PER_BLOCK == 0
+    skip = begin_row // ROWS_PER_BLOCK
     scalars = pl.BlockSpec(memory_space=pltpu.SMEM)
     vector = pl.BlockSpec(memory_space=pltpu.VMEM)
-    half = jax.ShapeDtypeStruct((levels // 2, capacity), jnp.bfloat16)
+    half = jax.ShapeDtypeStruct((levels // 2, rows * cols), jnp.bfloat16)
     half_spec = pl.BlockSpec((levels // 2, chunk), lambda i: (0, i))
     return pl.pallas_call(
-        localize_kernel,
-        grid=(capacity // chunk,),
+        functools.partial(localize_kernel, begin_row),
+        grid=(rows // ROWS_PER_BLOCK,),
         out_shape=(half, half),
         in_specs=[scalars, scalars, vector, vector, vector,
-                  pl.BlockSpec((1, levels, chunk), lambda i: (0, 0, i))],
+                  pl.BlockSpec((1, levels, chunk), lambda i: (0, 0, i + skip))],
         out_specs=(half_spec, half_spec),
         scratch_shapes=[pltpu.VMEM((levels, chunk + 2 * cols), jnp.float32)],
         name="localize",
@@ -253,7 +268,7 @@
 def body(
     alpha_weights, perturbations, coef_x, coef_y, level_scale, level_map, tile_widths, band_widths
 ):
-    _, lev_dev, rows, cols = alpha_weights.shape
+    _, lev_dev, _, cols = alpha_weights.shape
     _, levels, capacity = perturbations.shape
     blocks = cols // LANES
     tiles = tile_widths.shape[0]
@@ -263,12 +278,16 @@
     outgoing = smooth_and_cut(
         place, level_scale, level_map, tile_widths, alpha_weights, coef_x, coef_y, capacity
     )
-    arrived = lax.all_to_all(outgoing, "lev", split_axis=0, concat_axis=0, tiled=True)
-    arrived = arrived.reshape(tiles * SUBS, -1)
+    arrived = []
+    for one in outgoing:
+        if arrived:
+            one, arrived[-1] = lax.optimization_barrier((one, arrived[-1]))
+        one = lax.all_to_all(one, "lev", split_axis=0, concat_axis=0, tiled=True)
+        arrived.append(one.reshape(tiles * SUBS, -1))
 
     slot = jnp.arange(levels)
     core = (mem + slot // 16) % CORES
-    ring = (mem // CORES + slot // 4) % RING
+    ring = (mem // CORES + (1 - 2 * core) * (slot // 4)) % RING
     half = (mem // (CORES * RING) + slot // 2) % HALVES
     row_level = half * 16 + ring * 4 + core * 2 + slot % 2
     order = (row_level[:, None] == slot[None, :]).astype(jnp.bfloat16)
@@ -281,31 +300,48 @@
     weight = jnp.where(same_block, local.reshape(1, levels, tiles, 1, lev_dev), 0.0)
     weight = weight.astype(jnp.bfloat16).reshape(blocks * levels, tiles * SUBS)
 
-    own, other = localize(place, tile_widths, arrived, weight, order, perturbations)
-
+    results = []
+    begin = 0
+    for rows_here, one in zip(PIECES, arrived):
+        own, other = localize(
+            begin, rows_here, place, tile_widths, one, weight, order, perturbations
+        )
+        results.append(sum_members(own, other))
+        begin += rows_here
+    return jnp.concatenate(results, axis=1)
+
+
+def sum_members(own, other):
     def wide(x):
         return x.astype(jnp.float32)
 
-    members = CORES * RING * HALVES
-    came = lax.ppermute(other, "mem", [(i, i ^ 1) for i in range(members)])
-    pair = (wide(own) + wide(came)).astype(jnp.bfloat16).reshape(RING, 4, capacity)
-    total = wide(pair[0])
-    for d in range(1, RING):
-        ring_perm = [
-            (z * 8 + x * 2 + c, z * 8 + (x + d) % RING * 2 + c)
-            for z in range(HALVES)
-            for x in range(RING)
-            for c in range(CORES)
-        ]
-        total = total + wide(lax.ppermute(pair[d], "mem", ring_perm))
-    came = lax.ppermute(
-        total[2:].astype(jnp.bfloat16), "mem", [(i, (i + 8) % members) for i in range(members)]
-    )
-    return total[:2] + wide(came)
+    def narrow(x):
+        return x.astype(jnp.bfloat16)
+
+    def moved(dz, dx, dc):
+        pairs = []
+        for z in range(HALVES):
+            for x in range(RING):
+                for c in range(CORES):
+                    along = dx * (1 - 2 * c)
+                    to = ((z + dz) % HALVES, (x + along) % RING, (c + dc) % CORES)
+                    pairs.append(((z * RING + x) * CORES + c, (to[0] * RING + to[1]) * CORES + to[2]))
+        return pairs
+
+    came = lax.ppermute(other, "mem", moved(0, 0, 1))
+    pair = (wide(own) + wide(came)).reshape(RING, own.shape[0] // RING, own.shape[1])
+    relay = lax.ppermute(narrow(pair[2]), "mem", moved(0, 1, 0))
+    direct = lax.ppermute(narrow(pair[3]), "mem", moved(0, -1, 0))
+    joined = lax.ppermute(narrow(pair[1] + wide(relay)), "mem", moved(0, 1, 0))
+    total = pair[0] + wide(direct) + wide(joined)
+    keep = total.shape[0] // HALVES
+    far = lax.ppermute(narrow(total[keep:]), "mem", moved(1, 0, 0))
+    return total[:keep] + wide(far)
 
 
 def solution(mesh):
     placed = (P("mem", "lev", None, None), P("mem", None, "lev"), P(), P(), P(), P(), P(), P())
+
     return jax.shard_map(
         body, mesh=mesh, in_specs=placed, out_specs=P("mem", "lev"), check_vma=False
     )

time: 105 us -> 114 us (1.086); the launches traced: 104 us -> 112 us
  starting transfers between devices: 18.6 us -> 32.7 us
  waiting for transfers between devices: 56.3 us -> 47.5 us
  Pallas kernels: 22.1 us -> 23.7 us
    ppermute x5 -> x10, waiting for transfers between devices: 19.2 us -> 5.22 us  [the longest x2 5.2 us: sum_members(): far = lax.ppermute(narrow(total[keep:]), 'mem', moved(1, 0, 0))]
    ppermute x5 -> x10, starting transfers between devices: 9.38 us -> 19.9 us  [the longest x2 6.73 us: sum_members(): far = lax.ppermute(narrow(total[keep:]), 'mem', moved(1, 0, 0))]
    all_to_all x1 -> x2, waiting for transfers between devices: 37.1 us -> 42.3 us  [body(): one = lax.all_to_all(one, 'lev', split_axis=0, concat_axis=0, tiled=True)]
    all_to_all x1 -> x2, starting transfers between devices: 9.19 us -> 12.8 us  [body(): one = lax.all_to_all(one, 'lev', split_axis=0, concat_axis=0, tiled=True)]
    pallas_call x2 -> x3, Pallas kernels: 22.1 us -> 23.7 us  [the longest x1 15.9 us: smooth_and_cut(): pl.pallas_call(diffuse_kernel, out_shape=[jax.ShapeDtypeStruct((tiles, SU...]
    another operation x0 -> x2, other arithmetic: none -> 1.18 us
    convert_element_type x1 -> x2, other arithmetic: 1.31 us -> 0.14 us  [narrow(): return x.astype(jnp.bfloat16)]
  transfers between devices with their start and end apart: 6 -> 12, of which waited for: 5 -> 4; matrix products, arithmetic and copies ran while one was open for 2% -> 3% of each run, Pallas kernels for 0% -> 0%
where the time goes in v2:
time: 114 us; the launch traced here: 112 us
  waiting for transfers between devices  47.5 us (42%)
  starting transfers between devices  32.7 us (29%)
  Pallas kernels  23.7 us (21%)
  other arithmetic  4.95 us (4%)
  local copies, waits for them, and re-layouts  3.11 us (3%)
    all_to_all x2, waiting for transfers between devices, body(): one = lax.all_to_all(one, 'lev', split_axis=0, concat_axis=0, tiled=True)  42.3 us
    pallas_call x1, Pallas kernels, smooth_and_cut(): pl.pallas_call(diffuse_kernel, out_shape=[jax.ShapeDtypeStruct((tiles, SU...  15.9 us
    all_to_all x2, starting transfers between devices, body(): one = lax.all_to_all(one, 'lev', split_axis=0, concat_axis=0, tiled=True)  12.8 us
    pallas_call x2, Pallas kernels, localize(): pl.pallas_call(functools.partial(localize_kernel, begin_row), grid=(rows...  7.83 us
    ppermute x2, starting transfers between devices, sum_members(): far = lax.ppermute(narrow(total[keep:]), 'mem', moved(1, 0, 0))  6.73 us
    ppermute x2, starting transfers between devices, sum_members(): joined = lax.ppermute(narrow(pair[1] + wide(relay)), 'mem', moved(0, 1, 0))  6.06 us
    ppermute x2, waiting for transfers between devices, sum_members(): far = lax.ppermute(narrow(total[keep:]), 'mem', moved(1, 0, 0))  5.2 us
    ppermute x2, starting transfers between devices, sum_members(): came = lax.ppermute(other, 'mem', moved(0, 0, 1))  2.99 us
  transfers between devices with their start and end apart: 12, of which 4 were waited for; matrix products, arithmetic and copies ran while one was open for 3% of the time, Pallas kernels for 0%

profile of v2, /device:TPU:1, one launch (start us, length us, event | category | flops | bytes accessed | tf_op | source)
XLA Modules:
  0.0 112.2 jit_solution(473699919429091759)
XLA Ops:
  0.0 1.5 %fusion.1 = (bf16[512,512]{1,0:T(8,128)(2,1)}, bf16[512,512]{1,0:T(8,128)(2,1)}) fusion(s32[512]{0:T(512)S(1)} %get-tuple-element.33, s32[512]{0:T(512)S(1)} %get-tuple-element.36, s32[512]{0:T(512)S(1)} %get-tuple-element.34, s32[512]{0:T(512)S(1)} %get-tuple-element.35, pred[512]{0:T(512)(128)(4,1)S(1)} %get-tuple-element.37, ...), kind=kLoop, calls=%fused_computation.3 | loop fusion | flops 3145728 | bytes 1057792 | tf_op jit(solution)/shard_map/convert_element_type | solution.py:162
  1.5 15.9 %diffuse.1 = (bf16[16,8,3200]{2,1,0:T(8,128)(2,1)}, bf16[16,8,3200]{2,1,0:T(8,128)(2,1)}) custom-call(s32[1]{0:T(128)} %bitcast.place_ref, f32[32]{0:T(128)} %scale_ref.1, s32[32]{0:T(128)} %map_ref.1, s32[16]{0:T(128)} %width_ref.5, f32[1,2,384,512]{3,2,1,0:T(8,128)} %alpha_ref.1, f32[384,512]{1,0:T(8,128)} %cx_ref.1, f32[384,512]{1,0:T(8,128)} %cy_ref.1, ...), custom_call_target="tpu_custom_call" | custom-call | tf_op jit(solution)/shard_map/diffuse/pallas_call | solution.py:168
  17.5 0.0 copy-start.3
  17.5 0.0 copy-start.4
  17.5 9.2 %all-to-all-start = ((bf16[16,8,3200]{2,1,0:T(8,128)(2,1)}), bf16[16,8,3200]{2,1,0:T(8,128)(2,1)S(1)}, u32[]{:S(2)}, u32[]{:S(2)}) async-start(bf16[16,8,3200]{2,1,0:T(8,128)(2,1)} %get-tuple-element.14), calls=%async_computation | async-start | bytes 1638400 | tf_op jit(solution)/shard_map/all_to_all | solution.py:285
  26.7 0.1 sub.67
  26.8 0.2 select_reduce_fusion.1
  27.0 0.1 min.20
  27.1 0.1 compare_select_fusion
  27.2 0.1 select_convert_fusion
  27.3 0.1 convert_element_type.82
  27.5 0.7 copy.9.weight_ref
  28.2 0.7 fusion.7.order_ref
  28.9 19.9 %all-to-all-done = bf16[16,8,3200]{2,1,0:T(8,128)(2,1)S(1)} async-done(((bf16[16,8,3200]{2,1,0:T(8,128)(2,1)}), bf16[16,8,3200]{2,1,0:T(8,128)(2,1)S(1)}, u32[]{:S(2)}, u32[]{:S(2)}) %all-to-all-start) | async-done | bytes 819232 | tf_op jit(solution)/shard_map/all_to_all | solution.py:285
  48.8 0.9 copy-done
  49.8 3.9 %localize.2 = (bf16[16,12288]{1,0:T(8,128)(2,1)}, bf16[16,12288]{1,0:T(8,128)(2,1)}) custom-call(s32[1]{0:T(128)} %bitcast.place_ref, s32[16]{0:T(128)} %width_ref.5, bf16[128,3200]{1,0:T(8,128)(2,1)} %bitcast.5, bf16[128,128]{1,0:T(8,128)(2,1)} %copy.9.weight_ref, bf16[32,32]{1,0:T(8,128)(2,1)} %fusion.7.order_ref, bf16[1,32,24576]{2,1,0:T(8,128)(2,1)} %pert_ref.3), custom_call_target="tpu_custom_call" | custom-call | tf_op jit(solution)/shard_map/localize/pallas_call | solution.py:256
  53.7 1.7 %collective-permute-start = (bf16[16,12288]{1,0:T(8,128)(2,1)}, bf16[16,12288]{1,0:T(8,128)(2,1)S(1)}, u32[]{:S(2)}, u32[]{:S(2)}) collective-permute-start(bf16[16,12288]{1,0:T(8,128)(2,1)} %get-tuple-element.17), channel_id=1, source_target_pairs={{0,16},{16,0},{32,48},{48,32},{64,80},{80,64},{96,112},{112,96},{1... | collective-permute-start | bytes 1179656 | tf_op jit(solution)/shard_map/ppermute | solution.py:331
  55.4 3.6 %all-to-all-start.1 = ((bf16[16,8,3200]{2,1,0:T(8,128)(2,1)}), bf16[16,8,3200]{2,1,0:T(8,128)(2,1)S(1)}, u32[]{:S(2)}, u32[]{:S(2)}) async-start(bf16[16,8,3200]{2,1,0:T(8,128)(2,1)} %get-tuple-element.18), calls=%async_computation.1 | async-start | bytes 1638400 | tf_op jit(solution)/shard_map/all_to_all | solution.py:285
  59.0 0.0 collective-permute-done
  59.0 0.1 fusion.27
  59.1 22.4 %all-to-all-done.1 = bf16[16,8,3200]{2,1,0:T(8,128)(2,1)S(1)} async-done(((bf16[16,8,3200]{2,1,0:T(8,128)(2,1)}), bf16[16,8,3200]{2,1,0:T(8,128)(2,1)S(1)}, u32[]{:S(2)}, u32[]{:S(2)}) %all-to-all-start.1) | async-done | bytes 819232 | tf_op jit(solution)/shard_map/all_to_all | solution.py:285
  81.5 0.9 copy-done.1
  82.4 3.9 %localize.3 = (bf16[16,12288]{1,0:T(8,128)(2,1)}, bf16[16,12288]{1,0:T(8,128)(2,1)}) custom-call(s32[1]{0:T(128)} %bitcast.place_ref, s32[16]{0:T(128)} %width_ref.5, bf16[128,3200]{1,0:T(8,128)(2,1)} %bitcast.6, bf16[128,128]{1,0:T(8,128)(2,1)} %copy.9.weight_ref, bf16[32,32]{1,0:T(8,128)(2,1)} %fusion.7.order_ref, bf16[1,32,24576]{2,1,0:T(8,128)(2,1)} %pert_ref.3), custom_call_target="tpu_custom_call" | custom-call | tf_op jit(solution)/shard_map/localize/pallas_call | solution.py:256
  86.3 1.3 %collective-permute-start.5 = (bf16[16,12288]{1,0:T(8,128)(2,1)}, bf16[16,12288]{1,0:T(8,128)(2,1)S(1)}, u32[]{:S(2)}, u32[]{:S(2)}) collective-permute-start(bf16[16,12288]{1,0:T(8,128)(2,1)} %get-tuple-element.20), channel_id=1, source_target_pairs={{0,16},{16,0},{32,48},{48,32},{64,80},{80,64},{96,112},{112,96},{1... | collective-permute-start | bytes 1179656 | tf_op jit(solution)/shard_map/ppermute | solution.py:331
  87.6 0.1 fusion.29
  87.7 1.3 %collective-permute-start.1 = (bf16[4,12288]{1,0:T(4,128)(2,1)S(1)}, bf16[4,12288]{1,0:T(4,128)(2,1)S(1)}, u32[]{:S(2)}, u32[]{:S(2)}) collective-permute-start(bf16[4,12288]{1,0:T(4,128)(2,1)S(1)} %get-tuple-element.27), channel_id=1, source_target_pairs={{0,96},{16,48},{32,0},{48,80},{64,32},{80,112},{96,64},{112,16},{1... | collective-permute-start | bytes 294920 | tf_op jit(solution)/shard_map/ppermute | solution.py:334
  89.0 1.5 %collective-permute-start.2 = (bf16[4,12288]{1,0:T(4,128)(2,1)S(1)}, bf16[4,12288]{1,0:T(4,128)(2,1)S(1)}, u32[]{:S(2)}, u32[]{:S(2)}) collective-permute-start(bf16[4,12288]{1,0:T(4,128)(2,1)S(1)} %get-tuple-element.28), channel_id=1, source_target_pairs={{0,32},{16,112},{32,64},{48,16},{64,96},{80,48},{96,0},{112,80},{1... | collective-permute-start | bytes 294920 | tf_op jit(solution)/shard_map/ppermute | solution.py:333
  90.4 1.1 fusion.28
  91.5 0.1 fusion.30
  91.6 1.3 %collective-permute-start.7 = (bf16[4,12288]{1,0:T(4,128)(2,1)S(1)}, bf16[4,12288]{1,0:T(4,128)(2,1)S(1)}, u32[]{:S(2)}, u32[]{:S(2)}) collective-permute-start(bf16[4,12288]{1,0:T(4,128)(2,1)S(1)} %get-tuple-element.30), channel_id=1, source_target_pairs={{0,32},{16,112},{32,64},{48,16},{64,96},{80,48},{96,0},{112,80},{1... | collective-permute-start | bytes 294920 | tf_op jit(solution)/shard_map/ppermute | solution.py:333
  92.9 0.1 fusion.4
  93.0 3.3 %collective-permute-start.3 = (bf16[4,12288]{1,0:T(4,128)(2,1)S(1)}, bf16[4,12288]{1,0:T(4,128)(2,1)S(1)}, u32[]{:S(2)}, u32[]{:S(2)}) collective-permute-start(bf16[4,12288]{1,0:T(4,128)(2,1)S(1)} %fusion.4), channel_id=1, source_target_pairs={{0,32},{16,112},{32,64},{48,16},{64,96},{80,48},{96,0},{112,80},{1... | collective-permute-start | bytes 294920 | tf_op jit(solution)/shard_map/ppermute | solution.py:335
  96.3 0.0 collective-permute-start.6
  96.3 0.0 collective-permute-done.7
  96.3 0.1 fusion.2
  96.4 2.8 %collective-permute-start.8 = (bf16[4,12288]{1,0:T(4,128)(2,1)S(1)}, bf16[4,12288]{1,0:T(4,128)(2,1)S(1)}, u32[]{:S(2)}, u32[]{:S(2)}) collective-permute-start(bf16[4,12288]{1,0:T(4,128)(2,1)S(1)} %fusion.2), channel_id=1, source_target_pairs={{0,32},{16,112},{32,64},{48,16},{64,96},{80,48},{96,0},{112,80},{1... | collective-permute-start | bytes 294920 | tf_op jit(solution)/shard_map/ppermute | solution.py:335
  99.2 0.0 collective-permute-done.1
  99.2 0.1 fusion.5
  99.2 0.1 slice.91
  99.3 4.3 %collective-permute-start.4 = (bf16[2,12288]{1,0:T(2,128)(2,1)S(1)}, bf16[2,12288]{1,0:T(2,128)(2,1)S(1)}, u32[]{:S(2)}, u32[]{:S(2)}) collective-permute-start(bf16[2,12288]{1,0:T(2,128)(2,1)S(1)} %slice.91), channel_id=1, source_target_pairs={{0,128},{16,144},{32,160},{48,176},{64,192},{80,208},{96,224},{112... | collective-permute-start | bytes 147464 | tf_op jit(solution)/shard_map/ppermute | solution.py:338
  103.6 0.1 fusion.3
  103.7 0.1 slice.90
  103.7 2.4 %collective-permute-start.9 = (bf16[2,12288]{1,0:T(2,128)(2,1)S(1)}, bf16[2,12288]{1,0:T(2,128)(2,1)S(1)}, u32[]{:S(2)}, u32[]{:S(2)}) collective-permute-start(bf16[2,12288]{1,0:T(2,128)(2,1)S(1)} %slice.90), channel_id=1, source_target_pairs={{0,128},{16,144},{32,160},{48,176},{64,192},{80,208},{96,224},{112... | collective-permute-start | bytes 147464 | tf_op jit(solution)/shard_map/ppermute | solution.py:338
  106.2 0.7 collective-permute-done.4
  106.8 0.1 slice_add_fusion.5
  106.9 4.5 %collective-permute-done.9 = bf16[2,12288]{1,0:T(2,128)(2,1)S(1)} collective-permute-done((bf16[2,12288]{1,0:T(2,128)(2,1)S(1)}, bf16[2,12288]{1,0:T(2,128)(2,1)S(1)}, u32[]{:S(2)}, u32[]{:S(2)}) %collective-permute-start.9) | collective-permute-done | bytes 49184 | tf_op jit(solution)/shard_map/ppermute | solution.py:338
  111.4 0.1 slice_add_fusion.4
  111.5 0.8 pad_maximum_fusion
  (16 shorter events, 0.1 us)
Async XLA Ops:
  17.5 9.2 %copy-start.3 = (s32[32]{0:T(128)S(1)}, s32[32]{0:T(128)}, u32[]{:S(2)}) copy-start(s32[32]{0:T(128)} %map_ref.1) | copy-start | bytes 388
  17.5 9.3 %copy-start.4 = (s32[32]{0:T(128)S(1)}, s32[32]{0:T(128)}, u32[]{:S(2)}) copy-start(s32[32]{0:T(128)} %param.15) | copy-start | bytes 388
  17.5 31.3 %all-to-all-start = ((bf16[16,8,3200]{2,1,0:T(8,128)(2,1)}), bf16[16,8,3200]{2,1,0:T(8,128)(2,1)S(1)}, u32[]{:S(2)}, u32[]{:S(2)}) async-start(bf16[16,8,3200]{2,1,0:T(8,128)(2,1)} %get-tuple-element.14), calls=%async_computation | async-start | bytes 1638400 | tf_op jit(solution)/shard_map/all_to_all | solution.py:285
  48.8 0.9 copy-start
  53.7 5.3 %copy-start.2 = (bf16[16,12288]{1,0:T(8,128)(2,1)S(1)}, bf16[16,12288]{1,0:T(8,128)(2,1)}, u32[]{:S(2)}) copy-start(bf16[16,12288]{1,0:T(8,128)(2,1)} %get-tuple-element.16) | copy-start | bytes 1179652
  53.7 5.3 %collective-permute-start = (bf16[16,12288]{1,0:T(8,128)(2,1)}, bf16[16,12288]{1,0:T(8,128)(2,1)S(1)}, u32[]{:S(2)}, u32[]{:S(2)}) collective-permute-start(bf16[16,12288]{1,0:T(8,128)(2,1)} %get-tuple-element.17), channel_id=1, source_target_pairs={{0,16},{16,0},{32,48},{48,32},{64,80},{80,64},{96,112},{112,96},{1... | collective-permute-start | bytes 1179656 | tf_op jit(solution)/shard_map/ppermute | solution.py:331
  55.4 26.1 %all-to-all-start.1 = ((bf16[16,8,3200]{2,1,0:T(8,128)(2,1)}), bf16[16,8,3200]{2,1,0:T(8,128)(2,1)S(1)}, u32[]{:S(2)}, u32[]{:S(2)}) async-start(bf16[16,8,3200]{2,1,0:T(8,128)(2,1)} %get-tuple-element.18), calls=%async_computation.1 | async-start | bytes 1638400 | tf_op jit(solution)/shard_map/all_to_all | solution.py:285
  81.5 0.9 copy-start.1
  86.3 4.1 %collective-permute-start.5 = (bf16[16,12288]{1,0:T(8,128)(2,1)}, bf16[16,12288]{1,0:T(8,128)(2,1)S(1)}, u32[]{:S(2)}, u32[]{:S(2)}) collective-permute-start(bf16[16,12288]{1,0:T(8,128)(2,1)} %get-tuple-element.20), channel_id=1, source_target_pairs={{0,16},{16,0},{32,48},{48,32},{64,80},{80,64},{96,112},{112,96},{1... | collective-permute-start | bytes 1179656 | tf_op jit(solution)/shard_map/ppermute | solution.py:331
  87.7 11.5 %collective-permute-start.1 = (bf16[4,12288]{1,0:T(4,128)(2,1)S(1)}, bf16[4,12288]{1,0:T(4,128)(2,1)S(1)}, u32[]{:S(2)}, u32[]{:S(2)}) collective-permute-start(bf16[4,12288]{1,0:T(4,128)(2,1)S(1)} %get-tuple-element.27), channel_id=1, source_target_pairs={{0,96},{16,48},{32,0},{48,80},{64,32},{80,112},{96,64},{112,16},{1... | collective-permute-start | bytes 294920 | tf_op jit(solution)/shard_map/ppermute | solution.py:334
  89.0 4.0 %collective-permute-start.2 = (bf16[4,12288]{1,0:T(4,128)(2,1)S(1)}, bf16[4,12288]{1,0:T(4,128)(2,1)S(1)}, u32[]{:S(2)}, u32[]{:S(2)}) collective-permute-start(bf16[4,12288]{1,0:T(4,128)(2,1)S(1)} %get-tuple-element.28), channel_id=1, source_target_pairs={{0,32},{16,112},{32,64},{48,16},{64,96},{80,48},{96,0},{112,80},{1... | collective-permute-start | bytes 294920 | tf_op jit(solution)/shard_map/ppermute | solution.py:333
  91.6 4.7 %collective-permute-start.7 = (bf16[4,12288]{1,0:T(4,128)(2,1)S(1)}, bf16[4,12288]{1,0:T(4,128)(2,1)S(1)}, u32[]{:S(2)}, u32[]{:S(2)}) collective-permute-start(bf16[4,12288]{1,0:T(4,128)(2,1)S(1)} %get-tuple-element.30), channel_id=1, source_target_pairs={{0,32},{16,112},{32,64},{48,16},{64,96},{80,48},{96,0},{112,80},{1... | collective-permute-start | bytes 294920 | tf_op jit(solution)/shard_map/ppermute | solution.py:333
  93.0 6.2 %collective-permute-start.3 = (bf16[4,12288]{1,0:T(4,128)(2,1)S(1)}, bf16[4,12288]{1,0:T(4,128)(2,1)S(1)}, u32[]{:S(2)}, u32[]{:S(2)}) collective-permute-start(bf16[4,12288]{1,0:T(4,128)(2,1)S(1)} %fusion.4), channel_id=1, source_target_pairs={{0,32},{16,112},{32,64},{48,16},{64,96},{80,48},{96,0},{112,80},{1... | collective-permute-start | bytes 294920 | tf_op jit(solution)/shard_map/ppermute | solution.py:335
  96.3 7.3 %collective-permute-start.6 = (bf16[4,12288]{1,0:T(4,128)(2,1)S(1)}, bf16[4,12288]{1,0:T(4,128)(2,1)S(1)}, u32[]{:S(2)}, u32[]{:S(2)}) collective-permute-start(bf16[4,12288]{1,0:T(4,128)(2,1)S(1)} %get-tuple-element.29), channel_id=1, source_target_pairs={{0,96},{16,48},{32,0},{48,80},{64,32},{80,112},{96,64},{112,16},{1... | collective-permute-start | bytes 294920 | tf_op jit(solution)/shard_map/ppermute | solution.py:334
  96.4 7.2 %collective-permute-start.8 = (bf16[4,12288]{1,0:T(4,128)(2,1)S(1)}, bf16[4,12288]{1,0:T(4,128)(2,1)S(1)}, u32[]{:S(2)}, u32[]{:S(2)}) collective-permute-start(bf16[4,12288]{1,0:T(4,128)(2,1)S(1)} %fusion.2), channel_id=1, source_target_pairs={{0,32},{16,112},{32,64},{48,16},{64,96},{80,48},{96,0},{112,80},{1... | collective-permute-start | bytes 294920 | tf_op jit(solution)/shard_map/ppermute | solution.py:335
  99.3 7.6 %collective-permute-start.4 = (bf16[2,12288]{1,0:T(2,128)(2,1)S(1)}, bf16[2,12288]{1,0:T(2,128)(2,1)S(1)}, u32[]{:S(2)}, u32[]{:S(2)}) collective-permute-start(bf16[2,12288]{1,0:T(2,128)(2,1)S(1)} %slice.91), channel_id=1, source_target_pairs={{0,128},{16,144},{32,160},{48,176},{64,192},{80,208},{96,224},{112... | collective-permute-start | bytes 147464 | tf_op jit(solution)/shard_map/ppermute | solution.py:338
  103.7 7.7 %collective-permute-start.9 = (bf16[2,12288]{1,0:T(2,128)(2,1)S(1)}, bf16[2,12288]{1,0:T(2,128)(2,1)S(1)}, u32[]{:S(2)}, u32[]{:S(2)}) collective-permute-start(bf16[2,12288]{1,0:T(2,128)(2,1)S(1)} %slice.90), channel_id=1, source_target_pairs={{0,128},{16,144},{32,160},{48,176},{64,192},{80,208},{96,224},{112... | collective-permute-start | bytes 147464 | tf_op jit(solution)/shard_map/ppermute | solution.py:338

commit v3 on v2

--- a/solution.py
+++ b/solution.py
@@ -21,14 +21,10 @@
 
 
 def diffuse_kernel(
-    place_ref, scale_ref, map_ref, width_ref, alpha_ref, cx_ref, cy_ref, spread_ref, gather_ref,
-    *refs,
+    place_ref, scale_ref, map_ref, width_ref, alpha_ref, cx_ref, cy_ref,
+    out_ref, raw_scr, cx_scr, cy_scr, spread_ref, gather_ref, x_scr, f_scr, gx_scr, gy_scr, ax_scr,
+    ay_scr, ayr_scr, o_scr, msg_scr, sems, out_sem,
 ):
-    out_refs = refs[: len(PIECES)]
-    (
-        raw_scr, cx_scr, cy_scr, x_scr, f_scr, gx_scr, gy_scr, ax_scr, ay_scr, ayr_scr, o_scr,
-        msg_scr, sems, out_sem,
-    ) = refs[len(PIECES) :]
     rows, cols = cx_ref.shape
     levels = alpha_ref.shape[1]
     fold = rows // SUBS
@@ -54,6 +50,14 @@
     for k in range(2 + levels):
         for b in range(blocks):
             copies[b][k].start()
+
+    for b in range(blocks):
+        natural = lax.broadcasted_iota(jnp.int32, (cols, LANES), 0)
+        spaced = lax.broadcasted_iota(jnp.int32, (cols, LANES), 1)
+        match = jnp.where(natural == spaced * blocks + b, 1.0, 0.0)
+        spread_ref[:, part(b)] = match.astype(jnp.bfloat16)
+        match = jnp.where(natural % LANES * blocks + natural // LANES == spaced + b * LANES, 1.0, 0.0)
+        gather_ref[:, part(b)] = match.astype(jnp.bfloat16)
 
     def spread_columns(planes):
         for r in range(fold):
@@ -133,19 +137,16 @@
     spare = msg_scr.shape[1] - rows * LANES
     msg_scr[:, pl.ds(rows * LANES, spare)] = jnp.zeros((SUBS, spare), jnp.bfloat16)
     sends = []
-    begin = 0
-    for p, out_ref in enumerate(out_refs):
-        first_col = 0
-        for t in range(tiles):
-            first = pl.multiple_of((first_col // cols + begin) * LANES, LANES)
-            sends.append(
-                pltpu.make_async_copy(
-                    msg_scr.at[:, pl.ds(first, out_ref.shape[2])], out_ref.at[t], out_sem.at[p, t]
-                )
+    first_col = 0
+    for t in range(tiles):
+        first = pl.multiple_of(first_col // cols * LANES, LANES)
+        sends.append(
+            pltpu.make_async_copy(
+                msg_scr.at[:, pl.ds(first, out_ref.shape[2])], out_ref.at[t], out_sem.at[t]
             )
-            sends[-1].start()
-            first_col = first_col + width_ref[t]
-        begin += PIECES[p]
+        )
+        sends[-1].start()
+        first_col = first_col + width_ref[t]
     for one in sends:
         one.wait()
 
@@ -157,25 +158,22 @@
     assert levels * blocks == SUBS and rows % SUBS == 0
     tile_rows = capacity // cols + 1
     assert sum(PIECES) == tile_rows - 1
-    natural = lax.broadcasted_iota(jnp.int32, (cols, cols), 0)
-    spaced = lax.broadcasted_iota(jnp.int32, (cols, cols), 1)
-    spread = (natural == spaced % LANES * blocks + spaced // LANES).astype(jnp.bfloat16)
     anywhere = pl.BlockSpec(memory_space=pl.ANY)
     scalars = pl.BlockSpec(memory_space=pltpu.SMEM)
-    vector = pl.BlockSpec(memory_space=pltpu.VMEM)
     plane = pltpu.VMEM((blocks, rows, LANES), jnp.float32)
     whole = pltpu.VMEM((rows, cols), jnp.float32)
+    square = pltpu.VMEM((cols, cols), jnp.bfloat16)
     return pl.pallas_call(
         diffuse_kernel,
-        out_shape=[
-            jax.ShapeDtypeStruct((tiles, SUBS, (n + 1) * LANES), jnp.bfloat16) for n in PIECES
-        ],
-        in_specs=[scalars] * 4 + [anywhere] * 3 + [vector] * 2,
-        out_specs=[anywhere] * len(PIECES),
+        out_shape=jax.ShapeDtypeStruct((tiles, SUBS, tile_rows * LANES), jnp.bfloat16),
+        in_specs=[scalars] * 4 + [anywhere] * 3,
+        out_specs=anywhere,
         scratch_shapes=[
             pltpu.VMEM((levels, blocks, rows, LANES), jnp.float32),
             plane,
             plane,
+            square,
+            square,
             whole,
             pltpu.VMEM((rows + SUBS, cols), jnp.float32),
             whole,
@@ -186,14 +184,15 @@
             pltpu.VMEM((rows * SUBS, LANES), jnp.float32),
             pltpu.VMEM((SUBS, (rows + tile_rows) * LANES), jnp.bfloat16),
             pltpu.SemaphoreType.DMA((blocks, 2 + levels)),
-            pltpu.SemaphoreType.DMA((len(PIECES), tiles)),
+            pltpu.SemaphoreType.DMA((tiles,)),
         ],
         name="diffuse",
-    )(place, level_scale, level_map, tile_widths, alpha, coef_x, coef_y, spread, spread.T)
+    )(place, level_scale, level_map, tile_widths, alpha, coef_x, coef_y)
 
 
 def localize_kernel(
-    begin_row, place_ref, width_ref, x_ref, weight_ref, order_ref, pert_ref, own_ref, send_ref, s_scr
+    begin_row, place_ref, width_ref, x_ref, weight_ref, order_ref, pert_ref, own_ref, send_ref, s_scr,
+    here_scr, sem,
 ):
     step = pl.program_id(0)
     tiles = width_ref.shape[0]
@@ -211,9 +210,17 @@
     shift_lanes = shift % LANES
     width = width_ref[me] - begin_row * cols - step * chunk
     begin = pl.multiple_of(step * (count * LANES), LANES)
+
+    @pl.when(step == 0)
+    def _():
+        rows_here = pl.ds(begin_row * LANES, here_scr.shape[1])
+        copy = pltpu.make_async_copy(x_ref.at[:, rows_here], here_scr, sem)
+        copy.start()
+        copy.wait()
+
     spread = jnp.dot(
         weight_ref[...],
-        x_ref[:, pl.ds(begin, (count + 1) * LANES)],
+        here_scr[:, pl.ds(begin, (count + 1) * LANES)],
         preferred_element_type=jnp.float32,
     )
     for r in range(count + 1):
@@ -257,10 +264,15 @@
         functools.partial(localize_kernel, begin_row),
         grid=(rows // ROWS_PER_BLOCK,),
         out_shape=(half, half),
-        in_specs=[scalars, scalars, vector, vector, vector,
+        in_specs=[scalars, scalars, pl.BlockSpec(memory_space=pl.ANY), vector, vector,
                   pl.BlockSpec((1, levels, chunk), lambda i: (0, 0, i + skip))],
         out_specs=(half_spec, half_spec),
-        scratch_shapes=[pltpu.VMEM((levels, chunk + 2 * cols), jnp.float32)],
+        scratch_shapes=[
+            pltpu.VMEM((levels, chunk + 2 * cols), jnp.float32),
+            pltpu.VMEM((arrived.shape[0], (rows + 1) * LANES), jnp.bfloat16),
+            pltpu.SemaphoreType.DMA,
+        ],
+        compiler_params=pltpu.CompilerParams(vmem_limit_bytes=16 << 20),
         name="localize",
     )(place, tile_widths, arrived, weight, order, perturbations)
 
@@ -278,16 +290,12 @@
     outgoing = smooth_and_cut(
         place, level_scale, level_map, tile_widths, alpha_weights, coef_x, coef_y, capacity
     )
-    arrived = []
-    for one in outgoing:
-        if arrived:
-            one, arrived[-1] = lax.optimization_barrier((one, arrived[-1]))
-        one = lax.all_to_all(one, "lev", split_axis=0, concat_axis=0, tiled=True)
-        arrived.append(one.reshape(tiles * SUBS, -1))
+    arrived = lax.all_to_all(outgoing, "lev", split_axis=0, concat_axis=0, tiled=True)
+    arrived = arrived.reshape(tiles * SUBS, -1)
 
     slot = jnp.arange(levels)
     core = (mem + slot // 16) % CORES
-    ring = (mem // CORES + (1 - 2 * core) * (slot // 4)) % RING
+    ring = (mem // CORES + slot // 4) % RING
     half = (mem // (CORES * RING) + slot // 2) % HALVES
     row_level = half * 16 + ring * 4 + core * 2 + slot % 2
     order = (row_level[:, None] == slot[None, :]).astype(jnp.bfloat16)
@@ -302,9 +310,9 @@
 
     results = []
     begin = 0
-    for rows_here, one in zip(PIECES, arrived):
+    for rows_here in PIECES:
         own, other = localize(
-            begin, rows_here, place, tile_widths, one, weight, order, perturbations
+            begin, rows_here, place, tile_widths, arrived, weight, order, perturbations
         )
         results.append(sum_members(own, other))
         begin += rows_here
@@ -323,18 +331,18 @@
         for z in range(HALVES):
             for x in range(RING):
                 for c in range(CORES):
-                    along = dx * (1 - 2 * c)
-                    to = ((z + dz) % HALVES, (x + along) % RING, (c + dc) % CORES)
+                    to = ((z + dz) % HALVES, (x + dx) % RING, (c + dc) % CORES)
                     pairs.append(((z * RING + x) * CORES + c, (to[0] * RING + to[1]) * CORES + to[2]))
         return pairs
 
+    keep = own.shape[0] // RING
     came = lax.ppermute(other, "mem", moved(0, 0, 1))
-    pair = (wide(own) + wide(came)).reshape(RING, own.shape[0] // RING, own.shape[1])
-    relay = lax.ppermute(narrow(pair[2]), "mem", moved(0, 1, 0))
-    direct = lax.ppermute(narrow(pair[3]), "mem", moved(0, -1, 0))
-    joined = lax.ppermute(narrow(pair[1] + wide(relay)), "mem", moved(0, 1, 0))
-    total = pair[0] + wide(direct) + wide(joined)
-    keep = total.shape[0] // HALVES
+    total = wide(own[:keep]) + wide(came[:keep])
+    pair = narrow(wide(own[keep:]) + wide(came[keep:])).reshape(RING - 1, keep, -1)
+    around = [lax.ppermute(pair[d - 1], "mem", moved(0, d, 0)) for d in range(1, RING)]
+    for one in around:
+        total = total + wide(one)
+    keep //= HALVES
     far = lax.ppermute(narrow(total[keep:]), "mem", moved(1, 0, 0))
     return total[:keep] + wide(far)
 

time: 114 us -> 94.3 us (0.83); the launches traced: 112 us -> 94 us
  starting transfers between devices: 32.7 us -> 25.1 us
  Pallas kernels: 23.7 us -> 19.7 us
  other arithmetic: 4.95 us -> 2.03 us
  local copies, waits for them, and re-layouts: 3.11 us -> 0.72 us
  waiting for transfers between devices: 47.5 us -> 46.3 us
    all_to_all x2 -> x1, waiting for transfers between devices: 42.3 us -> 38.3 us  [body(): lax.all_to_all(outgoing, 'lev', split_axis=0, concat_axis=0, tiled=True)]
    all_to_all x2 -> x1, starting transfers between devices: 12.8 us -> 9.32 us  [body(): lax.all_to_all(outgoing, 'lev', split_axis=0, concat_axis=0, tiled=True)]
    ppermute x6, waiting for transfers between devices: 0.02 us -> 3.44 us  [sum_members(): lax.ppermute(pair[d - 1], 'mem', moved(0, d, 0))]
    pallas_call x2, Pallas kernels: 7.83 us -> 4.44 us  [localize(): pl.pallas_call(functools.partial(localize_kernel, begin_row), grid=(rows...]
    ppermute x6, starting transfers between devices: 10.2 us -> 7.07 us  [sum_members(): lax.ppermute(pair[d - 1], 'mem', moved(0, d, 0))]
    unnamed x10 -> x8, local copies, waits for them, and re-layouts: 1.86 us -> 0.03 us
    convert_element_type x1 -> x0, other arithmetic: 1.5 us -> none  [smooth_and_cut(): (natural == spaced % LANES * blocks + spaced // LANES).astype(jnp.bfloat16)]
    ppermute x2, starting transfers between devices: 2.99 us -> 1.6 us  [sum_members(): came = lax.ppermute(other, 'mem', moved(0, 0, 1))]
  transfers between devices with their start and end apart: 12 -> 11, of which waited for: 4 -> 4; matrix products, arithmetic and copies ran while one was open for 3% -> 2% of each run, Pallas kernels for 0% -> 2%
where the time goes in v3:
time: 94.3 us; the launch traced here: 94 us
  waiting for transfers between devices  46.3 us (49%)
  starting transfers between devices  25.1 us (27%)
  Pallas kernels  19.7 us (21%)
  other arithmetic  2.03 us (2%)
    all_to_all x1, waiting for transfers between devices, body(): lax.all_to_all(outgoing, 'lev', split_axis=0, concat_axis=0, tiled=True)  38.3 us
    pallas_call x1, Pallas kernels, smooth_and_cut(): pl.pallas_call(diffuse_kernel, out_shape=jax.ShapeDtypeStruct((tiles, SUB...  15.2 us
    all_to_all x1, starting transfers between devices, body(): lax.all_to_all(outgoing, 'lev', split_axis=0, concat_axis=0, tiled=True)  9.32 us
    ppermute x2, starting transfers between devices, sum_members(): far = lax.ppermute(narrow(total[keep:]), 'mem', moved(1, 0, 0))  7.07 us
    ppermute x6, starting transfers between devices, sum_members(): lax.ppermute(pair[d - 1], 'mem', moved(0, d, 0))  7.07 us
    ppermute x2, waiting for transfers between devices, sum_members(): far = lax.ppermute(narrow(total[keep:]), 'mem', moved(1, 0, 0))  4.57 us
    pallas_call x2, Pallas kernels, localize(): pl.pallas_call(functools.partial(localize_kernel, begin_row), grid=(rows...  4.44 us
    ppermute x6, waiting for transfers between devices, sum_members(): lax.ppermute(pair[d - 1], 'mem', moved(0, d, 0))  3.44 us
  transfers between devices with their start and end apart: 11, of which 4 were waited for; matrix products, arithmetic and copies ran while one was open for 2% of the time, Pallas kernels for 2%

profile of v3, /device:TPU:1, one launch (start us, length us, event | category | flops | bytes accessed | tf_op | source)
XLA Modules:
  0.0 94.0 jit_solution(7735628429054682575)
XLA Ops:
  0.0 15.2 %diffuse.1 = bf16[16,8,6272]{2,1,0:T(8,128)(2,1)} custom-call(s32[1]{0:T(128)} %bitcast.place_ref, f32[32]{0:T(128)} %scale_ref.1, s32[32]{0:T(128)} %map_ref.1, s32[16]{0:T(128)} %width_ref.5, f32[1,2,384,512]{3,2,1,0:T(8,128)} %alpha_ref.1, f32[384,512]{1,0:T(8,128)} %cx_ref.1, f32[384,512]{1,0:T(8,128)} %cy_ref.1), custom_call_target="tpu_custom_call" | custom-call | tf_op jit(solution)/shard_map/diffuse/pallas_call | solution.py:166
  15.3 0.0 copy-start.2
  15.3 0.0 copy-start.3
  15.3 0.0 copy-start
  15.3 0.0 copy-start.1
  15.3 9.3 %all-to-all-start = ((bf16[16,8,6272]{2,1,0:T(8,128)(2,1)}), bf16[16,8,6272]{2,1,0:T(8,128)(2,1)S(1)}, u32[]{:S(2)}, u32[]{:S(2)}) async-start(bf16[16,8,6272]{2,1,0:T(8,128)(2,1)} %diffuse.1), calls=%async_computation | async-start | bytes 3211264 | tf_op jit(solution)/shard_map/all_to_all | solution.py:293
  24.6 0.1 sub.48
  24.8 0.2 select_reduce_fusion.1
  24.9 0.1 min.20
  25.0 0.1 compare_select_fusion
  25.2 0.1 select_convert_fusion
  25.3 0.1 convert_element_type.83
  25.4 0.1 copy.9.weight_ref
  25.5 0.1 fusion.1.order_ref
  25.6 38.3 %all-to-all-done = bf16[16,8,6272]{2,1,0:T(8,128)(2,1)S(1)} async-done(((bf16[16,8,6272]{2,1,0:T(8,128)(2,1)}), bf16[16,8,6272]{2,1,0:T(8,128)(2,1)S(1)}, u32[]{:S(2)}, u32[]{:S(2)}) %all-to-all-start) | async-done | bytes 1605664 | tf_op jit(solution)/shard_map/all_to_all | solution.py:293
  63.9 2.2 %localize.3 = (bf16[16,12288]{1,0:T(8,128)(2,1)S(1)}, bf16[16,12288]{1,0:T(8,128)(2,1)S(1)}) custom-call(s32[1]{0:T(128)} %bitcast.place_ref, s32[16]{0:T(128)S(1)} %copy-done.1, bf16[128,6272]{1,0:T(8,128)(2,1)S(1)} %bitcast.4, bf16[128,128]{1,0:T(8,128)(2,1)S(1)} %copy.9.weight_ref, bf16[32,32]{1,0:T(8,128)(2,1)S(1)} %fusion.1.order_ref, ...), custom_call_target="tpu_custom_call" | custom-call | tf_op jit(solution)/shard_map/localize/pallas_call | solution.py:263
  66.2 1.5 %collective-permute-start.5 = (bf16[16,12288]{1,0:T(8,128)(2,1)S(1)}, bf16[16,12288]{1,0:T(8,128)(2,1)S(1)}, u32[]{:S(2)}, u32[]{:S(2)}) collective-permute-start(bf16[16,12288]{1,0:T(8,128)(2,1)S(1)} %get-tuple-element.12), channel_id=1, source_target_pairs={{0,16},{16,0},{32,48},{48,32},{64,80},{80,64},{96,112},{112,96},{1... | collective-permute-start | bytes 1179656 | tf_op jit(solution)/shard_map/ppermute | solution.py:339
  67.6 2.2 %localize.2 = (bf16[16,12288]{1,0:T(8,128)(2,1)S(1)}, bf16[16,12288]{1,0:T(8,128)(2,1)S(1)}) custom-call(s32[1]{0:T(128)} %bitcast.place_ref, s32[16]{0:T(128)S(1)} %copy-done.1, bf16[128,6272]{1,0:T(8,128)(2,1)S(1)} %bitcast.5, bf16[128,128]{1,0:T(8,128)(2,1)S(1)} %copy.9.weight_ref, bf16[32,32]{1,0:T(8,128)(2,1)S(1)} %fusion.1.order_ref, ...), custom_call_target="tpu_custom_call" | custom-call | tf_op jit(solution)/shard_map/localize/pallas_call | solution.py:263
  69.9 0.1 collective-permute-start
  70.0 0.0 collective-permute-done.5
  70.0 0.2 add_convert_fusion
  70.2 0.1 fusion.16
  70.3 2.6 %collective-permute-start.8 = (bf16[4,12288]{1,0:T(4,128)(2,1)S(1)}, bf16[4,12288]{1,0:T(4,128)(2,1)S(1)}, u32[]{:S(2)}, u32[]{:S(2)}) collective-permute-start(bf16[4,12288]{1,0:T(4,128)(2,1)S(1)} %get-tuple-element.19), channel_id=1, source_target_pairs={{0,96},{16,112},{32,0},{48,16},{64,32},{80,48},{96,64},{112,80},{1... | collective-permute-start | bytes 294920 | tf_op jit(solution)/shard_map/ppermute | solution.py:342
  72.8 0.5 collective-permute-start.7
  73.3 0.6 collective-permute-start.6
  74.0 0.0 collective-permute-done
  74.0 0.2 add_convert_fusion.1
  74.2 0.1 fusion.15
  74.3 2.1 %collective-permute-start.3 = (bf16[4,12288]{1,0:T(4,128)(2,1)S(1)}, bf16[4,12288]{1,0:T(4,128)(2,1)S(1)}, u32[]{:S(2)}, u32[]{:S(2)}) collective-permute-start(bf16[4,12288]{1,0:T(4,128)(2,1)S(1)} %get-tuple-element.16), channel_id=1, source_target_pairs={{0,96},{16,112},{32,0},{48,16},{64,32},{80,48},{96,64},{112,80},{1... | collective-permute-start | bytes 294920 | tf_op jit(solution)/shard_map/ppermute | solution.py:342
  76.4 1.3 %collective-permute-start.2 = (bf16[4,12288]{1,0:T(4,128)(2,1)S(1)}, bf16[4,12288]{1,0:T(4,128)(2,1)S(1)}, u32[]{:S(2)}, u32[]{:S(2)}) collective-permute-start(bf16[4,12288]{1,0:T(4,128)(2,1)S(1)} %get-tuple-element.17), channel_id=1, source_target_pairs={{0,64},{16,80},{32,96},{48,112},{64,0},{80,16},{96,32},{112,48},{1... | collective-permute-start | bytes 294920 | tf_op jit(solution)/shard_map/ppermute | solution.py:342
  77.7 0.0 collective-permute-done.8
  77.7 0.0 collective-permute-start.1
  77.7 0.2 collective-permute-done.7
  77.9 3.2 %collective-permute-done.6 = bf16[4,12288]{1,0:T(4,128)(2,1)S(1)} collective-permute-done((bf16[4,12288]{1,0:T(4,128)(2,1)S(1)}, bf16[4,12288]{1,0:T(4,128)(2,1)S(1)}, u32[]{:S(2)}, u32[]{:S(2)}) %collective-permute-start.6) | collective-permute-done | bytes 98336 | tf_op jit(solution)/shard_map/ppermute | solution.py:342
  81.1 0.1 convert_add_fusion
  81.2 0.1 slice.106
  81.3 4.3 %collective-permute-start.9 = (bf16[2,12288]{1,0:T(2,128)(2,1)S(1)}, bf16[2,12288]{1,0:T(2,128)(2,1)S(1)}, u32[]{:S(2)}, u32[]{:S(2)}) collective-permute-start(bf16[2,12288]{1,0:T(2,128)(2,1)S(1)} %slice.106), channel_id=1, source_target_pairs={{0,128},{16,144},{32,160},{48,176},{64,192},{80,208},{96,224},{112... | collective-permute-start | bytes 147464 | tf_op jit(solution)/shard_map/ppermute | solution.py:346
  85.6 0.0 collective-permute-done.3
  85.6 0.0 collective-permute-done.2
  85.6 0.0 collective-permute-done.1
  85.6 0.1 convert_add_fusion.1
  85.7 0.1 slice.107
  85.8 2.8 %collective-permute-start.4 = (bf16[2,12288]{1,0:T(2,128)(2,1)S(1)}, bf16[2,12288]{1,0:T(2,128)(2,1)S(1)}, u32[]{:S(2)}, u32[]{:S(2)}) collective-permute-start(bf16[2,12288]{1,0:T(2,128)(2,1)S(1)} %slice.107), channel_id=1, source_target_pairs={{0,128},{16,144},{32,160},{48,176},{64,192},{80,208},{96,224},{112... | collective-permute-start | bytes 147464 | tf_op jit(solution)/shard_map/ppermute | solution.py:346
  88.6 0.0 collective-permute-done.9
  88.6 0.1 slice_add_fusion
  88.6 4.6 %collective-permute-done.4 = bf16[2,12288]{1,0:T(2,128)(2,1)S(1)} collective-permute-done((bf16[2,12288]{1,0:T(2,128)(2,1)S(1)}, bf16[2,12288]{1,0:T(2,128)(2,1)S(1)}, u32[]{:S(2)}, u32[]{:S(2)}) %collective-permute-start.4) | collective-permute-done | bytes 49184 | tf_op jit(solution)/shard_map/ppermute | solution.py:346
  93.2 0.1 slice_add_fusion.1
  93.3 0.8 pad_maximum_fusion
  (6 shorter events, 0.0 us)
Async XLA Ops:
  15.3 9.4 %copy-start.2 = (s32[32]{0:T(128)S(1)}, s32[32]{0:T(128)}, u32[]{:S(2)}) copy-start(s32[32]{0:T(128)} %map_ref.1) | copy-start | bytes 388
  15.3 9.5 %copy-start.3 = (s32[32]{0:T(128)S(1)}, s32[32]{0:T(128)}, u32[]{:S(2)}) copy-start(s32[32]{0:T(128)} %param.15) | copy-start | bytes 388
  15.3 48.6 %copy-start = (bf16[1,32,24576]{2,1,0:T(8,128)(2,1)S(1)}, bf16[1,32,24576]{2,1,0:T(8,128)(2,1)}, u32[]{:S(2)}) copy-start(bf16[1,32,24576]{2,1,0:T(8,128)(2,1)} %pert_ref.3) | copy-start | bytes 4718596
  15.3 48.6 %copy-start.1 = (s32[16]{0:T(128)S(1)}, s32[16]{0:T(128)}, u32[]{:S(2)}) copy-start(s32[16]{0:T(128)} %width_ref.5) | copy-start | bytes 196
  15.3 48.6 %all-to-all-start = ((bf16[16,8,6272]{2,1,0:T(8,128)(2,1)}), bf16[16,8,6272]{2,1,0:T(8,128)(2,1)S(1)}, u32[]{:S(2)}, u32[]{:S(2)}) async-start(bf16[16,8,6272]{2,1,0:T(8,128)(2,1)} %diffuse.1), calls=%async_computation | async-start | bytes 3211264 | tf_op jit(solution)/shard_map/all_to_all | solution.py:293
  66.2 3.8 %collective-permute-start.5 = (bf16[16,12288]{1,0:T(8,128)(2,1)S(1)}, bf16[16,12288]{1,0:T(8,128)(2,1)S(1)}, u32[]{:S(2)}, u32[]{:S(2)}) collective-permute-start(bf16[16,12288]{1,0:T(8,128)(2,1)S(1)} %get-tuple-element.12), channel_id=1, source_target_pairs={{0,16},{16,0},{32,48},{48,32},{64,80},{80,64},{96,112},{112,96},{1... | collective-permute-start | bytes 1179656 | tf_op jit(solution)/shard_map/ppermute | solution.py:339
  69.9 4.1 %collective-permute-start = (bf16[16,12288]{1,0:T(8,128)(2,1)S(1)}, bf16[16,12288]{1,0:T(8,128)(2,1)S(1)}, u32[]{:S(2)}, u32[]{:S(2)}) collective-permute-start(bf16[16,12288]{1,0:T(8,128)(2,1)S(1)} %get-tuple-element.10), channel_id=1, source_target_pairs={{0,16},{16,0},{32,48},{48,32},{64,80},{80,64},{96,112},{112,96},{1... | collective-permute-start | bytes 1179656 | tf_op jit(solution)/shard_map/ppermute | solution.py:339
  70.3 7.4 %collective-permute-start.8 = (bf16[4,12288]{1,0:T(4,128)(2,1)S(1)}, bf16[4,12288]{1,0:T(4,128)(2,1)S(1)}, u32[]{:S(2)}, u32[]{:S(2)}) collective-permute-start(bf16[4,12288]{1,0:T(4,128)(2,1)S(1)} %get-tuple-element.19), channel_id=1, source_target_pairs={{0,96},{16,112},{32,0},{48,16},{64,32},{80,48},{96,64},{112,80},{1... | collective-permute-start | bytes 294920 | tf_op jit(solution)/shard_map/ppermute | solution.py:342
  72.8 5.1 %collective-permute-start.7 = (bf16[4,12288]{1,0:T(4,128)(2,1)S(1)}, bf16[4,12288]{1,0:T(4,128)(2,1)S(1)}, u32[]{:S(2)}, u32[]{:S(2)}) collective-permute-start(bf16[4,12288]{1,0:T(4,128)(2,1)S(1)} %get-tuple-element.20), channel_id=1, source_target_pairs={{0,64},{16,80},{32,96},{48,112},{64,0},{80,16},{96,32},{112,48},{1... | collective-permute-start | bytes 294920 | tf_op jit(solution)/shard_map/ppermute | solution.py:342
  73.3 7.7 %collective-permute-start.6 = (bf16[4,12288]{1,0:T(4,128)(2,1)S(1)}, bf16[4,12288]{1,0:T(4,128)(2,1)S(1)}, u32[]{:S(2)}, u32[]{:S(2)}) collective-permute-start(bf16[4,12288]{1,0:T(4,128)(2,1)S(1)} %get-tuple-element.18), channel_id=1, source_target_pairs={{0,32},{16,48},{32,64},{48,80},{64,96},{80,112},{96,0},{112,16},{1... | collective-permute-start | bytes 294920 | tf_op jit(solution)/shard_map/ppermute | solution.py:342
  74.3 11.3 %collective-permute-start.3 = (bf16[4,12288]{1,0:T(4,128)(2,1)S(1)}, bf16[4,12288]{1,0:T(4,128)(2,1)S(1)}, u32[]{:S(2)}, u32[]{:S(2)}) collective-permute-start(bf16[4,12288]{1,0:T(4,128)(2,1)S(1)} %get-tuple-element.16), channel_id=1, source_target_pairs={{0,96},{16,112},{32,0},{48,16},{64,32},{80,48},{96,64},{112,80},{1... | collective-permute-start | bytes 294920 | tf_op jit(solution)/shard_map/ppermute | solution.py:342
  76.4 9.2 %collective-permute-start.2 = (bf16[4,12288]{1,0:T(4,128)(2,1)S(1)}, bf16[4,12288]{1,0:T(4,128)(2,1)S(1)}, u32[]{:S(2)}, u32[]{:S(2)}) collective-permute-start(bf16[4,12288]{1,0:T(4,128)(2,1)S(1)} %get-tuple-element.17), channel_id=1, source_target_pairs={{0,64},{16,80},{32,96},{48,112},{64,0},{80,16},{96,32},{112,48},{1... | collective-permute-start | bytes 294920 | tf_op jit(solution)/shard_map/ppermute | solution.py:342
  77.7 7.9 %collective-permute-start.1 = (bf16[4,12288]{1,0:T(4,128)(2,1)S(1)}, bf16[4,12288]{1,0:T(4,128)(2,1)S(1)}, u32[]{:S(2)}, u32[]{:S(2)}) collective-permute-start(bf16[4,12288]{1,0:T(4,128)(2,1)S(1)} %get-tuple-element.15), channel_id=1, source_target_pairs={{0,32},{16,48},{32,64},{48,80},{64,96},{80,112},{96,0},{112,16},{1... | collective-permute-start | bytes 294920 | tf_op jit(solution)/shard_map/ppermute | solution.py:342
  81.3 7.3 %collective-permute-start.9 = (bf16[2,12288]{1,0:T(2,128)(2,1)S(1)}, bf16[2,12288]{1,0:T(2,128)(2,1)S(1)}, u32[]{:S(2)}, u32[]{:S(2)}) collective-permute-start(bf16[2,12288]{1,0:T(2,128)(2,1)S(1)} %slice.106), channel_id=1, source_target_pairs={{0,128},{16,144},{32,160},{48,176},{64,192},{80,208},{96,224},{112... | collective-permute-start | bytes 147464 | tf_op jit(solution)/shard_map/ppermute | solution.py:346
  85.8 7.4 %collective-permute-start.4 = (bf16[2,12288]{1,0:T(2,128)(2,1)S(1)}, bf16[2,12288]{1,0:T(2,128)(2,1)S(1)}, u32[]{:S(2)}, u32[]{:S(2)}) collective-permute-start(bf16[2,12288]{1,0:T(2,128)(2,1)S(1)} %slice.107), channel_id=1, source_target_pairs={{0,128},{16,144},{32,160},{48,176},{64,192},{80,208},{96,224},{112... | collective-permute-start | bytes 147464 | tf_op jit(solution)/shard_map/ppermute | solution.py:346

commit v4 on v3

--- a/solution.py
+++ b/solution.py
@@ -123,17 +123,21 @@
                     flux.append(fx)
                 here, before = after, flux
 
-        x_scr[...] = jnp.dot(
+        natural = jnp.dot(
             f_scr[pl.ds(0, rows), :].astype(jnp.bfloat16),
             gather_ref[...],
             preferred_element_type=jnp.float32,
         )
         for r in range(fold):
             for b in range(blocks):
-                o_scr[pl.ds(r * SUBS + b * levels + v, SUBS, stride=rows), :] = x_scr[at(r), part(b)]
-
-    for i in range(rows):
-        msg_scr[:, part(i)] = o_scr[at(i), :].astype(jnp.bfloat16)
+                o_scr[at(r * SUBS + b * levels + v), :] = natural[
+                    r * SUBS : (r + 1) * SUBS, b * LANES : (b + 1) * LANES
+                ]
+
+    for r in range(fold):
+        for i in range(SUBS):
+            row = o_scr[pl.ds(r * SUBS * SUBS + i, SUBS, stride=SUBS), :]
+            msg_scr[:, part(i * fold + r)] = row.astype(jnp.bfloat16)
     spare = msg_scr.shape[1] - rows * LANES
     msg_scr[:, pl.ds(rows * LANES, spare)] = jnp.zeros((SUBS, spare), jnp.bfloat16)
     sends = []
@@ -295,7 +299,7 @@
 
     slot = jnp.arange(levels)
     core = (mem + slot // 16) % CORES
-    ring = (mem // CORES + slot // 4) % RING
+    ring = (mem // CORES + (1 - 2 * core) * (slot // 4)) % RING
     half = (mem // (CORES * RING) + slot // 2) % HALVES
     row_level = half * 16 + ring * 4 + core * 2 + slot % 2
     order = (row_level[:, None] == slot[None, :]).astype(jnp.bfloat16)
@@ -331,17 +335,20 @@
         for z in range(HALVES):
             for x in range(RING):
                 for c in range(CORES):
-                    to = ((z + dz) % HALVES, (x + dx) % RING, (c + dc) % CORES)
+                    along = dx * (1 - 2 * c)
+                    to = ((z + dz) % HALVES, (x + along) % RING, (c + dc) % CORES)
                     pairs.append(((z * RING + x) * CORES + c, (to[0] * RING + to[1]) * CORES + to[2]))
         return pairs
 
     keep = own.shape[0] // RING
     came = lax.ppermute(other, "mem", moved(0, 0, 1))
     total = wide(own[:keep]) + wide(came[:keep])
-    pair = narrow(wide(own[keep:]) + wide(came[keep:])).reshape(RING - 1, keep, -1)
-    around = [lax.ppermute(pair[d - 1], "mem", moved(0, d, 0)) for d in range(1, RING)]
-    for one in around:
-        total = total + wide(one)
+    beside = wide(own[keep : 2 * keep]) + wide(came[keep : 2 * keep])
+    pair = narrow(wide(own[2 * keep :]) + wide(came[2 * keep :]))
+    relay = lax.ppermute(pair[:keep], "mem", moved(0, 1, 0))
+    direct = lax.ppermute(pair[keep:], "mem", moved(0, -1, 0))
+    joined = lax.ppermute(narrow(beside + wide(relay)), "mem", moved(0, 1, 0))
+    total = total + wide(direct) + wide(joined)
     keep //= HALVES
     far = lax.ppermute(narrow(total[keep:]), "mem", moved(1, 0, 0))
     return total[:keep] + wide(far)

time: 94.3 us -> 93.7 us (level); the launches traced: 94 us -> 92.3 us
  waiting for transfers between devices: 46.3 us -> 43.4 us
  starting transfers between devices: 25.1 us -> 26.9 us
    ppermute x6, waiting for transfers between devices: 3.44 us -> 0.02 us  [the longest x2 0.01 us: sum_members(): direct = lax.ppermute(pair[keep:], 'mem', moved(0, -1, 0))]
    ppermute x6, starting transfers between devices: 7.07 us -> 9.9 us  [the longest x2 5.31 us: sum_members(): relay = lax.ppermute(pair[:keep], 'mem', moved(0, 1, 0))]
    ppermute x2, starting transfers between devices: 7.07 us -> 6.12 us  [sum_members(): far = lax.ppermute(narrow(total[keep:]), 'mem', moved(1, 0, 0))]
  transfers between devices with their start and end apart: 11 -> 11, of which waited for: 4 -> 3; matrix products, arithmetic and copies ran while one was open for 2% -> 2% of each run, Pallas kernels for 2% -> 2%
where the time goes in v4:
time: 93.7 us; the launch traced here: 92.3 us
  waiting for transfers between devices  43.4 us (46%)
  starting transfers between devices  26.9 us (29%)
  Pallas kernels  19.2 us (20%)
  other arithmetic  2.01 us (2%)
    all_to_all x1, waiting for transfers between devices, body(): lax.all_to_all(outgoing, 'lev', split_axis=0, concat_axis=0, tiled=True)  38.3 us
    pallas_call x1, Pallas kernels, smooth_and_cut(): pl.pallas_call(diffuse_kernel, out_shape=jax.ShapeDtypeStruct((tiles, SUB...  14.7 us
    all_to_all x1, starting transfers between devices, body(): lax.all_to_all(outgoing, 'lev', split_axis=0, concat_axis=0, tiled=True)  9.32 us
    ppermute x2, starting transfers between devices, sum_members(): far = lax.ppermute(narrow(total[keep:]), 'mem', moved(1, 0, 0))  6.12 us
    ppermute x2, starting transfers between devices, sum_members(): relay = lax.ppermute(pair[:keep], 'mem', moved(0, 1, 0))  5.31 us
    ppermute x2, waiting for transfers between devices, sum_members(): far = lax.ppermute(narrow(total[keep:]), 'mem', moved(1, 0, 0))  5.05 us
    ppermute x2, starting transfers between devices, sum_members(): joined = lax.ppermute(narrow(beside + wide(relay)), 'mem', moved(0, 1, 0))  4.59 us
    pallas_call x2, Pallas kernels, localize(): pl.pallas_call(functools.partial(localize_kernel, begin_row), grid=(rows...  4.44 us
  transfers between devices with their start and end apart: 11, of which 3 were waited for; matrix products, arithmetic and copies ran while one was open for 2% of the time, Pallas kernels for 2%

profile of v4, /device:TPU:1, one launch (start us, length us, event | category | flops | bytes accessed | tf_op | source)
XLA Modules:
  0.0 92.3 jit_solution(8439616724102226300)
XLA Ops:
  0.0 14.7 %diffuse.1 = bf16[16,8,6272]{2,1,0:T(8,128)(2,1)} custom-call(s32[1]{0:T(128)} %bitcast.place_ref, f32[32]{0:T(128)} %scale_ref.1, s32[32]{0:T(128)} %map_ref.1, s32[16]{0:T(128)} %width_ref.5, f32[1,2,384,512]{3,2,1,0:T(8,128)} %alpha_ref.1, f32[384,512]{1,0:T(8,128)} %cx_ref.1, f32[384,512]{1,0:T(8,128)} %cy_ref.1), custom_call_target="tpu_custom_call" | custom-call | tf_op jit(solution)/shard_map/diffuse/pallas_call | solution.py:170
  14.7 0.0 copy-start.2
  14.7 0.0 copy-start.3
  14.8 0.0 copy-start
  14.8 0.0 copy-start.1
  14.8 9.3 %all-to-all-start = ((bf16[16,8,6272]{2,1,0:T(8,128)(2,1)}), bf16[16,8,6272]{2,1,0:T(8,128)(2,1)S(1)}, u32[]{:S(2)}, u32[]{:S(2)}) async-start(bf16[16,8,6272]{2,1,0:T(8,128)(2,1)} %diffuse.1), calls=%async_computation | async-start | bytes 3211264 | tf_op jit(solution)/shard_map/all_to_all | solution.py:297
  24.1 0.1 sub.57
  24.2 0.2 select_reduce_fusion.1
  24.4 0.1 min.20
  24.5 0.1 compare_select_fusion
  24.7 0.1 select_convert_fusion
  24.8 0.1 convert_element_type.101
  24.9 0.1 copy.9.weight_ref
  25.0 0.1 fusion.1.order_ref
  25.1 38.3 %all-to-all-done = bf16[16,8,6272]{2,1,0:T(8,128)(2,1)S(1)} async-done(((bf16[16,8,6272]{2,1,0:T(8,128)(2,1)}), bf16[16,8,6272]{2,1,0:T(8,128)(2,1)S(1)}, u32[]{:S(2)}, u32[]{:S(2)}) %all-to-all-start) | async-done | bytes 1605664 | tf_op jit(solution)/shard_map/all_to_all | solution.py:297
  63.4 2.2 %localize.3 = (bf16[16,12288]{1,0:T(8,128)(2,1)S(1)}, bf16[16,12288]{1,0:T(8,128)(2,1)S(1)}) custom-call(s32[1]{0:T(128)} %bitcast.place_ref, s32[16]{0:T(128)S(1)} %copy-done.1, bf16[128,6272]{1,0:T(8,128)(2,1)S(1)} %bitcast.4, bf16[128,128]{1,0:T(8,128)(2,1)S(1)} %copy.9.weight_ref, bf16[32,32]{1,0:T(8,128)(2,1)S(1)} %fusion.1.order_ref, ...), custom_call_target="tpu_custom_call" | custom-call | tf_op jit(solution)/shard_map/localize/pallas_call | solution.py:267
  65.6 1.5 %collective-permute-start.5 = (bf16[16,12288]{1,0:T(8,128)(2,1)S(1)}, bf16[16,12288]{1,0:T(8,128)(2,1)S(1)}, u32[]{:S(2)}, u32[]{:S(2)}) collective-permute-start(bf16[16,12288]{1,0:T(8,128)(2,1)S(1)} %get-tuple-element.12), channel_id=1, source_target_pairs={{0,16},{16,0},{32,48},{48,32},{64,80},{80,64},{96,112},{112,96},{1... | collective-permute-start | bytes 1179656 | tf_op jit(solution)/shard_map/ppermute | solution.py:344
  67.1 2.2 %localize.2 = (bf16[16,12288]{1,0:T(8,128)(2,1)S(1)}, bf16[16,12288]{1,0:T(8,128)(2,1)S(1)}) custom-call(s32[1]{0:T(128)} %bitcast.place_ref, s32[16]{0:T(128)S(1)} %copy-done.1, bf16[128,6272]{1,0:T(8,128)(2,1)S(1)} %bitcast.5, bf16[128,128]{1,0:T(8,128)(2,1)S(1)} %copy.9.weight_ref, bf16[32,32]{1,0:T(8,128)(2,1)S(1)} %fusion.1.order_ref, ...), custom_call_target="tpu_custom_call" | custom-call | tf_op jit(solution)/shard_map/localize/pallas_call | solution.py:267
  69.3 0.1 collective-permute-start
  69.5 0.0 collective-permute-done.5
  69.5 0.1 add_convert_fusion
  69.5 0.1 fusion.16
  69.6 2.6 %collective-permute-start.7 = (bf16[4,12288]{1,0:T(4,128)(2,1)S(1)}, bf16[4,12288]{1,0:T(4,128)(2,1)S(1)}, u32[]{:S(2)}, u32[]{:S(2)}) collective-permute-start(bf16[4,12288]{1,0:T(4,128)(2,1)S(1)} %get-tuple-element.18), channel_id=1, source_target_pairs={{0,32},{16,112},{32,64},{48,16},{64,96},{80,48},{96,0},{112,80},{1... | collective-permute-start | bytes 294920 | tf_op jit(solution)/shard_map/ppermute | solution.py:348
  72.1 0.0 collective-permute-start.6
  72.1 0.0 collective-permute-done
  72.2 0.1 add_convert_fusion.1
  72.2 0.1 fusion.15
  72.3 2.8 %collective-permute-start.2 = (bf16[4,12288]{1,0:T(4,128)(2,1)S(1)}, bf16[4,12288]{1,0:T(4,128)(2,1)S(1)}, u32[]{:S(2)}, u32[]{:S(2)}) collective-permute-start(bf16[4,12288]{1,0:T(4,128)(2,1)S(1)} %get-tuple-element.16), channel_id=1, source_target_pairs={{0,32},{16,112},{32,64},{48,16},{64,96},{80,48},{96,0},{112,80},{1... | collective-permute-start | bytes 294920 | tf_op jit(solution)/shard_map/ppermute | solution.py:348
  75.0 0.0 collective-permute-start.1
  75.0 0.2 add_convert_fusion.2
  75.2 2.8 %collective-permute-start.8 = (bf16[4,12288]{1,0:T(4,128)(2,1)S(1)}, bf16[4,12288]{1,0:T(4,128)(2,1)S(1)}, u32[]{:S(2)}, u32[]{:S(2)}) collective-permute-start(bf16[4,12288]{1,0:T(4,128)(2,1)S(1)} %add_convert_fusion.2), channel_id=1, source_target_pairs={{0,32},{16,112},{32,64},{48,16},{64,96},{80,48},{96,0},{112,80},{1... | collective-permute-start | bytes 294920 | tf_op jit(solution)/shard_map/ppermute | solution.py:350
  78.0 0.2 add_convert_fusion.3
  78.1 1.8 %collective-permute-start.3 = (bf16[4,12288]{1,0:T(4,128)(2,1)S(1)}, bf16[4,12288]{1,0:T(4,128)(2,1)S(1)}, u32[]{:S(2)}, u32[]{:S(2)}) collective-permute-start(bf16[4,12288]{1,0:T(4,128)(2,1)S(1)} %add_convert_fusion.3), channel_id=1, source_target_pairs={{0,32},{16,112},{32,64},{48,16},{64,96},{80,48},{96,0},{112,80},{1... | collective-permute-start | bytes 294920 | tf_op jit(solution)/shard_map/ppermute | solution.py:350
  79.9 0.0 collective-permute-done.6
  79.9 0.0 collective-permute-done.8
  80.0 0.1 convert_add_fusion
  80.1 0.1 slice.112
  80.1 4.3 %collective-permute-start.9 = (bf16[2,12288]{1,0:T(2,128)(2,1)S(1)}, bf16[2,12288]{1,0:T(2,128)(2,1)S(1)}, u32[]{:S(2)}, u32[]{:S(2)}) collective-permute-start(bf16[2,12288]{1,0:T(2,128)(2,1)S(1)} %slice.112), channel_id=1, source_target_pairs={{0,128},{16,144},{32,160},{48,176},{64,192},{80,208},{96,224},{112... | collective-permute-start | bytes 147464 | tf_op jit(solution)/shard_map/ppermute | solution.py:353
  84.4 0.0 collective-permute-done.1
  84.4 0.0 collective-permute-done.3
  84.4 0.1 convert_add_fusion.1
  84.5 0.1 slice.113
  84.6 1.8 %collective-permute-start.4 = (bf16[2,12288]{1,0:T(2,128)(2,1)S(1)}, bf16[2,12288]{1,0:T(2,128)(2,1)S(1)}, u32[]{:S(2)}, u32[]{:S(2)}) collective-permute-start(bf16[2,12288]{1,0:T(2,128)(2,1)S(1)} %slice.113), channel_id=1, source_target_pairs={{0,128},{16,144},{32,160},{48,176},{64,192},{80,208},{96,224},{112... | collective-permute-start | bytes 147464 | tf_op jit(solution)/shard_map/ppermute | solution.py:353
  86.4 0.7 collective-permute-done.9
  87.2 0.1 slice_add_fusion
  87.2 4.3 %collective-permute-done.4 = bf16[2,12288]{1,0:T(2,128)(2,1)S(1)} collective-permute-done((bf16[2,12288]{1,0:T(2,128)(2,1)S(1)}, bf16[2,12288]{1,0:T(2,128)(2,1)S(1)}, u32[]{:S(2)}, u32[]{:S(2)}) %collective-permute-start.4) | collective-permute-done | bytes 49184 | tf_op jit(solution)/shard_map/ppermute | solution.py:353
  91.5 0.1 slice_add_fusion.1
  91.6 0.8 pad_maximum_fusion
  (8 shorter events, 0.1 us)
Async XLA Ops:
  14.7 9.4 %copy-start.2 = (s32[32]{0:T(128)S(1)}, s32[32]{0:T(128)}, u32[]{:S(2)}) copy-start(s32[32]{0:T(128)} %map_ref.1) | copy-start | bytes 388
  14.7 9.5 %copy-start.3 = (s32[32]{0:T(128)S(1)}, s32[32]{0:T(128)}, u32[]{:S(2)}) copy-start(s32[32]{0:T(128)} %param.15) | copy-start | bytes 388
  14.8 48.6 %copy-start = (bf16[1,32,24576]{2,1,0:T(8,128)(2,1)S(1)}, bf16[1,32,24576]{2,1,0:T(8,128)(2,1)}, u32[]{:S(2)}) copy-start(bf16[1,32,24576]{2,1,0:T(8,128)(2,1)} %pert_ref.3) | copy-start | bytes 4718596
  14.8 48.6 %copy-start.1 = (s32[16]{0:T(128)S(1)}, s32[16]{0:T(128)}, u32[]{:S(2)}) copy-start(s32[16]{0:T(128)} %width_ref.5) | copy-start | bytes 196
  14.8 48.6 %all-to-all-start = ((bf16[16,8,6272]{2,1,0:T(8,128)(2,1)}), bf16[16,8,6272]{2,1,0:T(8,128)(2,1)S(1)}, u32[]{:S(2)}, u32[]{:S(2)}) async-start(bf16[16,8,6272]{2,1,0:T(8,128)(2,1)} %diffuse.1), calls=%async_computation | async-start | bytes 3211264 | tf_op jit(solution)/shard_map/all_to_all | solution.py:297
  65.6 3.8 %collective-permute-start.5 = (bf16[16,12288]{1,0:T(8,128)(2,1)S(1)}, bf16[16,12288]{1,0:T(8,128)(2,1)S(1)}, u32[]{:S(2)}, u32[]{:S(2)}) collective-permute-start(bf16[16,12288]{1,0:T(8,128)(2,1)S(1)} %get-tuple-element.12), channel_id=1, source_target_pairs={{0,16},{16,0},{32,48},{48,32},{64,80},{80,64},{96,112},{112,96},{1... | collective-permute-start | bytes 1179656 | tf_op jit(solution)/shard_map/ppermute | solution.py:344
  69.3 2.8 %collective-permute-start = (bf16[16,12288]{1,0:T(8,128)(2,1)S(1)}, bf16[16,12288]{1,0:T(8,128)(2,1)S(1)}, u32[]{:S(2)}, u32[]{:S(2)}) collective-permute-start(bf16[16,12288]{1,0:T(8,128)(2,1)S(1)} %get-tuple-element.10), channel_id=1, source_target_pairs={{0,16},{16,0},{32,48},{48,32},{64,80},{80,64},{96,112},{112,96},{1... | collective-permute-start | bytes 1179656 | tf_op jit(solution)/shard_map/ppermute | solution.py:344
  69.6 5.5 %collective-permute-start.7 = (bf16[4,12288]{1,0:T(4,128)(2,1)S(1)}, bf16[4,12288]{1,0:T(4,128)(2,1)S(1)}, u32[]{:S(2)}, u32[]{:S(2)}) collective-permute-start(bf16[4,12288]{1,0:T(4,128)(2,1)S(1)} %get-tuple-element.18), channel_id=1, source_target_pairs={{0,32},{16,112},{32,64},{48,16},{64,96},{80,48},{96,0},{112,80},{1... | collective-permute-start | bytes 294920 | tf_op jit(solution)/shard_map/ppermute | solution.py:348
  72.1 7.8 %collective-permute-start.6 = (bf16[4,12288]{1,0:T(4,128)(2,1)S(1)}, bf16[4,12288]{1,0:T(4,128)(2,1)S(1)}, u32[]{:S(2)}, u32[]{:S(2)}) collective-permute-start(bf16[4,12288]{1,0:T(4,128)(2,1)S(1)} %get-tuple-element.17), channel_id=1, source_target_pairs={{0,96},{16,48},{32,0},{48,80},{64,32},{80,112},{96,64},{112,16},{1... | collective-permute-start | bytes 294920 | tf_op jit(solution)/shard_map/ppermute | solution.py:349
  72.3 5.7 %collective-permute-start.2 = (bf16[4,12288]{1,0:T(4,128)(2,1)S(1)}, bf16[4,12288]{1,0:T(4,128)(2,1)S(1)}, u32[]{:S(2)}, u32[]{:S(2)}) collective-permute-start(bf16[4,12288]{1,0:T(4,128)(2,1)S(1)} %get-tuple-element.16), channel_id=1, source_target_pairs={{0,32},{16,112},{32,64},{48,16},{64,96},{80,48},{96,0},{112,80},{1... | collective-permute-start | bytes 294920 | tf_op jit(solution)/shard_map/ppermute | solution.py:348
  75.0 9.4 %collective-permute-start.1 = (bf16[4,12288]{1,0:T(4,128)(2,1)S(1)}, bf16[4,12288]{1,0:T(4,128)(2,1)S(1)}, u32[]{:S(2)}, u32[]{:S(2)}) collective-permute-start(bf16[4,12288]{1,0:T(4,128)(2,1)S(1)} %get-tuple-element.15), channel_id=1, source_target_pairs={{0,96},{16,48},{32,0},{48,80},{64,32},{80,112},{96,64},{112,16},{1... | collective-permute-start | bytes 294920 | tf_op jit(solution)/shard_map/ppermute | solution.py:349
  75.2 4.8 %collective-permute-start.8 = (bf16[4,12288]{1,0:T(4,128)(2,1)S(1)}, bf16[4,12288]{1,0:T(4,128)(2,1)S(1)}, u32[]{:S(2)}, u32[]{:S(2)}) collective-permute-start(bf16[4,12288]{1,0:T(4,128)(2,1)S(1)} %add_convert_fusion.2), channel_id=1, source_target_pairs={{0,32},{16,112},{32,64},{48,16},{64,96},{80,48},{96,0},{112,80},{1... | collective-permute-start | bytes 294920 | tf_op jit(solution)/shard_map/ppermute | solution.py:350
  78.1 6.3 %collective-permute-start.3 = (bf16[4,12288]{1,0:T(4,128)(2,1)S(1)}, bf16[4,12288]{1,0:T(4,128)(2,1)S(1)}, u32[]{:S(2)}, u32[]{:S(2)}) collective-permute-start(bf16[4,12288]{1,0:T(4,128)(2,1)S(1)} %add_convert_fusion.3), channel_id=1, source_target_pairs={{0,32},{16,112},{32,64},{48,16},{64,96},{80,48},{96,0},{112,80},{1... | collective-permute-start | bytes 294920 | tf_op jit(solution)/shard_map/ppermute | solution.py:350
  80.1 7.0 %collective-permute-start.9 = (bf16[2,12288]{1,0:T(2,128)(2,1)S(1)}, bf16[2,12288]{1,0:T(2,128)(2,1)S(1)}, u32[]{:S(2)}, u32[]{:S(2)}) collective-permute-start(bf16[2,12288]{1,0:T(2,128)(2,1)S(1)} %slice.112), channel_id=1, source_target_pairs={{0,128},{16,144},{32,160},{48,176},{64,192},{80,208},{96,224},{112... | collective-permute-start | bytes 147464 | tf_op jit(solution)/shard_map/ppermute | solution.py:353
  84.6 6.9 %collective-permute-start.4 = (bf16[2,12288]{1,0:T(2,128)(2,1)S(1)}, bf16[2,12288]{1,0:T(2,128)(2,1)S(1)}, u32[]{:S(2)}, u32[]{:S(2)}) collective-permute-start(bf16[2,12288]{1,0:T(2,128)(2,1)S(1)} %slice.113), channel_id=1, source_target_pairs={{0,128},{16,144},{32,160},{48,176},{64,192},{80,208},{96,224},{112... | collective-permute-start | bytes 147464 | tf_op jit(solution)/shard_map/ppermute | solution.py:353

commit v5 on v4

--- a/solution.py
+++ b/solution.py
@@ -12,6 +12,9 @@
 SUBS = 8
 ROWS_PER_BLOCK = 8
 PIECES = (24, 24)
+LINE = 4
+ROUND = 64
+ROUNDS = 2
 CORES, RING, HALVES = 2, 4, 2
 
 
@@ -22,9 +25,13 @@
 
 def diffuse_kernel(
     place_ref, scale_ref, map_ref, width_ref, alpha_ref, cx_ref, cy_ref,
-    out_ref, raw_scr, cx_scr, cy_scr, spread_ref, gather_ref, x_scr, f_scr, gx_scr, gy_scr, ax_scr,
-    ay_scr, ayr_scr, o_scr, msg_scr, sems, out_sem,
+    out_ref, *refs,
 ):
+    late_refs, more_ref = refs[: LINE * ROUNDS], refs[LINE * ROUNDS]
+    (
+        raw_scr, cx_scr, cy_scr, spread_ref, gather_ref, x_scr, f_scr, gx_scr, gy_scr, ax_scr,
+        ay_scr, ayr_scr, o_scr, msg_scr, late_scr, sems, out_sem, late_sem,
+    ) = refs[LINE * ROUNDS + 1 :]
     rows, cols = cx_ref.shape
     levels = alpha_ref.shape[1]
     fold = rows // SUBS
@@ -151,8 +158,39 @@
         )
         sends[-1].start()
         first_col = first_col + width_ref[t]
+    more = 0
+    tall = PIECES[0] + 1
+    for d in range(LINE):
+        plane = lax.rem(place_ref[0] + d, LINE)
+        filled = 0
+        for k in range(tiles // LINE):
+            first_col, count = late_rows(width_ref, k * LINE + plane, cols)
+            first = pl.multiple_of((first_col // cols + PIECES[0]) * LANES, LANES)
+            to = pl.multiple_of(filled * LANES, LANES)
+            late_scr[d, :, pl.ds(to, tall * LANES)] = msg_scr[:, pl.ds(first, tall * LANES)]
+            filled = filled + count
+        more = jnp.maximum(more, filled)
+    more_ref[0] = more
+    for k in range(ROUNDS):
+        for d in range(LINE):
+            span = pl.ds(k * ROUND * LANES, ROUND * LANES)
+            sends.append(
+                pltpu.make_async_copy(
+                    late_scr.at[d, :, span], late_refs[k * LINE + d], late_sem.at[k, d]
+                )
+            )
+            sends[-1].start()
     for one in sends:
         one.wait()
+
+
+def late_rows(width_ref, tile, cols):
+    first_col = 0
+    for t in range(width_ref.shape[0]):
+        first_col = first_col + jnp.where(t < tile, width_ref[t], 0)
+    width = width_ref[tile]
+    rows = (first_col + width - 1) // cols - first_col // cols + 1 - PIECES[0]
+    return first_col, jnp.where(width > PIECES[0] * cols, rows, 0)
 
 
 def smooth_and_cut(place, level_scale, level_map, tile_widths, alpha, coef_x, coef_y, capacity):
@@ -161,7 +199,8 @@
     blocks = cols // LANES
     assert levels * blocks == SUBS and rows % SUBS == 0
     tile_rows = capacity // cols + 1
-    assert sum(PIECES) == tile_rows - 1
+    assert sum(PIECES) == tile_rows - 1 and PIECES[0] == PIECES[1]
+    assert tiles // LINE * (PIECES[0] + 1) <= ROUNDS * ROUND
     anywhere = pl.BlockSpec(memory_space=pl.ANY)
     scalars = pl.BlockSpec(memory_space=pltpu.SMEM)
     plane = pltpu.VMEM((blocks, rows, LANES), jnp.float32)
@@ -169,9 +208,13 @@
     square = pltpu.VMEM((cols, cols), jnp.bfloat16)
     return pl.pallas_call(
         diffuse_kernel,
-        out_shape=jax.ShapeDtypeStruct((tiles, SUBS, tile_rows * LANES), jnp.bfloat16),
+        out_shape=[
+            jax.ShapeDtypeStruct((tiles, SUBS, (PIECES[0] + 1) * LANES), jnp.bfloat16),
+            *[jax.ShapeDtypeStruct((SUBS, ROUND * LANES), jnp.bfloat16)] * (LINE * ROUNDS),
+            jax.ShapeDtypeStruct((1,), jnp.int32),
+        ],
         in_specs=[scalars] * 4 + [anywhere] * 3,
-        out_specs=anywhere,
+        out_specs=[anywhere] * (1 + LINE * ROUNDS) + [scalars],
         scratch_shapes=[
             pltpu.VMEM((levels, blocks, rows, LANES), jnp.float32),
             plane,
@@ -187,17 +230,80 @@
             pltpu.VMEM((rows, LANES), jnp.float32),
             pltpu.VMEM((rows * SUBS, LANES), jnp.float32),
             pltpu.VMEM((SUBS, (rows + tile_rows) * LANES), jnp.bfloat16),
+            pltpu.VMEM((LINE, SUBS, ROUNDS * ROUND * LANES), jnp.bfloat16),
             pltpu.SemaphoreType.DMA((blocks, 2 + levels)),
             pltpu.SemaphoreType.DMA((tiles,)),
+            pltpu.SemaphoreType.DMA((ROUNDS, LINE)),
         ],
         name="diffuse",
     )(place, level_scale, level_map, tile_widths, alpha, coef_x, coef_y)
 
 
+def regroup_kernel(cols, place_ref, width_ref, *refs):
+    come_refs = refs[: LINE * ROUNDS]
+    out_refs = refs[LINE * ROUNDS : -3]
+    held_scr, in_sem, out_sem = refs[-3:]
+    tall = PIECES[0] + 1
+    copies = []
+    for k in range(ROUNDS):
+        for d in range(LINE):
+            span = pl.ds(k * ROUND * LANES, ROUND * LANES)
+            copies.append(
+                pltpu.make_async_copy(
+                    come_refs[k * LINE + d], held_scr.at[d, :, span], in_sem.at[k, d]
+                )
+            )
+            copies[-1].start()
+    for copy in copies:
+        copy.wait()
+    plane = lax.rem(place_ref[0], LINE)
+    groups = len(out_refs)
+    starts = [0]
+    for k in range(groups - 1):
+        starts.append(starts[-1] + late_rows(width_ref, k * LINE + plane, cols)[1])
+    copies = []
+    for e in range(groups):
+        group = lax.rem(place_ref[0] // LINE + e, groups)
+        first = 0
+        for k in range(groups):
+            first = jnp.where(group == k, starts[k], first)
+        first = pl.multiple_of(first * LANES, LANES)
+        for d in range(LINE):
+            copies.append(
+                pltpu.make_async_copy(
+                    held_scr.at[d, :, pl.ds(first, tall * LANES)], out_refs[e].at[d], out_sem.at[e, d]
+                )
+            )
+            copies[-1].start()
+    for copy in copies:
+        copy.wait()
+
+
+def regroup(place, tile_widths, come, cols):
+    groups = tile_widths.shape[0] // LINE
+    scalars = pl.BlockSpec(memory_space=pltpu.SMEM)
+    anywhere = pl.BlockSpec(memory_space=pl.ANY)
+    one = jax.ShapeDtypeStruct((LINE, SUBS, (PIECES[0] + 1) * LANES), jnp.bfloat16)
+    return pl.pallas_call(
+        functools.partial(regroup_kernel, cols),
+        out_shape=[one] * groups,
+        in_specs=[scalars] * 2 + [anywhere] * len(come),
+        out_specs=[anywhere] * groups,
+        scratch_shapes=[
+            pltpu.VMEM((LINE, SUBS, ROUNDS * ROUND * LANES), jnp.bfloat16),
+            pltpu.SemaphoreType.DMA((ROUNDS, LINE)),
+            pltpu.SemaphoreType.DMA((groups, LINE)),
+        ],
+        compiler_params=pltpu.CompilerParams(vmem_limit_bytes=8 << 20),
+        name="regroup",
+    )(place, tile_widths, *come)
+
+
 def localize_kernel(
-    begin_row, place_ref, width_ref, x_ref, weight_ref, order_ref, pert_ref, own_ref, send_ref, s_scr,
-    here_scr, sem,
+    begin_row, sources, place_ref, width_ref, *refs
 ):
+    x_refs = refs[:sources]
+    weight_ref, order_ref, pert_ref, own_ref, send_ref, s_scr, here_scr, sem = refs[sources:]
     step = pl.program_id(0)
     tiles = width_ref.shape[0]
     levels = order_ref.shape[0]
@@ -217,10 +323,15 @@
 
     @pl.when(step == 0)
     def _():
-        rows_here = pl.ds(begin_row * LANES, here_scr.shape[1])
-        copy = pltpu.make_async_copy(x_ref.at[:, rows_here], here_scr, sem)
-        copy.start()
-        copy.wait()
+        depth = here_scr.shape[0] // sources
+        copies = [
+            pltpu.make_async_copy(x_ref, here_scr.at[pl.ds(k * depth, depth), :], sem.at[k])
+            for k, x_ref in enumerate(x_refs)
+        ]
+        for copy in copies:
+            copy.start()
+        for copy in copies:
+            copy.wait()
 
     spread = jnp.dot(
         weight_ref[...],
@@ -265,20 +376,20 @@
     half = jax.ShapeDtypeStruct((levels // 2, rows * cols), jnp.bfloat16)
     half_spec = pl.BlockSpec((levels // 2, chunk), lambda i: (0, i))
     return pl.pallas_call(
-        functools.partial(localize_kernel, begin_row),
+        functools.partial(localize_kernel, begin_row, len(arrived)),
         grid=(rows // ROWS_PER_BLOCK,),
         out_shape=(half, half),
-        in_specs=[scalars, scalars, pl.BlockSpec(memory_space=pl.ANY), vector, vector,
+        in_specs=[scalars] * 2 + [pl.BlockSpec(memory_space=pl.ANY)] * len(arrived) + [vector, vector,
                   pl.BlockSpec((1, levels, chunk), lambda i: (0, 0, i + skip))],
         out_specs=(half_spec, half_spec),
         scratch_shapes=[
             pltpu.VMEM((levels, chunk + 2 * cols), jnp.float32),
-            pltpu.VMEM((arrived.shape[0], (rows + 1) * LANES), jnp.bfloat16),
-            pltpu.SemaphoreType.DMA,
+            pltpu.VMEM((weight.shape[1], (rows + 1) * LANES), jnp.bfloat16),
+            pltpu.SemaphoreType.DMA((len(arrived),)),
         ],
         compiler_params=pltpu.CompilerParams(vmem_limit_bytes=16 << 20),
         name="localize",
-    )(place, tile_widths, arrived, weight, order, perturbations)
+    )(place, tile_widths, *arrived, weight, order, perturbations)
 
 
 def body(
@@ -291,11 +402,36 @@
     mem = lax.axis_index("mem")
     place = lax.axis_index("lev").astype(jnp.int32).reshape(1)
 
-    outgoing = smooth_and_cut(
+    groups = tiles // LINE
+    outgoing, *late, more = smooth_and_cut(
         place, level_scale, level_map, tile_widths, alpha_weights, coef_x, coef_y, capacity
     )
+
+    def shifted(dy, dz):
+        return [
+            (y * LINE + z, (y + dy) % groups * LINE + (z + dz) % LINE)
+            for y in range(groups)
+            for z in range(LINE)
+        ]
+
+    def along_line(planes):
+        came = [planes[0]]
+        for d in range(1, LINE):
+            came.append(lax.ppermute(planes[d], "lev", shifted(0, d)))
+        return tuple(came)
+
+    come = along_line(late[:LINE])
     arrived = lax.all_to_all(outgoing, "lev", split_axis=0, concat_axis=0, tiled=True)
     arrived = arrived.reshape(tiles * SUBS, -1)
+    for k in range(1, ROUNDS):
+        rest = tuple(late[k * LINE : (k + 1) * LINE])
+        come += lax.cond(more[0] > k * ROUND, along_line, lambda planes: planes, rest)
+    grouped = regroup(place, tile_widths, come, cols)
+    joined = [grouped[0]]
+    for d in range(1, groups):
+        joined.append(lax.ppermute(grouped[d], "lev", shifted(d, 0)))
+    joined = [one.reshape(LINE * SUBS, -1) for one in joined]
+    inputs = ([arrived], joined)
 
     slot = jnp.arange(levels)
     core = (mem + slot // 16) % CORES
@@ -304,19 +440,29 @@
     row_level = half * 16 + ring * 4 + core * 2 + slot % 2
     order = (row_level[:, None] == slot[None, :]).astype(jnp.bfloat16)
     row_band = jnp.sum(jnp.where(row_level[:, None] == slot[None, :], band_widths[None, :], 0), 1)
-    col_band = jnp.sum(jnp.where(level_map[:, None] == slot[None, :], band_widths[None, :], 0), 1)
-    distance = jnp.abs(row_level[:, None] - level_map[None, :]).astype(jnp.float32)
-    mutual = jnp.minimum(row_band[:, None], col_band[None, :]).astype(jnp.float32)
-    local = jnp.where(distance <= mutual, jnp.exp(-distance * distance / (mutual * mutual)), 0.0)
-    same_block = (jnp.arange(blocks)[:, None] == jnp.arange(blocks)[None, :])[:, None, None, :, None]
-    weight = jnp.where(same_block, local.reshape(1, levels, tiles, 1, lev_dev), 0.0)
-    weight = weight.astype(jnp.bfloat16).reshape(blocks * levels, tiles * SUBS)
+    at = jnp.arange(tiles)
+    near = (place[0] // LINE - at // LINE) % groups * LINE + (place[0] - at) % LINE
+    near = (near[:, None] * lev_dev + jnp.arange(lev_dev)[None, :]).reshape(-1)
+    near_map = jnp.sum(jnp.where(near[:, None] == slot[None, :], level_map[None, :], 0), 1)
+
+    def weight_of(col_level):
+        col_band = jnp.sum(
+            jnp.where(col_level[:, None] == slot[None, :], band_widths[None, :], 0), 1
+        )
+        distance = jnp.abs(row_level[:, None] - col_level[None, :]).astype(jnp.float32)
+        mutual = jnp.minimum(row_band[:, None], col_band[None, :]).astype(jnp.float32)
+        local = jnp.where(distance <= mutual, jnp.exp(-distance * distance / (mutual * mutual)), 0.0)
+        same = (jnp.arange(blocks)[:, None] == jnp.arange(blocks)[None, :])[:, None, None, :, None]
+        weight = jnp.where(same, local.reshape(1, levels, tiles, 1, lev_dev), 0.0)
+        return weight.astype(jnp.bfloat16).reshape(blocks * levels, tiles * SUBS)
+
+    weights = (weight_of(level_map), weight_of(near_map))
 
     results = []
     begin = 0
-    for rows_here in PIECES:
+    for p, rows_here in enumerate(PIECES):
         own, other = localize(
-            begin, rows_here, place, tile_widths, arrived, weight, order, perturbations
+            begin, rows_here, place, tile_widths, inputs[p], weights[p], order, perturbations
         )
         results.append(sum_members(own, other))
         begin += rows_here

time: 93.7 us -> 113 us (1.21); the launches traced: 92.3 us -> 113 us
  starting transfers between devices: 26.9 us -> 37.6 us
  Pallas kernels: 19.2 us -> 24.6 us
  other arithmetic: 2.01 us -> 5.8 us
  local copies, waits for them, and re-layouts: 0.66 us -> 2.95 us
  waiting for transfers between devices: 43.4 us -> 41.2 us
    all_to_all x1, waiting for transfers between devices: 38.3 us -> 21.1 us  [body(): lax.all_to_all(outgoing, 'lev', split_axis=0, concat_axis=0, tiled=True)]
    ppermute x0 -> x6, waiting for transfers between devices: none -> 13.5 us  [the longest x3 7.72 us: body(): joined.append(lax.ppermute(grouped[d], 'lev', shifted(d, 0)))]
    ppermute x0 -> x6, starting transfers between devices: none -> 11.4 us  [the longest x3 6.33 us: along_line(): came.append(lax.ppermute(planes[d], 'lev', shifted(0, d)))]
    pallas_call x3 -> x4, Pallas kernels: 19.2 us -> 24.6 us  [the longest x1 15.5 us: smooth_and_cut(): pl.pallas_call(diffuse_kernel, out_shape=[jax.ShapeDtypeStruct((tiles, SU...]
    all_to_all x1, starting transfers between devices: 9.32 us -> 6.47 us  [body(): lax.all_to_all(outgoing, 'lev', split_axis=0, concat_axis=0, tiled=True)]
    convert_element_type x4, other arithmetic: 0.41 us -> 2.24 us  [narrow(): return x.astype(jnp.bfloat16)]
    unnamed x8 -> x14, local copies, waits for them, and re-layouts: 0.03 us -> 1.83 us
    ppermute x2, starting transfers between devices: 1.6 us -> 3.19 us  [sum_members(): came = lax.ppermute(other, 'mem', moved(0, 0, 1))]
  transfers between devices with their start and end apart: 11 -> 17, of which waited for: 3 -> 6; matrix products, arithmetic and copies ran while one was open for 2% -> 5% of each run, Pallas kernels for 2% -> 0%
where the time goes in v5:
time: 113 us
  waiting for transfers between devices  41.2 us (36%)
  starting transfers between devices  37.6 us (33%)
  Pallas kernels  24.6 us (22%)
  other arithmetic  5.8 us (5%)
  local copies, waits for them, and re-layouts  2.95 us (3%)
    all_to_all x1, waiting for transfers between devices, body(): lax.all_to_all(outgoing, 'lev', split_axis=0, concat_axis=0, tiled=True)  21.1 us
    pallas_call x1, Pallas kernels, smooth_and_cut(): pl.pallas_call(diffuse_kernel, out_shape=[jax.ShapeDtypeStruct((tiles, SU...  15.5 us
    ppermute x3, waiting for transfers between devices, body(): joined.append(lax.ppermute(grouped[d], 'lev', shifted(d, 0)))  7.72 us
    ppermute x2, waiting for transfers between devices, sum_members(): far = lax.ppermute(narrow(total[keep:]), 'mem', moved(1, 0, 0))  6.59 us
    all_to_all x1, starting transfers between devices, body(): lax.all_to_all(outgoing, 'lev', split_axis=0, concat_axis=0, tiled=True)  6.47 us
    ppermute x3, starting transfers between devices, along_line(): came.append(lax.ppermute(planes[d], 'lev', shifted(0, d)))  6.33 us
    ppermute x2, starting transfers between devices, sum_members(): far = lax.ppermute(narrow(total[keep:]), 'mem', moved(1, 0, 0))  6.2 us
    ppermute x3, waiting for transfers between devices, along_line(): came.append(lax.ppermute(planes[d], 'lev', shifted(0, d)))  5.77 us
  transfers between devices with their start and end apart: 17, of which 6 were waited for; matrix products, arithmetic and copies ran while one was open for 5% of the time, Pallas kernels for 0%

profile of v5, /device:TPU:1, one launch (start us, length us, event | category | flops | bytes accessed | tf_op | source)
XLA Modules:
  0.0 113.2 jit_solution(9707083488768473372)
XLA Ops:
  0.0 15.5 %diffuse.1 = (bf16[16,8,3200]{2,1,0:T(8,128)(2,1)}, bf16[8,8192]{1,0:T(8,128)(2,1)}, bf16[8,8192]{1,0:T(8,128)(2,1)}, bf16[8,8192]{1,0:T(8,128)(2,1)}, bf16[8,81...) custom-call(s32[1]{0:T(128)} %bitcast.place_ref, ...), custom_call_target="tpu_custom_call" | custom-call | tf_op jit(solution)/shard_map/diffuse/pallas_call | solution.py:209
  15.6 2.5 %collective-permute-start.8 = (bf16[8,8192]{1,0:T(8,128)(2,1)}, bf16[8,8192]{1,0:T(8,128)(2,1)S(1)}, u32[]{:S(2)}, u32[]{:S(2)}) collective-permute-start(bf16[8,8192]{1,0:T(8,128)(2,1)} %get-tuple-element.45), channel_id=1, source_target_pairs={{0,1},{1,2},{2,3},{3,0},{4,5},{5,6},{6,7},{7,4},{8,9},{9,10},{10,1... | collective-permute-start | bytes 393224 | tf_op jit(solution)/shard_map/ppermute | solution.py:420
  18.1 3.0 %collective-permute-start.9 = (bf16[8,8192]{1,0:T(8,128)(2,1)}, bf16[8,8192]{1,0:T(8,128)(2,1)S(1)}, u32[]{:S(2)}, u32[]{:S(2)}) collective-permute-start(bf16[8,8192]{1,0:T(8,128)(2,1)} %get-tuple-element.46), channel_id=1, source_target_pairs={{0,2},{1,3},{2,0},{3,1},{4,6},{5,7},{6,4},{7,5},{8,10},{9,11},{10,... | collective-permute-start | bytes 393224 | tf_op jit(solution)/shard_map/ppermute | solution.py:420
  21.8 0.8 collective-permute-start.10
  22.6 0.1 sub.103
  22.7 0.1 iota_add_fusion
  22.8 0.1 add.221
  22.9 0.2 select_reduce_fusion.1
  23.1 0.1 sub.114
  23.2 0.2 select_reduce_fusion.2
  23.4 0.1 min.37
  23.5 0.1 min.40
  23.6 0.2 compare_select_fusion.1
  23.8 0.8 select_convert_fusion.1
  24.6 0.1 convert_element_type.147
  24.7 0.1 copy.10.refs_4_
  24.8 5.8 %collective-permute-done.9.refs_2_ = bf16[8,8192]{1,0:T(8,128)(2,1)S(1)} collective-permute-done((bf16[8,8192]{1,0:T(8,128)(2,1)}, bf16[8,8192]{1,0:T(8,128)(2,1)S(1)}, u32[]{:S(2)}, u32[]{:S(2)}) %collective-permute-start.9) | collective-permute-done | bytes 131104 | tf_op jit(solution)/shard_map/ppermute | solution.py:420
  30.6 0.9 copy-done.1
  31.5 0.9 copy-done.2
  32.4 3.6 %regroup.1 = (bf16[4,8,3200]{2,1,0:T(8,128)(2,1)S(1)}, bf16[4,8,3200]{2,1,0:T(8,128)(2,1)S(1)}, bf16[4,8,3200]{2,1,0:T(8,128)(2,1)S(1)}, bf16[4,8,3200]{2,1,0:T(8,128)(2,1)S(1)}) custom-call(s32[1]{0:T(128)} %bitcast.place_ref, s32[16]{0:T(128)S(1)} %copy-done.3, bf16[8,8192]{1,0:T(8,128)(2,1)S(1)} %copy-done.1, ...), custom_call_target="tpu_custom_call" | custom-call | tf_op jit(solution)/shard_map/regroup/pallas_call | solution.py:287
  36.0 1.4 %collective-permute-start.11 = (bf16[4,8,3200]{2,1,0:T(8,128)(2,1)S(1)}, bf16[4,8,3200]{2,1,0:T(8,128)(2,1)S(1)}, u32[]{:S(2)}, u32[]{:S(2)}) collective-permute-start(bf16[4,8,3200]{2,1,0:T(8,128)(2,1)S(1)} %get-tuple-element.57), channel_id=1, source_target_pairs={{0,4},{1,5},{2,6},{3,7},{4,8},{5,9},{6,10},{7,11},{8,12},{9,13},{1... | collective-permute-start | bytes 614408 | tf_op jit(solution)/shard_map/ppermute | solution.py:432
  37.4 2.6 %collective-permute-start.12 = (bf16[4,8,3200]{2,1,0:T(8,128)(2,1)S(1)}, bf16[4,8,3200]{2,1,0:T(8,128)(2,1)S(1)}, u32[]{:S(2)}, u32[]{:S(2)}) collective-permute-start(bf16[4,8,3200]{2,1,0:T(8,128)(2,1)S(1)} %get-tuple-element.58), channel_id=1, source_target_pairs={{0,8},{1,9},{2,10},{3,11},{4,12},{5,13},{6,14},{7,15},{8,0},{9,1},... | collective-permute-start | bytes 614408 | tf_op jit(solution)/shard_map/ppermute | solution.py:432
  40.0 1.1 collective-permute-start.13
  41.1 0.1 fusion.2.refs_2_.refs_5_
  41.2 1.8 %collective-permute-done.11 = bf16[4,8,3200]{2,1,0:T(8,128)(2,1)S(1)} collective-permute-done((bf16[4,8,3200]{2,1,0:T(8,128)(2,1)S(1)}, bf16[4,8,3200]{2,1,0:T(8,128)(2,1)S(1)}, u32[]{:S(2)}, u32[]{:S(2)}) %collective-permute-start.11) | collective-permute-done | bytes 204832 | tf_op jit(solution)/shard_map/ppermute | solution.py:432
  42.9 5.9 %collective-permute-done.12 = bf16[4,8,3200]{2,1,0:T(8,128)(2,1)S(1)} collective-permute-done((bf16[4,8,3200]{2,1,0:T(8,128)(2,1)S(1)}, bf16[4,8,3200]{2,1,0:T(8,128)(2,1)S(1)}, u32[]{:S(2)}, u32[]{:S(2)}) %collective-permute-start.12) | collective-permute-done | bytes 204832 | tf_op jit(solution)/shard_map/ppermute | solution.py:432
  48.9 3.3 %localize.3 = (bf16[16,12288]{1,0:T(8,128)(2,1)S(1)}, bf16[16,12288]{1,0:T(8,128)(2,1)S(1)}) custom-call(s32[1]{0:T(128)} %bitcast.place_ref, s32[16]{0:T(128)S(1)} %copy-done.3, bf16[32,3200]{1,0:T(8,128)(2,1)S(1)} %bitcast.12, bf16[32,3200]{1,0:T(8,128)(2,1)S(1)} %bitcast.13, bf16[32,3200]{1,0:T(8,128)(2,1)S(1)} %bitcast.14, ...), custom_call_target="tpu_custom_call" | custom-call | tf_op jit(solution)/shard_map/localize/pallas_call | solution.py:378
  52.2 1.6 %collective-permute-start.14 = (bf16[16,12288]{1,0:T(8,128)(2,1)S(1)}, bf16[16,12288]{1,0:T(8,128)(2,1)}, u32[]{:S(2)}, u32[]{:S(2)}) collective-permute-start(bf16[16,12288]{1,0:T(8,128)(2,1)S(1)} %get-tuple-element.61), channel_id=1, source_target_pairs={{0,16},{16,0},{32,48},{48,32},{64,80},{80,64},{96,112},{112,96},{1... | collective-permute-start | bytes 1179656 | tf_op jit(solution)/shard_map/ppermute | solution.py:490
  53.8 6.5 %all-to-all-start = ((bf16[16,8,3200]{2,1,0:T(8,128)(2,1)}), bf16[16,8,3200]{2,1,0:T(8,128)(2,1)S(1)}, u32[]{:S(2)}, u32[]{:S(2)}) async-start(bf16[16,8,3200]{2,1,0:T(8,128)(2,1)} %get-tuple-element.41), calls=%async_computation | async-start | bytes 1638400 | tf_op jit(solution)/shard_map/all_to_all | solution.py:424
  60.3 0.1 convert_element_type.128
  60.4 0.1 copy.9.refs_1_
  60.6 1.0 add_convert_fusion
  61.6 21.1 %all-to-all-done = bf16[16,8,3200]{2,1,0:T(8,128)(2,1)S(1)} async-done(((bf16[16,8,3200]{2,1,0:T(8,128)(2,1)}), bf16[16,8,3200]{2,1,0:T(8,128)(2,1)S(1)}, u32[]{:S(2)}, u32[]{:S(2)}) %all-to-all-start) | async-done | bytes 819232 | tf_op jit(solution)/shard_map/all_to_all | solution.py:424
  82.7 2.3 %localize.2 = (bf16[16,12288]{1,0:T(8,128)(2,1)S(1)}, bf16[16,12288]{1,0:T(8,128)(2,1)S(1)}) custom-call(s32[1]{0:T(128)} %bitcast.place_ref, s32[16]{0:T(128)S(1)} %copy-done.3, bf16[128,3200]{1,0:T(8,128)(2,1)S(1)} %bitcast.11, bf16[128,128]{1,0:T(8,128)(2,1)S(1)} %copy.9.refs_1_, bf16[32,32]{1,0:T(8,128)(2,1)S(1)} %fusion.2.refs_2_.refs_5_, ...), custom_call_target="tpu_custom_call" | custom-call | tf_op jit(solution)/shard_map/localize/pallas_call | solution.py:378
  84.9 1.5 %collective-permute-start.3 = (bf16[16,12288]{1,0:T(8,128)(2,1)S(1)}, bf16[16,12288]{1,0:T(8,128)(2,1)S(1)}, u32[]{:S(2)}, u32[]{:S(2)}) collective-permute-start(bf16[16,12288]{1,0:T(8,128)(2,1)S(1)} %get-tuple-element.43), channel_id=1, source_target_pairs={{0,16},{16,0},{32,48},{48,32},{64,80},{80,64},{96,112},{112,96},{1... | collective-permute-start | bytes 1179656 | tf_op jit(solution)/shard_map/ppermute | solution.py:490
  86.5 2.6 %collective-permute-start.16 = (bf16[4,12288]{1,0:T(4,128)(2,1)S(1)}, bf16[4,12288]{1,0:T(4,128)(2,1)S(1)}, u32[]{:S(2)}, u32[]{:S(2)}) collective-permute-start(bf16[4,12288]{1,0:T(4,128)(2,1)S(1)} %get-tuple-element.68), channel_id=1, source_target_pairs={{0,32},{16,112},{32,64},{48,16},{64,96},{80,48},{96,0},{112,80},{1... | collective-permute-start | bytes 294920 | tf_op jit(solution)/shard_map/ppermute | solution.py:494
  89.2 2.8 %collective-permute-start.5 = (bf16[4,12288]{1,0:T(4,128)(2,1)S(1)}, bf16[4,12288]{1,0:T(4,128)(2,1)S(1)}, u32[]{:S(2)}, u32[]{:S(2)}) collective-permute-start(bf16[4,12288]{1,0:T(4,128)(2,1)S(1)} %get-tuple-element.66), channel_id=1, source_target_pairs={{0,32},{16,112},{32,64},{48,16},{64,96},{80,48},{96,0},{112,80},{1... | collective-permute-start | bytes 294920 | tf_op jit(solution)/shard_map/ppermute | solution.py:494
  92.0 1.1 add_convert_fusion.2
  93.1 2.3 %collective-permute-start.17 = (bf16[4,12288]{1,0:T(4,128)(2,1)S(1)}, bf16[4,12288]{1,0:T(4,128)(2,1)S(1)}, u32[]{:S(2)}, u32[]{:S(2)}) collective-permute-start(bf16[4,12288]{1,0:T(4,128)(2,1)S(1)} %add_convert_fusion.2), channel_id=1, source_target_pairs={{0,32},{16,112},{32,64},{48,16},{64,96},{80,48},{96,0},{112,80},{1... | collective-permute-start | bytes 294920 | tf_op jit(solution)/shard_map/ppermute | solution.py:496
  95.3 0.1 add_convert_fusion.3
  95.5 2.8 %collective-permute-start.6 = (bf16[4,12288]{1,0:T(4,128)(2,1)S(1)}, bf16[4,12288]{1,0:T(4,128)(2,1)S(1)}, u32[]{:S(2)}, u32[]{:S(2)}) collective-permute-start(bf16[4,12288]{1,0:T(4,128)(2,1)S(1)} %add_convert_fusion.3), channel_id=1, source_target_pairs={{0,32},{16,112},{32,64},{48,16},{64,96},{80,48},{96,0},{112,80},{1... | collective-permute-start | bytes 294920 | tf_op jit(solution)/shard_map/ppermute | solution.py:496
  98.2 1.0 convert_add_fusion
  99.3 5.5 %collective-permute-start.18 = (bf16[2,12288]{1,0:T(2,128)(2,1)S(1)}, bf16[2,12288]{1,0:T(2,128)(2,1)S(1)}, u32[]{:S(2)}, u32[]{:S(2)}) collective-permute-start(bf16[2,12288]{1,0:T(2,128)(2,1)S(1)} %slice.112), channel_id=1, source_target_pairs={{0,128},{16,144},{32,160},{48,176},{64,192},{80,208},{96,224},{112... | collective-permute-start | bytes 147464 | tf_op jit(solution)/shard_map/ppermute | solution.py:499
  104.8 0.1 convert_add_fusion.1
  105.0 0.7 collective-permute-start.7
  105.7 0.6 collective-permute-done.18
  106.4 6.0 %collective-permute-done.7 = bf16[2,12288]{1,0:T(2,128)(2,1)S(1)} collective-permute-done((bf16[2,12288]{1,0:T(2,128)(2,1)S(1)}, bf16[2,12288]{1,0:T(2,128)(2,1)S(1)}, u32[]{:S(2)}, u32[]{:S(2)}) %collective-permute-start.7) | collective-permute-done | bytes 49184 | tf_op jit(solution)/shard_map/ppermute | solution.py:499
  112.4 0.8 pad_maximum_fusion
  (36 shorter events, 0.5 us)
Async XLA Ops:
  0.0 22.6 %copy-start.5 = (s32[32]{0:T(128)S(1)}, s32[32]{0:T(128)}, u32[]{:S(2)}) copy-start(s32[32]{0:T(128)} %map_ref.1) | copy-start | bytes 388
  0.0 23.2 %copy-start.6 = (s32[32]{0:T(128)S(1)}, s32[32]{0:T(128)}, u32[]{:S(2)}) copy-start(s32[32]{0:T(128)} %param.17) | copy-start | bytes 388
  0.0 30.6 %copy-start.3 = (s32[16]{0:T(128)S(1)}, s32[16]{0:T(128)}, u32[]{:S(2)}) copy-start(s32[16]{0:T(128)} %width_ref.7) | copy-start | bytes 196
  15.5 33.3 %copy-start = (bf16[1,32,24576]{2,1,0:T(8,128)(2,1)S(1)}, bf16[1,32,24576]{2,1,0:T(8,128)(2,1)}, u32[]{:S(2)}) copy-start(bf16[1,32,24576]{2,1,0:T(8,128)(2,1)} %refs_6_.1) | copy-start | bytes 4718596
  15.6 9.3 %collective-permute-start.8 = (bf16[8,8192]{1,0:T(8,128)(2,1)}, bf16[8,8192]{1,0:T(8,128)(2,1)S(1)}, u32[]{:S(2)}, u32[]{:S(2)}) collective-permute-start(bf16[8,8192]{1,0:T(8,128)(2,1)} %get-tuple-element.45), channel_id=1, source_target_pairs={{0,1},{1,2},{2,3},{3,0},{4,5},{5,6},{6,7},{7,4},{8,9},{9,10},{10,1... | collective-permute-start | bytes 393224 | tf_op jit(solution)/shard_map/ppermute | solution.py:420
  18.1 12.5 %collective-permute-start.9 = (bf16[8,8192]{1,0:T(8,128)(2,1)}, bf16[8,8192]{1,0:T(8,128)(2,1)S(1)}, u32[]{:S(2)}, u32[]{:S(2)}) collective-permute-start(bf16[8,8192]{1,0:T(8,128)(2,1)} %get-tuple-element.46), channel_id=1, source_target_pairs={{0,2},{1,3},{2,0},{3,1},{4,6},{5,7},{6,4},{7,5},{8,10},{9,11},{10,... | collective-permute-start | bytes 393224 | tf_op jit(solution)/shard_map/ppermute | solution.py:420
  21.8 8.8 %collective-permute-start.10 = (bf16[8,8192]{1,0:T(8,128)(2,1)}, bf16[8,8192]{1,0:T(8,128)(2,1)S(1)}, u32[]{:S(2)}, u32[]{:S(2)}) collective-permute-start(bf16[8,8192]{1,0:T(8,128)(2,1)} %get-tuple-element.47), channel_id=1, source_target_pairs={{0,3},{1,0},{2,1},{3,2},{4,7},{5,4},{6,5},{7,6},{8,11},{9,8},{10,9... | collective-permute-start | bytes 393224 | tf_op jit(solution)/shard_map/ppermute | solution.py:420
  30.6 0.9 copy-start.1
  31.5 0.9 copy-start.2
  36.0 6.9 %collective-permute-start.11 = (bf16[4,8,3200]{2,1,0:T(8,128)(2,1)S(1)}, bf16[4,8,3200]{2,1,0:T(8,128)(2,1)S(1)}, u32[]{:S(2)}, u32[]{:S(2)}) collective-permute-start(bf16[4,8,3200]{2,1,0:T(8,128)(2,1)S(1)} %get-tuple-element.57), channel_id=1, source_target_pairs={{0,4},{1,5},{2,6},{3,7},{4,8},{5,9},{6,10},{7,11},{8,12},{9,13},{1... | collective-permute-start | bytes 614408 | tf_op jit(solution)/shard_map/ppermute | solution.py:432
  37.4 11.5 %collective-permute-start.12 = (bf16[4,8,3200]{2,1,0:T(8,128)(2,1)S(1)}, bf16[4,8,3200]{2,1,0:T(8,128)(2,1)S(1)}, u32[]{:S(2)}, u32[]{:S(2)}) collective-permute-start(bf16[4,8,3200]{2,1,0:T(8,128)(2,1)S(1)} %get-tuple-element.58), channel_id=1, source_target_pairs={{0,8},{1,9},{2,10},{3,11},{4,12},{5,13},{6,14},{7,15},{8,0},{9,1},... | collective-permute-start | bytes 614408 | tf_op jit(solution)/shard_map/ppermute | solution.py:432
  40.0 8.9 %collective-permute-start.13 = (bf16[4,8,3200]{2,1,0:T(8,128)(2,1)S(1)}, bf16[4,8,3200]{2,1,0:T(8,128)(2,1)S(1)}, u32[]{:S(2)}, u32[]{:S(2)}) collective-permute-start(bf16[4,8,3200]{2,1,0:T(8,128)(2,1)S(1)} %get-tuple-element.59), channel_id=1, source_target_pairs={{0,12},{1,13},{2,14},{3,15},{4,0},{5,1},{6,2},{7,3},{8,4},{9,5},{1... | collective-permute-start | bytes 614408 | tf_op jit(solution)/shard_map/ppermute | solution.py:432
  52.2 8.1 %copy-start.4 = (bf16[4,32,16,4,2]{1,0,4,3,2:T(4,128)(2,1)S(1)}, bf16[4,32,16,4,2]{1,0,4,3,2:T(4,128)(2,1)}, u32[]{:S(2)}) copy-start(bf16[4,32,16,4,2]{1,0,4,3,2:T(4,128)(2,1)} %get-tuple-element.71) | copy-start | bytes 98308
  52.2 8.4 %collective-permute-start.14 = (bf16[16,12288]{1,0:T(8,128)(2,1)S(1)}, bf16[16,12288]{1,0:T(8,128)(2,1)}, u32[]{:S(2)}, u32[]{:S(2)}) collective-permute-start(bf16[16,12288]{1,0:T(8,128)(2,1)S(1)} %get-tuple-element.61), channel_id=1, source_target_pairs={{0,16},{16,0},{32,48},{48,32},{64,80},{80,64},{96,112},{112,96},{1... | collective-permute-start | bytes 1179656 | tf_op jit(solution)/shard_map/ppermute | solution.py:490
  53.8 28.8 %all-to-all-start = ((bf16[16,8,3200]{2,1,0:T(8,128)(2,1)}), bf16[16,8,3200]{2,1,0:T(8,128)(2,1)S(1)}, u32[]{:S(2)}, u32[]{:S(2)}) async-start(bf16[16,8,3200]{2,1,0:T(8,128)(2,1)} %get-tuple-element.41), calls=%async_computation | async-start | bytes 1638400 | tf_op jit(solution)/shard_map/all_to_all | solution.py:424
  84.9 4.2 %collective-permute-start.3 = (bf16[16,12288]{1,0:T(8,128)(2,1)S(1)}, bf16[16,12288]{1,0:T(8,128)(2,1)S(1)}, u32[]{:S(2)}, u32[]{:S(2)}) collective-permute-start(bf16[16,12288]{1,0:T(8,128)(2,1)S(1)} %get-tuple-element.43), channel_id=1, source_target_pairs={{0,16},{16,0},{32,48},{48,32},{64,80},{80,64},{96,112},{112,96},{1... | collective-permute-start | bytes 1179656 | tf_op jit(solution)/shard_map/ppermute | solution.py:490
  86.5 5.4 %collective-permute-start.16 = (bf16[4,12288]{1,0:T(4,128)(2,1)S(1)}, bf16[4,12288]{1,0:T(4,128)(2,1)S(1)}, u32[]{:S(2)}, u32[]{:S(2)}) collective-permute-start(bf16[4,12288]{1,0:T(4,128)(2,1)S(1)} %get-tuple-element.68), channel_id=1, source_target_pairs={{0,32},{16,112},{32,64},{48,16},{64,96},{80,48},{96,0},{112,80},{1... | collective-permute-start | bytes 294920 | tf_op jit(solution)/shard_map/ppermute | solution.py:494
  89.1 9.1 %collective-permute-start.15 = (bf16[4,12288]{1,0:T(4,128)(2,1)S(1)}, bf16[4,12288]{1,0:T(4,128)(2,1)S(1)}, u32[]{:S(2)}, u32[]{:S(2)}) collective-permute-start(bf16[4,12288]{1,0:T(4,128)(2,1)S(1)} %get-tuple-element.67), channel_id=1, source_target_pairs={{0,96},{16,48},{32,0},{48,80},{64,32},{80,112},{96,64},{112,16},{1... | collective-permute-start | bytes 294920 | tf_op jit(solution)/shard_map/ppermute | solution.py:495
  89.2 6.1 %collective-permute-start.5 = (bf16[4,12288]{1,0:T(4,128)(2,1)S(1)}, bf16[4,12288]{1,0:T(4,128)(2,1)S(1)}, u32[]{:S(2)}, u32[]{:S(2)}) collective-permute-start(bf16[4,12288]{1,0:T(4,128)(2,1)S(1)} %get-tuple-element.66), channel_id=1, source_target_pairs={{0,32},{16,112},{32,64},{48,16},{64,96},{80,48},{96,0},{112,80},{1... | collective-permute-start | bytes 294920 | tf_op jit(solution)/shard_map/ppermute | solution.py:494
  93.1 5.2 %collective-permute-start.17 = (bf16[4,12288]{1,0:T(4,128)(2,1)S(1)}, bf16[4,12288]{1,0:T(4,128)(2,1)S(1)}, u32[]{:S(2)}, u32[]{:S(2)}) collective-permute-start(bf16[4,12288]{1,0:T(4,128)(2,1)S(1)} %add_convert_fusion.2), channel_id=1, source_target_pairs={{0,32},{16,112},{32,64},{48,16},{64,96},{80,48},{96,0},{112,80},{1... | collective-permute-start | bytes 294920 | tf_op jit(solution)/shard_map/ppermute | solution.py:496
  95.3 9.5 %collective-permute-start.4 = (bf16[4,12288]{1,0:T(4,128)(2,1)S(1)}, bf16[4,12288]{1,0:T(4,128)(2,1)S(1)}, u32[]{:S(2)}, u32[]{:S(2)}) collective-permute-start(bf16[4,12288]{1,0:T(4,128)(2,1)S(1)} %get-tuple-element.65), channel_id=1, source_target_pairs={{0,96},{16,48},{32,0},{48,80},{64,32},{80,112},{96,64},{112,16},{1... | collective-permute-start | bytes 294920 | tf_op jit(solution)/shard_map/ppermute | solution.py:495
  95.5 9.4 %collective-permute-start.6 = (bf16[4,12288]{1,0:T(4,128)(2,1)S(1)}, bf16[4,12288]{1,0:T(4,128)(2,1)S(1)}, u32[]{:S(2)}, u32[]{:S(2)}) collective-permute-start(bf16[4,12288]{1,0:T(4,128)(2,1)S(1)} %add_convert_fusion.3), channel_id=1, source_target_pairs={{0,32},{16,112},{32,64},{48,16},{64,96},{80,48},{96,0},{112,80},{1... | collective-permute-start | bytes 294920 | tf_op jit(solution)/shard_map/ppermute | solution.py:496
  99.3 7.0 %collective-permute-start.18 = (bf16[2,12288]{1,0:T(2,128)(2,1)S(1)}, bf16[2,12288]{1,0:T(2,128)(2,1)S(1)}, u32[]{:S(2)}, u32[]{:S(2)}) collective-permute-start(bf16[2,12288]{1,0:T(2,128)(2,1)S(1)} %slice.112), channel_id=1, source_target_pairs={{0,128},{16,144},{32,160},{48,176},{64,192},{80,208},{96,224},{112... | collective-permute-start | bytes 147464 | tf_op jit(solution)/shard_map/ppermute | solution.py:499
  105.0 7.3 %collective-permute-start.7 = (bf16[2,12288]{1,0:T(2,128)(2,1)S(1)}, bf16[2,12288]{1,0:T(2,128)(2,1)S(1)}, u32[]{:S(2)}, u32[]{:S(2)}) collective-permute-start(bf16[2,12288]{1,0:T(2,128)(2,1)S(1)} %slice.113), channel_id=1, source_target_pairs={{0,128},{16,144},{32,160},{48,176},{64,192},{80,208},{96,224},{112... | collective-permute-start | bytes 147464 | tf_op jit(solution)/shard_map/ppermute | solution.py:499

commit v6 on v4

v6 whole, which is shorter than its diff:
```python
import functools

import jax
import jax.numpy as jnp
from jax import lax
from jax.experimental import pallas as pl
from jax.experimental.pallas import tpu as pltpu
from jax.sharding import PartitionSpec as P

STEPS = 16
LANES = 128
SUBS = 8
ROWS_PER_BLOCK = 8
CORES, RING, HALVES = 2, 4, 2
PIECES = (24, 24)
LINE = 4


def split_bf16(x):
    high = x.astype(jnp.bfloat16)
    return high, (x - high.astype(jnp.float32)).astype(jnp.bfloat16)


def diffuse_kernel(
    level, place_ref, scale_ref, map_ref, width_ref, alpha_ref, cx_ref, cy_ref, *refs
):
    out_refs = refs[:-15]
    (
        raw_scr, cx_scr, cy_scr, spread_scr, gather_scr, x_scr, f_scr, ax_scr, ay_scr, ayr_scr,
        o_scr, msg_scr, starts, sems, out_sem,
    ) = refs[-15:]
    rows, cols = cx_ref.shape
    levels = alpha_ref.shape[1]
    fold = rows // SUBS
    blocks = cols // LANES
    pack = SUBS // blocks
    tiles = width_ref.shape[0]

    def part(b):
        return pl.ds(b * LANES, LANES)

    def at(r):
        return pl.ds(r * SUBS, SUBS)

    sources = (cx_ref, cy_ref, alpha_ref.at[0, level])
    planes = (cx_scr, cy_scr, raw_scr)
    copies = [
        [
            pltpu.make_async_copy(source.at[:, part(b)], plane.at[b], sems.at[k, b])
            for b in range(blocks)
        ]
        for k, (source, plane) in enumerate(zip(sources, planes))
    ]
    for one in copies:
        for copy in one:
            copy.start()

    for b in range(blocks):
        natural = lax.broadcasted_iota(jnp.int32, (cols, LANES), 0)
        spaced = lax.broadcasted_iota(jnp.int32, (cols, LANES), 1)
        match = jnp.where(natural == spaced * blocks + b, 1.0, 0.0)
        spread_scr[:, part(b)] = match.astype(jnp.bfloat16)
        match = jnp.where(natural % LANES * blocks + natural // LANES == spaced + b * LANES, 1.0, 0.0)
        gather_scr[:, part(b)] = match.astype(jnp.bfloat16)

    def spread_columns(k):
        for copy in copies[k]:
            copy.wait()
        for r in range(fold):
            for b in range(blocks):
                x_scr[at(r), part(b)] = planes[k][b, pl.ds(r, SUBS, stride=fold), :]
        high, low = split_bf16(x_scr[...])
        return jnp.dot(high, spread_scr[...], preferred_element_type=jnp.float32) + jnp.dot(
            low, spread_scr[...], preferred_element_type=jnp.float32
        )

    lane = lax.broadcasted_iota(jnp.int32, (SUBS, LANES), 1)
    sub = lax.broadcasted_iota(jnp.int32, (SUBS, LANES), 0)
    gain = scale_ref[map_ref[place_ref[0] * levels + level]]
    ax_scr[...] = spread_columns(0) * gain
    ay_scr[...] = spread_columns(1) * gain
    for b in range(blocks):
        ax_scr[at(fold - 1), part(b)] = jnp.where(
            sub == SUBS - 1, 0.0, ax_scr[at(fold - 1), part(b)]
        )
    for r in range(fold):
        ay = jnp.where(lane == LANES - 1, 0.0, ay_scr[at(r), part(blocks - 1)])
        ay_scr[at(r), part(blocks - 1)] = ay
        ayr_scr[at(r), :] = pltpu.roll(ay, 1, 1)
    f_scr[pl.ds(0, rows), :] = spread_columns(2)

    @pl.loop(0, STEPS)
    def _(step):
        wrap = [pltpu.roll(f_scr[at(0), part(b)], SUBS - 1, 0) for b in range(blocks)]
        for b in range(blocks):
            f_scr[at(fold), part(b)] = wrap[b]
        here = [f_scr[at(fold - 1), part(b)] for b in range(blocks)]
        before = [
            pltpu.roll(ax_scr[at(fold - 1), part(b)] * (wrap[b] - here[b]), 1, 0)
            for b in range(blocks)
        ]
        here = [f_scr[at(0), part(b)] for b in range(blocks)]
        for r in range(fold):
            after = [f_scr[at(r + 1), part(b)] for b in range(blocks)]
            right = pltpu.roll(here[0], LANES - 1, 1)
            left = pltpu.roll(here[blocks - 1], 1, 1)
            last_y = ayr_scr[at(r), :] * (here[0] - left)
            flux = []
            for b in range(blocks):
                fx = ax_scr[at(r), part(b)] * (after[b] - here[b])
                beside = here[b + 1] if b < blocks - 1 else right
                fy = ay_scr[at(r), part(b)] * (beside - here[b])
                f_scr[at(r), part(b)] = here[b] + (fx - before[b]) + (fy - last_y)
                last_y = fy
                flux.append(fx)
            here, before = after, flux

    natural = jnp.dot(
        f_scr[pl.ds(0, rows), :].astype(jnp.bfloat16),
        gather_scr[...],
        preferred_element_type=jnp.float32,
    )
    for r in range(fold):
        for b in range(blocks):
            o_scr[at(r * blocks + b), :] = natural[
                r * SUBS : (r + 1) * SUBS, b * LANES : (b + 1) * LANES
            ]
    for r in range(fold // pack):
        for i in range(SUBS):
            row = o_scr[pl.ds(r * SUBS * SUBS + i, SUBS, stride=SUBS), :]
            msg_scr[:, part(i * (fold // pack) + r)] = row.astype(jnp.bfloat16)
    used = rows // pack * LANES
    msg_scr[:, pl.ds(used, msg_scr.shape[1] - used)] = jnp.zeros(
        (SUBS, msg_scr.shape[1] - used), jnp.bfloat16
    )
    first_col = 0
    for t in range(tiles):
        starts[t] = first_col
        first_col = first_col + width_ref[t]
    sends = []
    groups = tiles // LINE
    for k in range(tiles):
        d, e = k // groups, k % groups
        if len(out_refs) > 1:
            tile = lax.rem(place_ref[0] // LINE + e, groups) * LINE + lax.rem(place_ref[0] + d, LINE)
            target = out_refs[d].at[e]
        else:
            tile, target = k, out_refs[0].at[k]
        first = pl.multiple_of(starts[tile] // (cols * pack) * LANES, LANES)
        sends.append(
            pltpu.make_async_copy(
                msg_scr.at[:, pl.ds(first, out_refs[0].shape[2])], target, out_sem.at[k]
            )
        )
        sends[-1].start()
    for one in sends:
        one.wait()


def smooth_and_cut(level, place, level_scale, level_map, tile_widths, alpha, coef_x, coef_y, tall):
    rows, cols = alpha.shape[2:]
    tiles = tile_widths.shape[0]
    blocks = cols // LANES
    pack = SUBS // blocks
    assert SUBS % blocks == 0 and rows % (SUBS * pack) == 0
    anywhere = pl.BlockSpec(memory_space=pl.ANY)
    scalars = pl.BlockSpec(memory_space=pltpu.SMEM)
    plane = pltpu.VMEM((blocks, rows, LANES), jnp.float32)
    whole = pltpu.VMEM((rows, cols), jnp.float32)
    square = pltpu.VMEM((cols, cols), jnp.bfloat16)
    split = LINE if level == 0 else 1
    return pl.pallas_call(
        functools.partial(diffuse_kernel, level),
        out_shape=[
            jax.ShapeDtypeStruct((tiles // split, SUBS, (tall // pack + 1) * LANES), jnp.bfloat16)
        ]
        * split,
        in_specs=[scalars] * 4 + [anywhere] * 3,
        out_specs=[anywhere] * split,
        scratch_shapes=[
            plane,
            plane,
            plane,
            square,
            square,
            whole,
            pltpu.VMEM((rows + SUBS, cols), jnp.float32),
            whole,
            whole,
            pltpu.VMEM((rows, LANES), jnp.float32),
            pltpu.VMEM((rows * blocks, LANES), jnp.float32),
            pltpu.VMEM((SUBS, ((rows + tall) // pack + 1) * LANES), jnp.bfloat16),
            pltpu.SMEM((tiles,), jnp.int32),
            pltpu.SemaphoreType.DMA((3, blocks)),
            pltpu.SemaphoreType.DMA((tiles,)),
        ],
        name="diffuse",
    )(place, level_scale, level_map, tile_widths, alpha, coef_x, coef_y)


def localize_kernel(
    begin_row, cols, parts, place_ref, width_ref, *refs
):
    x_refs = refs[: sum(parts)]
    weight_ref, order_ref, pert_ref, own_ref, send_ref, s_scr, here_scr, sem = refs[sum(parts) :]
    step = pl.program_id(0)
    tiles = width_ref.shape[0]
    levels = order_ref.shape[0]
    blocks = cols // LANES
    group = weight_ref.shape[1] // levels
    pack = group // blocks
    chunk = pert_ref.shape[2]
    count = chunk // (cols * pack)
    me = place_ref[0]
    first_col = 0
    for t in range(tiles):
        first_col = first_col + jnp.where(t < me, width_ref[t], 0)
    shift = first_col % (cols * pack)
    shift_blocks = shift // LANES
    shift_lanes = shift % LANES
    width = width_ref[me] - begin_row * cols - step * chunk

    @pl.when(step == 0)
    def _():
        lanes = pl.ds(begin_row // pack * LANES, here_scr.shape[2])
        copies = []
        for v, n in enumerate(parts):
            depth = here_scr.shape[1] // n
            for k in range(n):
                m = len(copies)
                target = here_scr.at[v, pl.ds(k * depth, depth), :]
                copies.append(pltpu.make_async_copy(x_refs[m].at[:, lanes], target, sem.at[m]))
                copies[-1].start()
        for copy in copies:
            copy.wait()

    spread = 0.0
    first = pl.multiple_of(step * (count * LANES), LANES)
    for v in range(len(parts)):
        spread = spread + jnp.dot(
            weight_ref[v],
            here_scr[v, :, pl.ds(first, (count + 1) * LANES)],
            preferred_element_type=jnp.float32,
        )
    for r in range(count + 1):
        for b in range(group):
            s_scr[:, pl.ds((r * group + b) * LANES, LANES)] = spread[
                b * levels : (b + 1) * levels, r * LANES : (r + 1) * LANES
            ]
    ordered = jnp.dot(order_ref[...], pert_ref[0], preferred_element_type=jnp.float32)
    lane = lax.broadcasted_iota(jnp.int32, (levels, LANES), 1)
    keep = lane < LANES - shift_lanes
    half = levels // 2

    def rolled(k):
        block = s_scr[:, pl.ds(pl.multiple_of((k + shift_blocks) * LANES, LANES), LANES)]
        return pltpu.roll(block, lax.rem(LANES - shift_lanes, LANES), 1)

    here = rolled(0)
    for k in range(count * group):
        after = rolled(k + 1)
        at = jnp.where(keep, here, after)
        part = pl.ds(k * LANES, LANES)
        value = ordered[:, k * LANES : (k + 1) * LANES] * at
        value = jnp.where(lane < width - k * LANES, value, 0.0).astype(jnp.bfloat16)
        own_ref[:, part] = value[:half]
        send_ref[:, part] = value[half:]
        here = after


def localize(begin_row, rows, cols, place, tile_widths, arrived, weight, order, perturbations):
    levels = perturbations.shape[1]
    chunk = ROWS_PER_BLOCK * cols
    assert rows % ROWS_PER_BLOCK == 0 and begin_row % ROWS_PER_BLOCK == 0
    skip = begin_row // ROWS_PER_BLOCK
    group = weight.shape[1] // levels
    parts = tuple(len(one) for one in arrived)
    scalars = pl.BlockSpec(memory_space=pltpu.SMEM)
    vector = pl.BlockSpec(memory_space=pltpu.VMEM)
    half = jax.ShapeDtypeStruct((levels // 2, rows * cols), jnp.bfloat16)
    half_spec = pl.BlockSpec((levels // 2, chunk), lambda i: (0, i))
    return pl.pallas_call(
        functools.partial(localize_kernel, begin_row, cols, parts),
        grid=(rows // ROWS_PER_BLOCK,),
        out_shape=(half, half),
        in_specs=[scalars] * 2 + [pl.BlockSpec(memory_space=pl.ANY)] * sum(parts) + [vector, vector,
                  pl.BlockSpec((1, levels, chunk), lambda i: (0, 0, i + skip))],
        out_specs=(half_spec, half_spec),
        scratch_shapes=[
            pltpu.VMEM((levels, chunk + group * LANES), jnp.float32),
            pltpu.VMEM(
                (len(parts), weight.shape[2], (rows // (group * LANES // cols) + 1) * LANES),
                jnp.bfloat16,
            ),
            pltpu.SemaphoreType.DMA((sum(parts),)),
        ],
        compiler_params=pltpu.CompilerParams(vmem_limit_bytes=16 << 20),
        name="localize",
    )(place, tile_widths, *sum(map(list, arrived), []), weight, order, perturbations)


def body(
    alpha_weights, perturbations, coef_x, coef_y, level_scale, level_map, tile_widths, band_widths
):
    _, lev_dev, _, cols = alpha_weights.shape
    _, levels, capacity = perturbations.shape
    tiles = tile_widths.shape[0]
    tall = capacity // cols
    assert sum(PIECES) == tall and lev_dev == 2
    groups = tiles // LINE
    mem = lax.axis_index("mem")
    place = lax.axis_index("lev").astype(jnp.int32).reshape(1)

    def shifted(dy, dz):
        return [
            (y * LINE + z, (y + dy) % groups * LINE + (z + dz) % LINE)
            for y in range(groups)
            for z in range(LINE)
        ]

    def smooth(v):
        return smooth_and_cut(
            v, place, level_scale, level_map, tile_widths, alpha_weights, coef_x, coef_y, tall
        )

    planes = smooth(0)
    come = [planes[0]]
    for d in range(1, LINE):
        come.append(lax.ppermute(planes[d], "lev", shifted(0, d)))
    outgoing = smooth(1)[0]
    arrived = lax.all_to_all(outgoing, "lev", split_axis=0, concat_axis=0, tiled=True)
    joined = []
    for e in range(groups):
        one = jnp.concatenate([plane[e] for plane in come], axis=0)
        if e > 0:
            one = lax.ppermute(one, "lev", shifted(e, 0))
        joined.append(one)
    inputs = (joined, [arrived.reshape(tiles * SUBS, -1)])

    slot = jnp.arange(levels)
    core = (mem + slot // 16) % CORES
    ring = (mem // CORES + (1 - 2 * core) * (slot // 4)) % RING
    half = (mem // (CORES * RING) + slot // 2) % HALVES
    row_level = half * 16 + ring * 4 + core * 2 + slot % 2
    order = (row_level[:, None] == slot[None, :]).astype(jnp.bfloat16)
    row_band = jnp.sum(jnp.where(row_level[:, None] == slot[None, :], band_widths[None, :], 0), 1)
    at = jnp.arange(tiles)
    near = (place[0] // LINE - at // LINE) % groups * LINE + (place[0] - at) % LINE
    col_slot = jnp.stack([near * lev_dev, at * lev_dev + 1])
    match = col_slot[:, :, None] == slot
    col_level = jnp.sum(jnp.where(match, level_map, 0), 2)
    match = col_level[:, :, None] == slot
    col_band = jnp.sum(jnp.where(match, band_widths, 0), 2)
    distance = jnp.abs(row_level[None, :, None] - col_level[:, None, :]).astype(jnp.float32)
    mutual = jnp.minimum(row_band[None, :, None], col_band[:, None, :]).astype(jnp.float32)
    local = jnp.where(distance <= mutual, jnp.exp(-distance * distance / (mutual * mutual)), 0.0)
    group = jnp.arange(SUBS)
    same = (group[:, None, None, None] == group).reshape(1, SUBS, 1, 1, SUBS)
    weight = jnp.where(same, local[:, None, :, :, None], 0.0).astype(jnp.bfloat16)
    weight = weight.reshape(lev_dev, SUBS * levels, tiles * SUBS)

    results = []
    begin = 0
    for rows_here in PIECES:
        own, other = localize(
            begin, rows_here, cols, place, tile_widths, inputs, weight, order, perturbations
        )
        results.append(sum_members(own, other))
        begin += rows_here
    return jnp.concatenate(results, axis=1)


def sum_members(own, other):
    def wide(x):
        return x.astype(jnp.float32)

    def narrow(x):
        return x.astype(jnp.bfloat16)

    def moved(dz, dx, dc):
        pairs = []
        for z in range(HALVES):
            for x in range(RING):
                for c in range(CORES):
                    along = dx * (1 - 2 * c)
                    to = ((z + dz) % HALVES, (x + along) % RING, (c + dc) % CORES)
                    pairs.append(((z * RING + x) * CORES + c, (to[0] * RING + to[1]) * CORES + to[2]))
        return pairs

    keep = own.shape[0] // RING
    came = lax.ppermute(other, "mem", moved(0, 0, 1))
    total = wide(own[:keep]) + wide(came[:keep])
    beside = wide(own[keep : 2 * keep]) + wide(came[keep : 2 * keep])
    pair = narrow(wide(own[2 * keep :]) + wide(came[2 * keep :]))
    relay = lax.ppermute(pair[:keep], "mem", moved(0, 1, 0))
    direct = lax.ppermute(pair[keep:], "mem", moved(0, -1, 0))
    joined = lax.ppermute(narrow(beside + wide(relay)), "mem", moved(0, 1, 0))
    total = total + wide(direct) + wide(joined)
    keep //= HALVES
    far = lax.ppermute(narrow(total[keep:]), "mem", moved(1, 0, 0))
    return total[:keep] + wide(far)


def solution(mesh):
    placed = (P("mem", "lev", None, None), P("mem", None, "lev"), P(), P(), P(), P(), P(), P())

    return jax.shard_map(
        body, mesh=mesh, in_specs=placed, out_specs=P("mem", "lev"), check_vma=False
    )
```

time: 93.7 us -> 87.2 us (0.931)
  the two profiles are of different devices: /device:TPU:1 before, /device:TPU:32 now
where the time goes in v6:
time: 87.2 us; the launch traced here: 86.9 us
  starting transfers between devices  32.1 us (37%)
  waiting for transfers between devices  26.7 us (31%)
  Pallas kernels  24.2 us (28%)
  other arithmetic  2.33 us (3%)
  local copies, waits for them, and re-layouts  1.35 us (2%)
    pallas_call x2, Pallas kernels, smooth_and_cut(): pl.pallas_call(functools.partial(diffuse_kernel, level), out_shape=[jax.S...  18.7 us
    ppermute x3, waiting for transfers between devices, body(): one = lax.ppermute(one, 'lev', shifted(e, 0))  14.9 us
    ppermute x2, starting transfers between devices, sum_members(): far = lax.ppermute(narrow(total[keep:]), 'mem', moved(1, 0, 0))  8.25 us
    ppermute x2, waiting for transfers between devices, sum_members(): far = lax.ppermute(narrow(total[keep:]), 'mem', moved(1, 0, 0))  6.16 us
    all_to_all x1, starting transfers between devices, body(): lax.all_to_all(outgoing, 'lev', split_axis=0, concat_axis=0, tiled=True)  6.09 us
    pallas_call x2, Pallas kernels, localize(): pl.pallas_call(functools.partial(localize_kernel, begin_row, cols, parts)...  5.5 us
    ppermute x3, starting transfers between devices, body(): come.append(lax.ppermute(planes[d], 'lev', shifted(0, d)))  5.38 us
    ppermute x2, starting transfers between devices, sum_members(): direct = lax.ppermute(pair[keep:], 'mem', moved(0, -1, 0))  4.71 us
  transfers between devices with their start and end apart: 17, of which 7 were waited for; matrix products, arithmetic and copies ran while one was open for 3% of the time, Pallas kernels for 14%

profile of v6, /device:TPU:32, one launch (start us, length us, event | category | flops | bytes accessed | tf_op | source)
XLA Modules:
  0.0 86.9 jit_solution(17593228998631575747)
XLA Ops:
  0.0 9.4 %diffuse.2 = (bf16[4,8,3200]{2,1,0:T(8,128)(2,1)}, bf16[4,8,3200]{2,1,0:T(8,128)(2,1)}, bf16[4,8,3200]{2,1,0:T(8,128)(2,1)}, bf16[4,8,3200]{2,1,0:T(8,128)(2,1)}) custom-call(s32[1]{0:T(128)} %bitcast.place_ref, f32[32]{0:T(128)} %scale_ref.3, s32[32]{0:T(128)} %map_ref.3, s32[16]{0:T(128)} %width_ref.7, f32[1,2,384,512]{3,2,1,0:T(8,128)} %alpha_ref.3, ...), custom_call_target="tpu_custom_call" | custom-call | tf_op jit(solution)/shard_map/diffuse/pallas_call | solution.py:172
  9.4 2.0 %collective-permute-start = (bf16[4,8,3200]{2,1,0:T(8,128)(2,1)}, bf16[4,8,3200]{2,1,0:T(8,128)(2,1)S(1)}, u32[]{:S(2)}, u32[]{:S(2)}) collective-permute-start(bf16[4,8,3200]{2,1,0:T(8,128)(2,1)} %get-tuple-element.14), channel_id=1, source_target_pairs={{0,1},{1,2},{2,3},{3,0},{4,5},{5,6},{6,7},{7,4},{8,9},{9,10},{10,1... | collective-permute-start | bytes 614408 | tf_op jit(solution)/shard_map/ppermute | solution.py:329
  11.4 2.3 %collective-permute-start.1 = (bf16[4,8,3200]{2,1,0:T(8,128)(2,1)}, bf16[4,8,3200]{2,1,0:T(8,128)(2,1)S(1)}, u32[]{:S(2)}, u32[]{:S(2)}) collective-permute-start(bf16[4,8,3200]{2,1,0:T(8,128)(2,1)} %get-tuple-element.15), channel_id=1, source_target_pairs={{0,2},{1,3},{2,0},{3,1},{4,6},{5,7},{6,4},{7,5},{8,10},{9,11},{10,... | collective-permute-start | bytes 614408 | tf_op jit(solution)/shard_map/ppermute | solution.py:329
  13.6 1.1 %collective-permute-start.2 = (bf16[4,8,3200]{2,1,0:T(8,128)(2,1)}, bf16[4,8,3200]{2,1,0:T(8,128)(2,1)S(1)}, u32[]{:S(2)}, u32[]{:S(2)}) collective-permute-start(bf16[4,8,3200]{2,1,0:T(8,128)(2,1)} %get-tuple-element.16), channel_id=1, source_target_pairs={{0,3},{1,0},{2,1},{3,2},{4,7},{5,4},{6,5},{7,6},{8,11},{9,8},{10,9... | collective-permute-start | bytes 614408 | tf_op jit(solution)/shard_map/ppermute | solution.py:329
  14.8 9.3 %diffuse.3 = bf16[16,8,3200]{2,1,0:T(8,128)(2,1)} custom-call(s32[1]{0:T(128)} %bitcast.place_ref, f32[32]{0:T(128)} %scale_ref.3, s32[32]{0:T(128)} %map_ref.3, s32[16]{0:T(128)} %width_ref.7, f32[1,2,384,512]{3,2,1,0:T(8,128)} %alpha_ref.3, f32[384,512]{1,0:T(8,128)} %cx_ref.3, f32[384,512]{1,0:T(8,128)} %cy_ref.3), custom_call_target="tpu_custom_call" | custom-call | tf_op jit(solution)/shard_map/diffuse/pallas_call | solution.py:172
  24.1 6.1 %all-to-all-start = ((bf16[16,8,3200]{2,1,0:T(8,128)(2,1)}), bf16[16,8,3200]{2,1,0:T(8,128)(2,1)S(1)}, u32[]{:S(2)}, u32[]{:S(2)}) async-start(bf16[16,8,3200]{2,1,0:T(8,128)(2,1)} %diffuse.3), calls=%async_computation | async-start | bytes 1638400 | tf_op jit(solution)/shard_map/all_to_all | solution.py:331
  30.3 0.2 select_reduce_fusion.2
  30.5 0.2 select_reduce_fusion.1
  30.7 0.2 select_reduce_fusion
  30.9 0.1 fusion.2
  31.0 0.1 broadcast_in_dim.79
  31.1 0.4 broadcast_in_dim.80
  31.4 0.1 copy.12
  31.6 0.1 broadcast_in_dim.70
  31.7 0.2 broadcast_in_dim.71
  31.9 0.1 copy.11
  32.1 0.1 fusion.3.refs_6_
  32.3 2.8 %collective-permute-start.5 = (bf16[32,3200]{1,0:T(8,128)(2,1)S(1)}, bf16[32,3200]{1,0:T(8,128)(2,1)S(1)}, u32[]{:S(2)}, u32[]{:S(2)}) collective-permute-start(bf16[32,3200]{1,0:T(8,128)(2,1)S(1)} %pad_maximum_fusion.3), channel_id=1, source_target_pairs={{0,12},{1,13},{2,14},{3,15},{4,0},{5,1},{6,2},{7,3},{8,4},{9,5},{1... | collective-permute-start | bytes 614408 | tf_op jit(solution)/shard_map/ppermute | solution.py:336
  35.1 0.9 %collective-permute-start.4 = (bf16[32,3200]{1,0:T(8,128)(2,1)S(1)}, bf16[32,3200]{1,0:T(8,128)(2,1)S(1)}, u32[]{:S(2)}, u32[]{:S(2)}) collective-permute-start(bf16[32,3200]{1,0:T(8,128)(2,1)S(1)} %pad_maximum_fusion.2), channel_id=1, source_target_pairs={{0,8},{1,9},{2,10},{3,11},{4,12},{5,13},{6,14},{7,15},{8,0},{9,1},... | collective-permute-start | bytes 614408 | tf_op jit(solution)/shard_map/ppermute | solution.py:336
  36.1 0.9 %collective-permute-start.3 = (bf16[32,3200]{1,0:T(8,128)(2,1)S(1)}, bf16[32,3200]{1,0:T(8,128)(2,1)S(1)}, u32[]{:S(2)}, u32[]{:S(2)}) collective-permute-start(bf16[32,3200]{1,0:T(8,128)(2,1)S(1)} %pad_maximum_fusion.1), channel_id=1, source_target_pairs={{0,4},{1,5},{2,6},{3,7},{4,8},{5,9},{6,10},{7,11},{8,12},{9,13},{1... | collective-permute-start | bytes 614408 | tf_op jit(solution)/shard_map/ppermute | solution.py:336
  37.0 10.4 %collective-permute-done.5.refs_3_ = bf16[32,3200]{1,0:T(8,128)(2,1)S(1)} collective-permute-done((bf16[32,3200]{1,0:T(8,128)(2,1)S(1)}, bf16[32,3200]{1,0:T(8,128)(2,1)S(1)}, u32[]{:S(2)}, u32[]{:S(2)}) %collective-permute-start.5) | collective-permute-done | bytes 204832 | tf_op jit(solution)/shard_map/ppermute | solution.py:336
  47.4 1.6 %collective-permute-done.4.refs_2_ = bf16[32,3200]{1,0:T(8,128)(2,1)S(1)} collective-permute-done((bf16[32,3200]{1,0:T(8,128)(2,1)S(1)}, bf16[32,3200]{1,0:T(8,128)(2,1)S(1)}, u32[]{:S(2)}, u32[]{:S(2)}) %collective-permute-start.4) | collective-permute-done | bytes 204832 | tf_op jit(solution)/shard_map/ppermute | solution.py:336
  49.0 2.9 %collective-permute-done.3.refs_1_ = bf16[32,3200]{1,0:T(8,128)(2,1)S(1)} collective-permute-done((bf16[32,3200]{1,0:T(8,128)(2,1)S(1)}, bf16[32,3200]{1,0:T(8,128)(2,1)S(1)}, u32[]{:S(2)}, u32[]{:S(2)}) %collective-permute-start.3) | collective-permute-done | bytes 204832 | tf_op jit(solution)/shard_map/ppermute | solution.py:336
  52.0 2.8 %localize.2 = (bf16[16,12288]{1,0:T(8,128)(2,1)S(1)}, bf16[16,12288]{1,0:T(8,128)(2,1)S(1)}) custom-call(s32[1]{0:T(128)} %bitcast.place_ref, s32[16]{0:T(128)S(1)} %copy-done.1, bf16[32,3200]{1,0:T(8,128)(2,1)S(1)} %pad_maximum_fusion.refs_0_, bf16[32,3200]{1,0:T(8,128)(2,1)S(1)} %collective-permute-done.3.refs_1_, ...), custom_call_target="tpu_custom_call" | custom-call | tf_op jit(solution)/shard_map/localize/pallas_call | solution.py:282
  54.7 0.4 collective-permute-start.6
  55.1 2.7 %localize.3 = (bf16[16,12288]{1,0:T(8,128)(2,1)S(1)}, bf16[16,12288]{1,0:T(8,128)(2,1)S(1)}) custom-call(s32[1]{0:T(128)} %bitcast.place_ref, s32[16]{0:T(128)S(1)} %copy-done.1, bf16[32,3200]{1,0:T(8,128)(2,1)S(1)} %pad_maximum_fusion.refs_0_, bf16[32,3200]{1,0:T(8,128)(2,1)S(1)} %collective-permute-done.3.refs_1_, ...), custom_call_target="tpu_custom_call" | custom-call | tf_op jit(solution)/shard_map/localize/pallas_call | solution.py:282
  57.9 0.5 collective-permute-start.11
  58.4 0.1 fusion.23
  58.5 1.6 %collective-permute-start.8 = (bf16[4,12288]{1,0:T(4,128)(2,1)S(1)}, bf16[4,12288]{1,0:T(4,128)(2,1)S(1)}, u32[]{:S(2)}, u32[]{:S(2)}) collective-permute-start(bf16[4,12288]{1,0:T(4,128)(2,1)S(1)} %get-tuple-element.38), channel_id=1, source_target_pairs={{0,32},{16,112},{32,64},{48,16},{64,96},{80,48},{96,0},{112,80},{1... | collective-permute-start | bytes 294920 | tf_op jit(solution)/shard_map/ppermute | solution.py:395
  60.1 1.7 %collective-permute-start.7 = (bf16[4,12288]{1,0:T(4,128)(2,1)S(1)}, bf16[4,12288]{1,0:T(4,128)(2,1)S(1)}, u32[]{:S(2)}, u32[]{:S(2)}) collective-permute-start(bf16[4,12288]{1,0:T(4,128)(2,1)S(1)} %get-tuple-element.37), channel_id=1, source_target_pairs={{0,96},{16,48},{32,0},{48,80},{64,32},{80,112},{96,64},{112,16},{1... | collective-permute-start | bytes 294920 | tf_op jit(solution)/shard_map/ppermute | solution.py:396
  61.9 0.1 fusion.24
  61.9 0.4 collective-permute-start.13
  62.3 3.0 %collective-permute-start.12 = (bf16[4,12288]{1,0:T(4,128)(2,1)S(1)}, bf16[4,12288]{1,0:T(4,128)(2,1)S(1)}, u32[]{:S(2)}, u32[]{:S(2)}) collective-permute-start(bf16[4,12288]{1,0:T(4,128)(2,1)S(1)} %get-tuple-element.39), channel_id=1, source_target_pairs={{0,96},{16,48},{32,0},{48,80},{64,32},{80,112},{96,64},{112,16},{1... | collective-permute-start | bytes 294920 | tf_op jit(solution)/shard_map/ppermute | solution.py:396
  65.3 0.2 add_convert_fusion.3
  65.4 0.1 collective-permute-start.9
  65.5 2.3 %collective-permute-done.13 = bf16[4,12288]{1,0:T(4,128)(2,1)S(1)} collective-permute-done((bf16[4,12288]{1,0:T(4,128)(2,1)S(1)}, bf16[4,12288]{1,0:T(4,128)(2,1)S(1)}, u32[]{:S(2)}, u32[]{:S(2)}) %collective-permute-start.13) | collective-permute-done | bytes 98336 | tf_op jit(solution)/shard_map/ppermute | solution.py:395
  67.8 0.1 add_convert_fusion.2
  68.0 0.1 collective-permute-start.14
  68.1 3.2 %collective-permute-done.9 = bf16[4,12288]{1,0:T(4,128)(2,1)S(1)} collective-permute-done((bf16[4,12288]{1,0:T(4,128)(2,1)S(1)}, bf16[4,12288]{1,0:T(4,128)(2,1)S(1)}, u32[]{:S(2)}, u32[]{:S(2)}) %collective-permute-start.9) | collective-permute-done | bytes 98336 | tf_op jit(solution)/shard_map/ppermute | solution.py:397
  71.3 0.1 convert_add_fusion.1
  71.4 0.1 slice.205
  71.5 5.9 %collective-permute-start.10 = (bf16[2,12288]{1,0:T(2,128)(2,1)S(1)}, bf16[2,12288]{1,0:T(2,128)(2,1)S(1)}, u32[]{:S(2)}, u32[]{:S(2)}) collective-permute-start(bf16[2,12288]{1,0:T(2,128)(2,1)S(1)} %slice.205), channel_id=1, source_target_pairs={{0,128},{16,144},{32,160},{48,176},{64,192},{80,208},{96,224},{112... | collective-permute-start | bytes 147464 | tf_op jit(solution)/shard_map/ppermute | solution.py:400
  77.3 0.1 convert_add_fusion
  77.4 0.1 slice.204
  77.5 2.4 %collective-permute-start.15 = (bf16[2,12288]{1,0:T(2,128)(2,1)S(1)}, bf16[2,12288]{1,0:T(2,128)(2,1)S(1)}, u32[]{:S(2)}, u32[]{:S(2)}) collective-permute-start(bf16[2,12288]{1,0:T(2,128)(2,1)S(1)} %slice.204), channel_id=1, source_target_pairs={{0,128},{16,144},{32,160},{48,176},{64,192},{80,208},{96,224},{112... | collective-permute-start | bytes 147464 | tf_op jit(solution)/shard_map/ppermute | solution.py:400
  79.9 0.3 collective-permute-done.10
  80.2 5.9 %collective-permute-done.15 = bf16[2,12288]{1,0:T(2,128)(2,1)S(1)} collective-permute-done((bf16[2,12288]{1,0:T(2,128)(2,1)S(1)}, bf16[2,12288]{1,0:T(2,128)(2,1)S(1)}, u32[]{:S(2)}, u32[]{:S(2)}) %collective-permute-start.15) | collective-permute-done | bytes 49184 | tf_op jit(solution)/shard_map/ppermute | solution.py:400
  86.2 0.8 pad_maximum_fusion.4
  (38 shorter events, 0.5 us)
Async XLA Ops:
  9.4 22.8 %collective-permute-start = (bf16[4,8,3200]{2,1,0:T(8,128)(2,1)}, bf16[4,8,3200]{2,1,0:T(8,128)(2,1)S(1)}, u32[]{:S(2)}, u32[]{:S(2)}) collective-permute-start(bf16[4,8,3200]{2,1,0:T(8,128)(2,1)} %get-tuple-element.14), channel_id=1, source_target_pairs={{0,1},{1,2},{2,3},{3,0},{4,5},{5,6},{6,7},{7,4},{8,9},{9,10},{10,1... | collective-permute-start | bytes 614408 | tf_op jit(solution)/shard_map/ppermute | solution.py:329
  11.4 20.9 %collective-permute-start.1 = (bf16[4,8,3200]{2,1,0:T(8,128)(2,1)}, bf16[4,8,3200]{2,1,0:T(8,128)(2,1)S(1)}, u32[]{:S(2)}, u32[]{:S(2)}) collective-permute-start(bf16[4,8,3200]{2,1,0:T(8,128)(2,1)} %get-tuple-element.15), channel_id=1, source_target_pairs={{0,2},{1,3},{2,0},{3,1},{4,6},{5,7},{6,4},{7,5},{8,10},{9,11},{10,... | collective-permute-start | bytes 614408 | tf_op jit(solution)/shard_map/ppermute | solution.py:329
  13.6 18.6 %collective-permute-start.2 = (bf16[4,8,3200]{2,1,0:T(8,128)(2,1)}, bf16[4,8,3200]{2,1,0:T(8,128)(2,1)S(1)}, u32[]{:S(2)}, u32[]{:S(2)}) collective-permute-start(bf16[4,8,3200]{2,1,0:T(8,128)(2,1)} %get-tuple-element.16), channel_id=1, source_target_pairs={{0,3},{1,0},{2,1},{3,2},{4,7},{5,4},{6,5},{7,6},{8,11},{9,8},{10,9... | collective-permute-start | bytes 614408 | tf_op jit(solution)/shard_map/ppermute | solution.py:329
  24.1 6.2 %copy-start.3 = (s32[32]{0:T(128)S(1)}, s32[32]{0:T(128)}, u32[]{:S(2)}) copy-start(s32[32]{0:T(128)} %map_ref.3) | copy-start | bytes 388
  24.1 6.4 %copy-start.4 = (s32[32]{0:T(128)S(1)}, s32[32]{0:T(128)}, u32[]{:S(2)}) copy-start(s32[32]{0:T(128)} %param.15) | copy-start | bytes 388
  24.1 7.9 %copy-start.2 = (bf16[4,8,3200]{2,1,0:T(8,128)(2,1)S(1)}, bf16[4,8,3200]{2,1,0:T(8,128)(2,1)}, u32[]{:S(2)}) copy-start(bf16[4,8,3200]{2,1,0:T(8,128)(2,1)} %get-tuple-element.13) | copy-start | bytes 614404
  24.1 27.9 %all-to-all-start = ((bf16[16,8,3200]{2,1,0:T(8,128)(2,1)}), bf16[16,8,3200]{2,1,0:T(8,128)(2,1)S(1)}, u32[]{:S(2)}, u32[]{:S(2)}) async-start(bf16[16,8,3200]{2,1,0:T(8,128)(2,1)} %diffuse.3), calls=%async_computation | async-start | bytes 1638400 | tf_op jit(solution)/shard_map/all_to_all | solution.py:331
  32.1 19.9 %copy-start = (bf16[1,32,24576]{2,1,0:T(8,128)(2,1)S(1)}, bf16[1,32,24576]{2,1,0:T(8,128)(2,1)}, u32[]{:S(2)}) copy-start(bf16[1,32,24576]{2,1,0:T(8,128)(2,1)} %refs_7_.3) | copy-start | bytes 4718596
  32.1 19.9 %copy-start.1 = (s32[16]{0:T(128)S(1)}, s32[16]{0:T(128)}, u32[]{:S(2)}) copy-start(s32[16]{0:T(128)} %width_ref.7) | copy-start | bytes 196
  32.3 15.1 %collective-permute-start.5 = (bf16[32,3200]{1,0:T(8,128)(2,1)S(1)}, bf16[32,3200]{1,0:T(8,128)(2,1)S(1)}, u32[]{:S(2)}, u32[]{:S(2)}) collective-permute-start(bf16[32,3200]{1,0:T(8,128)(2,1)S(1)} %pad_maximum_fusion.3), channel_id=1, source_target_pairs={{0,12},{1,13},{2,14},{3,15},{4,0},{5,1},{6,2},{7,3},{8,4},{9,5},{1... | collective-permute-start | bytes 614408 | tf_op jit(solution)/shard_map/ppermute | solution.py:336
  35.1 13.9 %collective-permute-start.4 = (bf16[32,3200]{1,0:T(8,128)(2,1)S(1)}, bf16[32,3200]{1,0:T(8,128)(2,1)S(1)}, u32[]{:S(2)}, u32[]{:S(2)}) collective-permute-start(bf16[32,3200]{1,0:T(8,128)(2,1)S(1)} %pad_maximum_fusion.2), channel_id=1, source_target_pairs={{0,8},{1,9},{2,10},{3,11},{4,12},{5,13},{6,14},{7,15},{8,0},{9,1},... | collective-permute-start | bytes 614408 | tf_op jit(solution)/shard_map/ppermute | solution.py:336
  36.1 15.9 %collective-permute-start.3 = (bf16[32,3200]{1,0:T(8,128)(2,1)S(1)}, bf16[32,3200]{1,0:T(8,128)(2,1)S(1)}, u32[]{:S(2)}, u32[]{:S(2)}) collective-permute-start(bf16[32,3200]{1,0:T(8,128)(2,1)S(1)} %pad_maximum_fusion.1), channel_id=1, source_target_pairs={{0,4},{1,5},{2,6},{3,7},{4,8},{5,9},{6,10},{7,11},{8,12},{9,13},{1... | collective-permute-start | bytes 614408 | tf_op jit(solution)/shard_map/ppermute | solution.py:336
  54.7 3.6 %collective-permute-start.6 = (bf16[16,12288]{1,0:T(8,128)(2,1)S(1)}, bf16[16,12288]{1,0:T(8,128)(2,1)S(1)}, u32[]{:S(2)}, u32[]{:S(2)}) collective-permute-start(bf16[16,12288]{1,0:T(8,128)(2,1)S(1)} %get-tuple-element.18), channel_id=1, source_target_pairs={{0,16},{16,0},{32,48},{48,32},{64,80},{80,64},{96,112},{112,96},{1... | collective-permute-start | bytes 1179656 | tf_op jit(solution)/shard_map/ppermute | solution.py:391
  57.9 3.9 %collective-permute-start.11 = (bf16[16,12288]{1,0:T(8,128)(2,1)S(1)}, bf16[16,12288]{1,0:T(8,128)(2,1)S(1)}, u32[]{:S(2)}, u32[]{:S(2)}) collective-permute-start(bf16[16,12288]{1,0:T(8,128)(2,1)S(1)} %get-tuple-element.20), channel_id=1, source_target_pairs={{0,16},{16,0},{32,48},{48,32},{64,80},{80,64},{96,112},{112,96},{1... | collective-permute-start | bytes 1179656 | tf_op jit(solution)/shard_map/ppermute | solution.py:391
  58.5 6.8 %collective-permute-start.8 = (bf16[4,12288]{1,0:T(4,128)(2,1)S(1)}, bf16[4,12288]{1,0:T(4,128)(2,1)S(1)}, u32[]{:S(2)}, u32[]{:S(2)}) collective-permute-start(bf16[4,12288]{1,0:T(4,128)(2,1)S(1)} %get-tuple-element.38), channel_id=1, source_target_pairs={{0,32},{16,112},{32,64},{48,16},{64,96},{80,48},{96,0},{112,80},{1... | collective-permute-start | bytes 294920 | tf_op jit(solution)/shard_map/ppermute | solution.py:395
  60.1 8.0 %collective-permute-start.7 = (bf16[4,12288]{1,0:T(4,128)(2,1)S(1)}, bf16[4,12288]{1,0:T(4,128)(2,1)S(1)}, u32[]{:S(2)}, u32[]{:S(2)}) collective-permute-start(bf16[4,12288]{1,0:T(4,128)(2,1)S(1)} %get-tuple-element.37), channel_id=1, source_target_pairs={{0,96},{16,48},{32,0},{48,80},{64,32},{80,112},{96,64},{112,16},{1... | collective-permute-start | bytes 294920 | tf_op jit(solution)/shard_map/ppermute | solution.py:396
  61.9 5.9 %collective-permute-start.13 = (bf16[4,12288]{1,0:T(4,128)(2,1)S(1)}, bf16[4,12288]{1,0:T(4,128)(2,1)S(1)}, u32[]{:S(2)}, u32[]{:S(2)}) collective-permute-start(bf16[4,12288]{1,0:T(4,128)(2,1)S(1)} %get-tuple-element.40), channel_id=1, source_target_pairs={{0,32},{16,112},{32,64},{48,16},{64,96},{80,48},{96,0},{112,80},{1... | collective-permute-start | bytes 294920 | tf_op jit(solution)/shard_map/ppermute | solution.py:395
  62.3 15.0 %collective-permute-start.12 = (bf16[4,12288]{1,0:T(4,128)(2,1)S(1)}, bf16[4,12288]{1,0:T(4,128)(2,1)S(1)}, u32[]{:S(2)}, u32[]{:S(2)}) collective-permute-start(bf16[4,12288]{1,0:T(4,128)(2,1)S(1)} %get-tuple-element.39), channel_id=1, source_target_pairs={{0,96},{16,48},{32,0},{48,80},{64,32},{80,112},{96,64},{112,16},{1... | collective-permute-start | bytes 294920 | tf_op jit(solution)/shard_map/ppermute | solution.py:396
  65.4 5.9 %collective-permute-start.9 = (bf16[4,12288]{1,0:T(4,128)(2,1)S(1)}, bf16[4,12288]{1,0:T(4,128)(2,1)S(1)}, u32[]{:S(2)}, u32[]{:S(2)}) collective-permute-start(bf16[4,12288]{1,0:T(4,128)(2,1)S(1)} %add_convert_fusion.3), channel_id=1, source_target_pairs={{0,32},{16,112},{32,64},{48,16},{64,96},{80,48},{96,0},{112,80},{1... | collective-permute-start | bytes 294920 | tf_op jit(solution)/shard_map/ppermute | solution.py:397
  68.0 9.4 %collective-permute-start.14 = (bf16[4,12288]{1,0:T(4,128)(2,1)S(1)}, bf16[4,12288]{1,0:T(4,128)(2,1)S(1)}, u32[]{:S(2)}, u32[]{:S(2)}) collective-permute-start(bf16[4,12288]{1,0:T(4,128)(2,1)S(1)} %add_convert_fusion.2), channel_id=1, source_target_pairs={{0,32},{16,112},{32,64},{48,16},{64,96},{80,48},{96,0},{112,80},{1... | collective-permute-start | bytes 294920 | tf_op jit(solution)/shard_map/ppermute | solution.py:397
  71.5 8.7 %collective-permute-start.10 = (bf16[2,12288]{1,0:T(2,128)(2,1)S(1)}, bf16[2,12288]{1,0:T(2,128)(2,1)S(1)}, u32[]{:S(2)}, u32[]{:S(2)}) collective-permute-start(bf16[2,12288]{1,0:T(2,128)(2,1)S(1)} %slice.205), channel_id=1, source_target_pairs={{0,128},{16,144},{32,160},{48,176},{64,192},{80,208},{96,224},{112... | collective-permute-start | bytes 147464 | tf_op jit(solution)/shard_map/ppermute | solution.py:400
  77.5 8.6 %collective-permute-start.15 = (bf16[2,12288]{1,0:T(2,128)(2,1)S(1)}, bf16[2,12288]{1,0:T(2,128)(2,1)S(1)}, u32[]{:S(2)}, u32[]{:S(2)}) collective-permute-start(bf16[2,12288]{1,0:T(2,128)(2,1)S(1)} %slice.204), channel_id=1, source_target_pairs={{0,128},{16,144},{32,160},{48,176},{64,192},{80,208},{96,224},{112... | collective-permute-start | bytes 147464 | tf_op jit(solution)/shard_map/ppermute | solution.py:400

commit v7 on v6

--- a/solution.py
+++ b/solution.py
@@ -339,7 +339,8 @@
 
     slot = jnp.arange(levels)
     core = (mem + slot // 16) % CORES
-    ring = (mem // CORES + (1 - 2 * core) * (slot // 4)) % RING
+    step = slot // 4 % RING
+    ring = mem // CORES % RING ^ jnp.where(step == 3, 2, jnp.where(step == 0, 0, (step + core) % 2 * 2 + 1))
     half = (mem // (CORES * RING) + slot // 2) % HALVES
     row_level = half * 16 + ring * 4 + core * 2 + slot % 2
     order = (row_level[:, None] == slot[None, :]).astype(jnp.bfloat16)
@@ -377,27 +378,25 @@
     def narrow(x):
         return x.astype(jnp.bfloat16)
 
-    def moved(dz, dx, dc):
+    def moved(dz, flips, dc):
         pairs = []
         for z in range(HALVES):
             for x in range(RING):
                 for c in range(CORES):
-                    along = dx * (1 - 2 * c)
-                    to = ((z + dz) % HALVES, (x + along) % RING, (c + dc) % CORES)
+                    to = ((z + dz) % HALVES, x ^ flips[c], (c + dc) % CORES)
                     pairs.append(((z * RING + x) * CORES + c, (to[0] * RING + to[1]) * CORES + to[2]))
         return pairs
 
-    keep = own.shape[0] // RING
-    came = lax.ppermute(other, "mem", moved(0, 0, 1))
-    total = wide(own[:keep]) + wide(came[:keep])
-    beside = wide(own[keep : 2 * keep]) + wide(came[keep : 2 * keep])
-    pair = narrow(wide(own[2 * keep :]) + wide(came[2 * keep :]))
-    relay = lax.ppermute(pair[:keep], "mem", moved(0, 1, 0))
-    direct = lax.ppermute(pair[keep:], "mem", moved(0, -1, 0))
-    joined = lax.ppermute(narrow(beside + wide(relay)), "mem", moved(0, 1, 0))
-    total = total + wide(direct) + wide(joined)
+    keep = own.shape[0] // 2
+    came = lax.ppermute(other, "mem", moved(0, (0, 0), 1))
+    mine = wide(own[:keep]) + wide(came[:keep])
+    gone = narrow(wide(own[keep:]) + wide(came[keep:]))
+    mine = mine + wide(lax.ppermute(gone, "mem", moved(0, (1, 3), 0)))
+    keep //= 2
+    beside = lax.ppermute(narrow(mine[keep:]), "mem", moved(0, (3, 1), 0))
+    total = mine[:keep] + wide(beside)
     keep //= HALVES
-    far = lax.ppermute(narrow(total[keep:]), "mem", moved(1, 0, 0))
+    far = lax.ppermute(narrow(total[keep:]), "mem", moved(1, (0, 0), 0))
     return total[:keep] + wide(far)
 
 

time: 87.2 us -> 86.3 us (0.990)
  the two profiles are of different devices: /device:TPU:32 before, /device:TPU:6 now
where the time goes in v7:
time: 86.3 us; the launch traced here: 86.1 us
  starting transfers between devices  29.2 us (34%)
  waiting for transfers between devices  28.9 us (33%)
  Pallas kernels  24.1 us (28%)
  other arithmetic  2.1 us (2%)
  local copies, waits for them, and re-layouts  1.3 us (2%)
    pallas_call x2, Pallas kernels, smooth_and_cut(): pl.pallas_call(functools.partial(diffuse_kernel, level), out_shape=[jax.S...  18.6 us
    ppermute x3, waiting for transfers between devices, body(): one = lax.ppermute(one, 'lev', shifted(e, 0))  12.1 us
    ppermute x2, starting transfers between devices, sum_members(): far = lax.ppermute(narrow(total[keep:]), 'mem', moved(1, (0, 0), 0))  8.07 us
    ppermute x3, starting transfers between devices, body(): come.append(lax.ppermute(planes[d], 'lev', shifted(0, d)))  6.27 us
    ppermute x2, waiting for transfers between devices, sum_members(): far = lax.ppermute(narrow(total[keep:]), 'mem', moved(1, (0, 0), 0))  6.15 us
    pallas_call x2, Pallas kernels, localize(): pl.pallas_call(functools.partial(localize_kernel, begin_row, cols, parts)...  5.5 us
    all_to_all x1, starting transfers between devices, body(): lax.all_to_all(outgoing, 'lev', split_axis=0, concat_axis=0, tiled=True)  5.18 us
    ppermute x3, starting transfers between devices, body(): one = lax.ppermute(one, 'lev', shifted(e, 0))  5.06 us
  transfers between devices with their start and end apart: 15, of which 10 were waited for; matrix products, arithmetic and copies ran while one was open for 3% of the time, Pallas kernels for 14%

profile of v7, /device:TPU:6, one launch (start us, length us, event | category | flops | bytes accessed | tf_op | source)
XLA Modules:
  0.0 86.1 jit_solution(11378136724439526440)
XLA Ops:
  0.0 9.3 %diffuse.2 = (bf16[4,8,3200]{2,1,0:T(8,128)(2,1)}, bf16[4,8,3200]{2,1,0:T(8,128)(2,1)}, bf16[4,8,3200]{2,1,0:T(8,128)(2,1)}, bf16[4,8,3200]{2,1,0:T(8,128)(2,1)}) custom-call(s32[1]{0:T(128)} %bitcast.place_ref, f32[32]{0:T(128)} %scale_ref.3, s32[32]{0:T(128)} %map_ref.3, s32[16]{0:T(128)} %width_ref.7, f32[1,2,384,512]{3,2,1,0:T(8,128)} %alpha_ref.3, ...), custom_call_target="tpu_custom_call" | custom-call | tf_op jit(solution)/shard_map/diffuse/pallas_call | solution.py:172
  9.3 2.0 %collective-permute-start = (bf16[4,8,3200]{2,1,0:T(8,128)(2,1)}, bf16[4,8,3200]{2,1,0:T(8,128)(2,1)S(1)}, u32[]{:S(2)}, u32[]{:S(2)}) collective-permute-start(bf16[4,8,3200]{2,1,0:T(8,128)(2,1)} %get-tuple-element.14), channel_id=1, source_target_pairs={{0,1},{1,2},{2,3},{3,0},{4,5},{5,6},{6,7},{7,4},{8,9},{9,10},{10,1... | collective-permute-start | bytes 614408 | tf_op jit(solution)/shard_map/ppermute | solution.py:329
  11.3 3.3 %collective-permute-start.1 = (bf16[4,8,3200]{2,1,0:T(8,128)(2,1)}, bf16[4,8,3200]{2,1,0:T(8,128)(2,1)S(1)}, u32[]{:S(2)}, u32[]{:S(2)}) collective-permute-start(bf16[4,8,3200]{2,1,0:T(8,128)(2,1)} %get-tuple-element.15), channel_id=1, source_target_pairs={{0,2},{1,3},{2,0},{3,1},{4,6},{5,7},{6,4},{7,5},{8,10},{9,11},{10,... | collective-permute-start | bytes 614408 | tf_op jit(solution)/shard_map/ppermute | solution.py:329
  14.6 1.0 %collective-permute-start.2 = (bf16[4,8,3200]{2,1,0:T(8,128)(2,1)}, bf16[4,8,3200]{2,1,0:T(8,128)(2,1)S(1)}, u32[]{:S(2)}, u32[]{:S(2)}) collective-permute-start(bf16[4,8,3200]{2,1,0:T(8,128)(2,1)} %get-tuple-element.16), channel_id=1, source_target_pairs={{0,3},{1,0},{2,1},{3,2},{4,7},{5,4},{6,5},{7,6},{8,11},{9,8},{10,9... | collective-permute-start | bytes 614408 | tf_op jit(solution)/shard_map/ppermute | solution.py:329
  15.6 9.3 %diffuse.3 = bf16[16,8,3200]{2,1,0:T(8,128)(2,1)} custom-call(s32[1]{0:T(128)} %bitcast.place_ref, f32[32]{0:T(128)} %scale_ref.3, s32[32]{0:T(128)} %map_ref.3, s32[16]{0:T(128)} %width_ref.7, f32[1,2,384,512]{3,2,1,0:T(8,128)} %alpha_ref.3, f32[384,512]{1,0:T(8,128)} %cx_ref.3, f32[384,512]{1,0:T(8,128)} %cy_ref.3), custom_call_target="tpu_custom_call" | custom-call | tf_op jit(solution)/shard_map/diffuse/pallas_call | solution.py:172
  25.0 5.2 %all-to-all-start = ((bf16[16,8,3200]{2,1,0:T(8,128)(2,1)}), bf16[16,8,3200]{2,1,0:T(8,128)(2,1)S(1)}, u32[]{:S(2)}, u32[]{:S(2)}) async-start(bf16[16,8,3200]{2,1,0:T(8,128)(2,1)} %diffuse.3), calls=%async_computation | async-start | bytes 1638400 | tf_op jit(solution)/shard_map/all_to_all | solution.py:331
  30.3 0.2 select_reduce_fusion.2
  30.5 0.2 select_reduce_fusion.1
  30.7 0.2 select_reduce_fusion
  30.9 0.1 fusion.2
  31.0 0.1 broadcast_in_dim.82
  31.1 0.4 broadcast_in_dim.83
  31.4 0.1 copy.12
  31.5 0.1 broadcast_in_dim.73
  31.7 0.2 broadcast_in_dim.74
  31.9 0.1 copy.11
  32.1 0.1 fusion.3.refs_6_
  32.3 3.2 %collective-permute-start.5 = (bf16[32,3200]{1,0:T(8,128)(2,1)S(1)}, bf16[32,3200]{1,0:T(8,128)(2,1)S(1)}, u32[]{:S(2)}, u32[]{:S(2)}) collective-permute-start(bf16[32,3200]{1,0:T(8,128)(2,1)S(1)} %pad_maximum_fusion.3), channel_id=1, source_target_pairs={{0,12},{1,13},{2,14},{3,15},{4,0},{5,1},{6,2},{7,3},{8,4},{9,5},{1... | collective-permute-start | bytes 614408 | tf_op jit(solution)/shard_map/ppermute | solution.py:336
  35.5 0.9 %collective-permute-start.4 = (bf16[32,3200]{1,0:T(8,128)(2,1)S(1)}, bf16[32,3200]{1,0:T(8,128)(2,1)S(1)}, u32[]{:S(2)}, u32[]{:S(2)}) collective-permute-start(bf16[32,3200]{1,0:T(8,128)(2,1)S(1)} %pad_maximum_fusion.2), channel_id=1, source_target_pairs={{0,8},{1,9},{2,10},{3,11},{4,12},{5,13},{6,14},{7,15},{8,0},{9,1},... | collective-permute-start | bytes 614408 | tf_op jit(solution)/shard_map/ppermute | solution.py:336
  36.5 0.9 %collective-permute-start.3 = (bf16[32,3200]{1,0:T(8,128)(2,1)S(1)}, bf16[32,3200]{1,0:T(8,128)(2,1)S(1)}, u32[]{:S(2)}, u32[]{:S(2)}) collective-permute-start(bf16[32,3200]{1,0:T(8,128)(2,1)S(1)} %pad_maximum_fusion.1), channel_id=1, source_target_pairs={{0,4},{1,5},{2,6},{3,7},{4,8},{5,9},{6,10},{7,11},{8,12},{9,13},{1... | collective-permute-start | bytes 614408 | tf_op jit(solution)/shard_map/ppermute | solution.py:336
  37.4 8.7 %collective-permute-done.5.refs_3_ = bf16[32,3200]{1,0:T(8,128)(2,1)S(1)} collective-permute-done((bf16[32,3200]{1,0:T(8,128)(2,1)S(1)}, bf16[32,3200]{1,0:T(8,128)(2,1)S(1)}, u32[]{:S(2)}, u32[]{:S(2)}) %collective-permute-start.5) | collective-permute-done | bytes 204832 | tf_op jit(solution)/shard_map/ppermute | solution.py:336
  46.2 0.2 collective-permute-done.4.refs_2_
  46.3 3.2 %collective-permute-done.3.refs_1_ = bf16[32,3200]{1,0:T(8,128)(2,1)S(1)} collective-permute-done((bf16[32,3200]{1,0:T(8,128)(2,1)S(1)}, bf16[32,3200]{1,0:T(8,128)(2,1)S(1)}, u32[]{:S(2)}, u32[]{:S(2)}) %collective-permute-start.3) | collective-permute-done | bytes 204832 | tf_op jit(solution)/shard_map/ppermute | solution.py:336
  49.5 3.0 %all-to-all-done = bf16[16,8,3200]{2,1,0:T(8,128)(2,1)S(1)} async-done(((bf16[16,8,3200]{2,1,0:T(8,128)(2,1)}), bf16[16,8,3200]{2,1,0:T(8,128)(2,1)S(1)}, u32[]{:S(2)}, u32[]{:S(2)}) %all-to-all-start) | async-done | bytes 819232 | tf_op jit(solution)/shard_map/all_to_all | solution.py:331
  52.6 2.7 %localize.2 = (bf16[16,12288]{1,0:T(8,128)(2,1)S(1)}, bf16[16,12288]{1,0:T(8,128)(2,1)S(1)}) custom-call(s32[1]{0:T(128)} %bitcast.place_ref, s32[16]{0:T(128)S(1)} %copy-done.1, bf16[32,3200]{1,0:T(8,128)(2,1)S(1)} %pad_maximum_fusion.refs_0_, bf16[32,3200]{1,0:T(8,128)(2,1)S(1)} %collective-permute-done.3.refs_1_, ...), custom_call_target="tpu_custom_call" | custom-call | tf_op jit(solution)/shard_map/localize/pallas_call | solution.py:282
  55.3 0.3 collective-permute-start.6
  55.6 2.8 %localize.3 = (bf16[16,12288]{1,0:T(8,128)(2,1)S(1)}, bf16[16,12288]{1,0:T(8,128)(2,1)S(1)}) custom-call(s32[1]{0:T(128)} %bitcast.place_ref, s32[16]{0:T(128)S(1)} %copy-done.1, bf16[32,3200]{1,0:T(8,128)(2,1)S(1)} %pad_maximum_fusion.refs_0_, bf16[32,3200]{1,0:T(8,128)(2,1)S(1)} %collective-permute-done.3.refs_1_, ...), custom_call_target="tpu_custom_call" | custom-call | tf_op jit(solution)/shard_map/localize/pallas_call | solution.py:282
  58.4 0.6 collective-permute-start.10
  58.9 0.1 add_convert_fusion.1
  59.0 0.9 %collective-permute-start.7 = (bf16[8,12288]{1,0:T(8,128)(2,1)S(1)}, bf16[8,12288]{1,0:T(8,128)(2,1)S(1)}, u32[]{:S(2)}, u32[]{:S(2)}) collective-permute-start(bf16[8,12288]{1,0:T(8,128)(2,1)S(1)} %add_convert_fusion.1), channel_id=1, source_target_pairs={{0,32},{16,112},{32,0},{48,80},{64,96},{80,48},{96,64},{112,16},{1... | collective-permute-start | bytes 589832 | tf_op jit(solution)/shard_map/ppermute | solution.py:394
  59.9 0.4 collective-permute-done.10
  60.3 0.9 %collective-permute-start.11 = (bf16[8,12288]{1,0:T(8,128)(2,1)S(1)}, bf16[8,12288]{1,0:T(8,128)(2,1)S(1)}, u32[]{:S(2)}, u32[]{:S(2)}) collective-permute-start(bf16[8,12288]{1,0:T(8,128)(2,1)S(1)} %add_convert_fusion), channel_id=1, source_target_pairs={{0,32},{16,112},{32,0},{48,80},{64,96},{80,48},{96,64},{112,16},{1... | collective-permute-start | bytes 589832 | tf_op jit(solution)/shard_map/ppermute | solution.py:394
  61.2 3.5 %collective-permute-done.7 = bf16[8,12288]{1,0:T(8,128)(2,1)S(1)} collective-permute-done((bf16[8,12288]{1,0:T(8,128)(2,1)S(1)}, bf16[8,12288]{1,0:T(8,128)(2,1)S(1)}, u32[]{:S(2)}, u32[]{:S(2)}) %collective-permute-start.7) | collective-permute-done | bytes 196640 | tf_op jit(solution)/shard_map/ppermute | solution.py:394
  64.7 0.1 convert_add_fusion.1
  64.8 0.6 collective-permute-start.8
  65.4 1.4 %collective-permute-done.11 = bf16[8,12288]{1,0:T(8,128)(2,1)S(1)} collective-permute-done((bf16[8,12288]{1,0:T(8,128)(2,1)S(1)}, bf16[8,12288]{1,0:T(8,128)(2,1)S(1)}, u32[]{:S(2)}, u32[]{:S(2)}) %collective-permute-start.11) | collective-permute-done | bytes 196640 | tf_op jit(solution)/shard_map/ppermute | solution.py:394
  66.8 0.1 convert_add_fusion
  67.0 1.4 %collective-permute-start.12 = (bf16[4,12288]{1,0:T(4,128)(2,1)S(1)}, bf16[4,12288]{1,0:T(4,128)(2,1)S(1)}, u32[]{:S(2)}, u32[]{:S(2)}) collective-permute-start(bf16[4,12288]{1,0:T(4,128)(2,1)S(1)} %slice.188), channel_id=1, source_target_pairs={{0,96},{16,48},{32,64},{48,16},{64,32},{80,112},{96,0},{112,80},{1... | collective-permute-start | bytes 294920 | tf_op jit(solution)/shard_map/ppermute | solution.py:396
  68.4 2.4 %collective-permute-done.8 = bf16[4,12288]{1,0:T(4,128)(2,1)S(1)} collective-permute-done((bf16[4,12288]{1,0:T(4,128)(2,1)S(1)}, bf16[4,12288]{1,0:T(4,128)(2,1)S(1)}, u32[]{:S(2)}, u32[]{:S(2)}) %collective-permute-start.8) | collective-permute-done | bytes 98336 | tf_op jit(solution)/shard_map/ppermute | solution.py:396
  70.8 0.1 slice.191
  70.9 6.1 %collective-permute-start.9 = (bf16[2,12288]{1,0:T(2,128)(2,1)S(1)}, bf16[2,12288]{1,0:T(2,128)(2,1)S(1)}, u32[]{:S(2)}, u32[]{:S(2)}) collective-permute-start(bf16[2,12288]{1,0:T(2,128)(2,1)S(1)} %slice.191), channel_id=1, source_target_pairs={{0,128},{16,144},{32,160},{48,176},{64,192},{80,208},{96,224},{112... | collective-permute-start | bytes 147464 | tf_op jit(solution)/shard_map/ppermute | solution.py:399
  77.0 0.1 slice_add_fusion
  77.0 0.1 slice.190
  77.1 2.0 %collective-permute-start.13 = (bf16[2,12288]{1,0:T(2,128)(2,1)S(1)}, bf16[2,12288]{1,0:T(2,128)(2,1)S(1)}, u32[]{:S(2)}, u32[]{:S(2)}) collective-permute-start(bf16[2,12288]{1,0:T(2,128)(2,1)S(1)} %slice.190), channel_id=1, source_target_pairs={{0,128},{16,144},{32,160},{48,176},{64,192},{80,208},{96,224},{112... | collective-permute-start | bytes 147464 | tf_op jit(solution)/shard_map/ppermute | solution.py:399
  79.1 0.6 collective-permute-done.9
  79.7 0.1 slice_add_fusion.3
  79.7 5.6 %collective-permute-done.13 = bf16[2,12288]{1,0:T(2,128)(2,1)S(1)} collective-permute-done((bf16[2,12288]{1,0:T(2,128)(2,1)S(1)}, bf16[2,12288]{1,0:T(2,128)(2,1)S(1)}, u32[]{:S(2)}, u32[]{:S(2)}) %collective-permute-start.13) | collective-permute-done | bytes 49184 | tf_op jit(solution)/shard_map/ppermute | solution.py:399
  85.3 0.8 pad_maximum_fusion.4
  (34 shorter events, 0.5 us)
Async XLA Ops:
  9.3 22.9 %collective-permute-start = (bf16[4,8,3200]{2,1,0:T(8,128)(2,1)}, bf16[4,8,3200]{2,1,0:T(8,128)(2,1)S(1)}, u32[]{:S(2)}, u32[]{:S(2)}) collective-permute-start(bf16[4,8,3200]{2,1,0:T(8,128)(2,1)} %get-tuple-element.14), channel_id=1, source_target_pairs={{0,1},{1,2},{2,3},{3,0},{4,5},{5,6},{6,7},{7,4},{8,9},{9,10},{10,1... | collective-permute-start | bytes 614408 | tf_op jit(solution)/shard_map/ppermute | solution.py:329
  11.3 20.9 %collective-permute-start.1 = (bf16[4,8,3200]{2,1,0:T(8,128)(2,1)}, bf16[4,8,3200]{2,1,0:T(8,128)(2,1)S(1)}, u32[]{:S(2)}, u32[]{:S(2)}) collective-permute-start(bf16[4,8,3200]{2,1,0:T(8,128)(2,1)} %get-tuple-element.15), channel_id=1, source_target_pairs={{0,2},{1,3},{2,0},{3,1},{4,6},{5,7},{6,4},{7,5},{8,10},{9,11},{10,... | collective-permute-start | bytes 614408 | tf_op jit(solution)/shard_map/ppermute | solution.py:329
  14.6 17.7 %collective-permute-start.2 = (bf16[4,8,3200]{2,1,0:T(8,128)(2,1)}, bf16[4,8,3200]{2,1,0:T(8,128)(2,1)S(1)}, u32[]{:S(2)}, u32[]{:S(2)}) collective-permute-start(bf16[4,8,3200]{2,1,0:T(8,128)(2,1)} %get-tuple-element.16), channel_id=1, source_target_pairs={{0,3},{1,0},{2,1},{3,2},{4,7},{5,4},{6,5},{7,6},{8,11},{9,8},{10,9... | collective-permute-start | bytes 614408 | tf_op jit(solution)/shard_map/ppermute | solution.py:329
  24.9 5.3 %copy-start.3 = (s32[32]{0:T(128)S(1)}, s32[32]{0:T(128)}, u32[]{:S(2)}) copy-start(s32[32]{0:T(128)} %map_ref.3) | copy-start | bytes 388
  24.9 5.6 %copy-start.4 = (s32[32]{0:T(128)S(1)}, s32[32]{0:T(128)}, u32[]{:S(2)}) copy-start(s32[32]{0:T(128)} %param.15) | copy-start | bytes 388
  25.0 7.1 %copy-start.2 = (bf16[4,8,3200]{2,1,0:T(8,128)(2,1)S(1)}, bf16[4,8,3200]{2,1,0:T(8,128)(2,1)}, u32[]{:S(2)}) copy-start(bf16[4,8,3200]{2,1,0:T(8,128)(2,1)} %get-tuple-element.13) | copy-start | bytes 614404
  25.0 27.6 %all-to-all-start = ((bf16[16,8,3200]{2,1,0:T(8,128)(2,1)}), bf16[16,8,3200]{2,1,0:T(8,128)(2,1)S(1)}, u32[]{:S(2)}, u32[]{:S(2)}) async-start(bf16[16,8,3200]{2,1,0:T(8,128)(2,1)} %diffuse.3), calls=%async_computation | async-start | bytes 1638400 | tf_op jit(solution)/shard_map/all_to_all | solution.py:331
  32.1 20.5 %copy-start = (bf16[1,32,24576]{2,1,0:T(8,128)(2,1)S(1)}, bf16[1,32,24576]{2,1,0:T(8,128)(2,1)}, u32[]{:S(2)}) copy-start(bf16[1,32,24576]{2,1,0:T(8,128)(2,1)} %refs_7_.3) | copy-start | bytes 4718596
  32.1 20.5 %copy-start.1 = (s32[16]{0:T(128)S(1)}, s32[16]{0:T(128)}, u32[]{:S(2)}) copy-start(s32[16]{0:T(128)} %width_ref.7) | copy-start | bytes 196
  32.3 13.9 %collective-permute-start.5 = (bf16[32,3200]{1,0:T(8,128)(2,1)S(1)}, bf16[32,3200]{1,0:T(8,128)(2,1)S(1)}, u32[]{:S(2)}, u32[]{:S(2)}) collective-permute-start(bf16[32,3200]{1,0:T(8,128)(2,1)S(1)} %pad_maximum_fusion.3), channel_id=1, source_target_pairs={{0,12},{1,13},{2,14},{3,15},{4,0},{5,1},{6,2},{7,3},{8,4},{9,5},{1... | collective-permute-start | bytes 614408 | tf_op jit(solution)/shard_map/ppermute | solution.py:336
  35.5 10.8 %collective-permute-start.4 = (bf16[32,3200]{1,0:T(8,128)(2,1)S(1)}, bf16[32,3200]{1,0:T(8,128)(2,1)S(1)}, u32[]{:S(2)}, u32[]{:S(2)}) collective-permute-start(bf16[32,3200]{1,0:T(8,128)(2,1)S(1)} %pad_maximum_fusion.2), channel_id=1, source_target_pairs={{0,8},{1,9},{2,10},{3,11},{4,12},{5,13},{6,14},{7,15},{8,0},{9,1},... | collective-permute-start | bytes 614408 | tf_op jit(solution)/shard_map/ppermute | solution.py:336
  36.5 13.0 %collective-permute-start.3 = (bf16[32,3200]{1,0:T(8,128)(2,1)S(1)}, bf16[32,3200]{1,0:T(8,128)(2,1)S(1)}, u32[]{:S(2)}, u32[]{:S(2)}) collective-permute-start(bf16[32,3200]{1,0:T(8,128)(2,1)S(1)} %pad_maximum_fusion.1), channel_id=1, source_target_pairs={{0,4},{1,5},{2,6},{3,7},{4,8},{5,9},{6,10},{7,11},{8,12},{9,13},{1... | collective-permute-start | bytes 614408 | tf_op jit(solution)/shard_map/ppermute | solution.py:336
  55.3 3.6 %collective-permute-start.6 = (bf16[16,12288]{1,0:T(8,128)(2,1)S(1)}, bf16[16,12288]{1,0:T(8,128)(2,1)S(1)}, u32[]{:S(2)}, u32[]{:S(2)}) collective-permute-start(bf16[16,12288]{1,0:T(8,128)(2,1)S(1)} %get-tuple-element.18), channel_id=1, source_target_pairs={{0,16},{16,0},{32,48},{48,32},{64,80},{80,64},{96,112},{112,96},{1... | collective-permute-start | bytes 1179656 | tf_op jit(solution)/shard_map/ppermute | solution.py:391
  58.4 1.9 %collective-permute-start.10 = (bf16[16,12288]{1,0:T(8,128)(2,1)S(1)}, bf16[16,12288]{1,0:T(8,128)(2,1)S(1)}, u32[]{:S(2)}, u32[]{:S(2)}) collective-permute-start(bf16[16,12288]{1,0:T(8,128)(2,1)S(1)} %get-tuple-element.20), channel_id=1, source_target_pairs={{0,16},{16,0},{32,48},{48,32},{64,80},{80,64},{96,112},{112,96},{1... | collective-permute-start | bytes 1179656 | tf_op jit(solution)/shard_map/ppermute | solution.py:391
  59.0 5.8 %collective-permute-start.7 = (bf16[8,12288]{1,0:T(8,128)(2,1)S(1)}, bf16[8,12288]{1,0:T(8,128)(2,1)S(1)}, u32[]{:S(2)}, u32[]{:S(2)}) collective-permute-start(bf16[8,12288]{1,0:T(8,128)(2,1)S(1)} %add_convert_fusion.1), channel_id=1, source_target_pairs={{0,32},{16,112},{32,0},{48,80},{64,96},{80,48},{96,64},{112,16},{1... | collective-permute-start | bytes 589832 | tf_op jit(solution)/shard_map/ppermute | solution.py:394
  60.3 6.5 %collective-permute-start.11 = (bf16[8,12288]{1,0:T(8,128)(2,1)S(1)}, bf16[8,12288]{1,0:T(8,128)(2,1)S(1)}, u32[]{:S(2)}, u32[]{:S(2)}) collective-permute-start(bf16[8,12288]{1,0:T(8,128)(2,1)S(1)} %add_convert_fusion), channel_id=1, source_target_pairs={{0,32},{16,112},{32,0},{48,80},{64,96},{80,48},{96,64},{112,16},{1... | collective-permute-start | bytes 589832 | tf_op jit(solution)/shard_map/ppermute | solution.py:394
  64.8 5.9 %collective-permute-start.8 = (bf16[4,12288]{1,0:T(4,128)(2,1)S(1)}, bf16[4,12288]{1,0:T(4,128)(2,1)S(1)}, u32[]{:S(2)}, u32[]{:S(2)}) collective-permute-start(bf16[4,12288]{1,0:T(4,128)(2,1)S(1)} %slice.189), channel_id=1, source_target_pairs={{0,96},{16,48},{32,64},{48,16},{64,32},{80,112},{96,0},{112,80},{1... | collective-permute-start | bytes 294920 | tf_op jit(solution)/shard_map/ppermute | solution.py:396
  67.0 10.0 %collective-permute-start.12 = (bf16[4,12288]{1,0:T(4,128)(2,1)S(1)}, bf16[4,12288]{1,0:T(4,128)(2,1)S(1)}, u32[]{:S(2)}, u32[]{:S(2)}) collective-permute-start(bf16[4,12288]{1,0:T(4,128)(2,1)S(1)} %slice.188), channel_id=1, source_target_pairs={{0,96},{16,48},{32,64},{48,16},{64,32},{80,112},{96,0},{112,80},{1... | collective-permute-start | bytes 294920 | tf_op jit(solution)/shard_map/ppermute | solution.py:396
  70.9 8.8 %collective-permute-start.9 = (bf16[2,12288]{1,0:T(2,128)(2,1)S(1)}, bf16[2,12288]{1,0:T(2,128)(2,1)S(1)}, u32[]{:S(2)}, u32[]{:S(2)}) collective-permute-start(bf16[2,12288]{1,0:T(2,128)(2,1)S(1)} %slice.191), channel_id=1, source_target_pairs={{0,128},{16,144},{32,160},{48,176},{64,192},{80,208},{96,224},{112... | collective-permute-start | bytes 147464 | tf_op jit(solution)/shard_map/ppermute | solution.py:399
  77.1 8.2 %collective-permute-start.13 = (bf16[2,12288]{1,0:T(2,128)(2,1)S(1)}, bf16[2,12288]{1,0:T(2,128)(2,1)S(1)}, u32[]{:S(2)}, u32[]{:S(2)}) collective-permute-start(bf16[2,12288]{1,0:T(2,128)(2,1)S(1)} %slice.190), channel_id=1, source_target_pairs={{0,128},{16,144},{32,160},{48,176},{64,192},{80,208},{96,224},{112... | collective-permute-start | bytes 147464 | tf_op jit(solution)/shard_map/ppermute | solution.py:399

commit v8 on v7

--- a/solution.py
+++ b/solution.py
@@ -12,7 +12,7 @@
 SUBS = 8
 ROWS_PER_BLOCK = 8
 CORES, RING, HALVES = 2, 4, 2
-PIECES = (24, 24)
+PIECES = (32, 16)
 LINE = 4
 
 
@@ -198,18 +198,40 @@
     )(place, level_scale, level_map, tile_widths, alpha, coef_x, coef_y)
 
 
+def reorder_kernel(order_ref, pert_ref, out_ref):
+    rows = jnp.dot(order_ref[...], pert_ref[0], preferred_element_type=jnp.float32)
+    out_ref[...] = rows.astype(out_ref.dtype)
+
+
+def reorder(order, perturbations):
+    _, levels, capacity = perturbations.shape
+    chunk = capacity // 6
+    return pl.pallas_call(
+        reorder_kernel,
+        grid=(capacity // chunk,),
+        out_shape=jax.ShapeDtypeStruct((levels, capacity), perturbations.dtype),
+        in_specs=[
+            pl.BlockSpec(memory_space=pltpu.VMEM),
+            pl.BlockSpec((1, levels, chunk), lambda i: (0, 0, i)),
+        ],
+        out_specs=pl.BlockSpec((levels, chunk), lambda i: (0, i)),
+        compiler_params=pltpu.CompilerParams(vmem_limit_bytes=8 << 20),
+        name="reorder",
+    )(order, perturbations)
+
+
 def localize_kernel(
     begin_row, cols, parts, place_ref, width_ref, *refs
 ):
     x_refs = refs[: sum(parts)]
-    weight_ref, order_ref, pert_ref, own_ref, send_ref, s_scr, here_scr, sem = refs[sum(parts) :]
+    weight_ref, pert_ref, own_ref, send_ref, s_scr, here_scr, sem = refs[sum(parts) :]
     step = pl.program_id(0)
     tiles = width_ref.shape[0]
-    levels = order_ref.shape[0]
+    levels = pert_ref.shape[0]
     blocks = cols // LANES
     group = weight_ref.shape[1] // levels
     pack = group // blocks
-    chunk = pert_ref.shape[2]
+    chunk = pert_ref.shape[1]
     count = chunk // (cols * pack)
     me = place_ref[0]
     first_col = 0
@@ -247,7 +269,7 @@
             s_scr[:, pl.ds((r * group + b) * LANES, LANES)] = spread[
                 b * levels : (b + 1) * levels, r * LANES : (r + 1) * LANES
             ]
-    ordered = jnp.dot(order_ref[...], pert_ref[0], preferred_element_type=jnp.float32)
+    ordered = pert_ref[...].astype(jnp.float32)
     lane = lax.broadcasted_iota(jnp.int32, (levels, LANES), 1)
     keep = lane < LANES - shift_lanes
     half = levels // 2
@@ -268,8 +290,8 @@
         here = after
 
 
-def localize(begin_row, rows, cols, place, tile_widths, arrived, weight, order, perturbations):
-    levels = perturbations.shape[1]
+def localize(begin_row, rows, cols, place, tile_widths, arrived, weight, ordered):
+    levels = ordered.shape[0]
     chunk = ROWS_PER_BLOCK * cols
     assert rows % ROWS_PER_BLOCK == 0 and begin_row % ROWS_PER_BLOCK == 0
     skip = begin_row // ROWS_PER_BLOCK
@@ -283,8 +305,8 @@
         functools.partial(localize_kernel, begin_row, cols, parts),
         grid=(rows // ROWS_PER_BLOCK,),
         out_shape=(half, half),
-        in_specs=[scalars] * 2 + [pl.BlockSpec(memory_space=pl.ANY)] * sum(parts) + [vector, vector,
-                  pl.BlockSpec((1, levels, chunk), lambda i: (0, 0, i + skip))],
+        in_specs=[scalars] * 2 + [pl.BlockSpec(memory_space=pl.ANY)] * sum(parts)
+        + [vector, pl.BlockSpec((levels, chunk), lambda i: (0, i + skip))],
         out_specs=(half_spec, half_spec),
         scratch_shapes=[
             pltpu.VMEM((levels, chunk + group * LANES), jnp.float32),
@@ -294,9 +316,9 @@
             ),
             pltpu.SemaphoreType.DMA((sum(parts),)),
         ],
-        compiler_params=pltpu.CompilerParams(vmem_limit_bytes=16 << 20),
+        compiler_params=pltpu.CompilerParams(vmem_limit_bytes=8 << 20),
         name="localize",
-    )(place, tile_widths, *sum(map(list, arrived), []), weight, order, perturbations)
+    )(place, tile_widths, *sum(map(list, arrived), []), weight, ordered)
 
 
 def body(
@@ -344,6 +366,7 @@
     half = (mem // (CORES * RING) + slot // 2) % HALVES
     row_level = half * 16 + ring * 4 + core * 2 + slot % 2
     order = (row_level[:, None] == slot[None, :]).astype(jnp.bfloat16)
+    ordered = reorder(order, perturbations)
     row_band = jnp.sum(jnp.where(row_level[:, None] == slot[None, :], band_widths[None, :], 0), 1)
     at = jnp.arange(tiles)
     near = (place[0] // LINE - at // LINE) % groups * LINE + (place[0] - at) % LINE
@@ -363,9 +386,7 @@
     results = []
     begin = 0
     for rows_here in PIECES:
-        own, other = localize(
-            begin, rows_here, cols, place, tile_widths, inputs, weight, order, perturbations
-        )
+        own, other = localize(begin, rows_here, cols, place, tile_widths, inputs, weight, ordered)
         results.append(sum_members(own, other))
         begin += rows_here
     return jnp.concatenate(results, axis=1)
@@ -391,12 +412,15 @@
     came = lax.ppermute(other, "mem", moved(0, (0, 0), 1))
     mine = wide(own[:keep]) + wide(came[:keep])
     gone = narrow(wide(own[keep:]) + wide(came[keep:]))
-    mine = mine + wide(lax.ppermute(gone, "mem", moved(0, (1, 3), 0)))
+    got = lax.ppermute(gone, "mem", moved(0, (1, 3), 0))
+    mine = mine + wide(got)
     keep //= 2
-    beside = lax.ppermute(narrow(mine[keep:]), "mem", moved(0, (3, 1), 0))
+    narrowed = narrow(mine[keep:])
+    beside = lax.ppermute(narrowed, "mem", moved(0, (3, 1), 0))
     total = mine[:keep] + wide(beside)
     keep //= HALVES
-    far = lax.ppermute(narrow(total[keep:]), "mem", moved(1, (0, 0), 0))
+    narrowed = narrow(total[keep:])
+    far = lax.ppermute(narrowed, "mem", moved(1, (0, 0), 0))
     return total[:keep] + wide(far)
 
 

time: 86.3 us -> 87.4 us (1.013)
  the two profiles are of different devices: /device:TPU:6 before, /device:TPU:32 now
where the time goes in v8:
time: 87.4 us; the launch traced here: 87 us
  starting transfers between devices  36.4 us (42%)
  Pallas kernels  25.4 us (29%)
  waiting for transfers between devices  18.4 us (21%)
  local copies, waits for them, and re-layouts  4.46 us (5%)
  other arithmetic  2.11 us (2%)
    pallas_call x2, Pallas kernels, smooth_and_cut(): pl.pallas_call(functools.partial(diffuse_kernel, level), out_shape=[jax.S...  18.6 us
    ppermute x3, waiting for transfers between devices, body(): one = lax.ppermute(one, 'lev', shifted(e, 0))  10.7 us
    ppermute x2, starting transfers between devices, sum_members(): far = lax.ppermute(narrowed, 'mem', moved(1, (0, 0), 0))  8.41 us
    all_to_all x1, starting transfers between devices, body(): lax.all_to_all(outgoing, 'lev', split_axis=0, concat_axis=0, tiled=True)  6.43 us
    ppermute x3, starting transfers between devices, body(): come.append(lax.ppermute(planes[d], 'lev', shifted(0, d)))  6.27 us
    ppermute x3, starting transfers between devices, body(): one = lax.ppermute(one, 'lev', shifted(e, 0))  5.84 us
    ppermute x2, starting transfers between devices, sum_members(): beside = lax.ppermute(narrowed, 'mem', moved(0, (3, 1), 0))  5.51 us
    ppermute x2, waiting for transfers between devices, sum_members(): far = lax.ppermute(narrowed, 'mem', moved(1, (0, 0), 0))  5.4 us
  transfers between devices with their start and end apart: 15, of which 5 were waited for; matrix products, arithmetic and copies ran while one was open for 5% of the time, Pallas kernels for 16%

profile of v8, /device:TPU:32, one launch (start us, length us, event | category | flops | bytes accessed | tf_op | source)
XLA Modules:
  0.0 87.0 jit_solution(8372739411094079170)
XLA Ops:
  0.0 9.3 %diffuse.2 = (bf16[4,8,3200]{2,1,0:T(8,128)(2,1)}, bf16[4,8,3200]{2,1,0:T(8,128)(2,1)}, bf16[4,8,3200]{2,1,0:T(8,128)(2,1)}, bf16[4,8,3200]{2,1,0:T(8,128)(2,1)}) custom-call(s32[1]{0:T(128)} %bitcast.place_ref, f32[32]{0:T(128)} %scale_ref.3, s32[32]{0:T(128)} %map_ref.3, s32[16]{0:T(128)} %width_ref.7, f32[1,2,384,512]{3,2,1,0:T(8,128)} %alpha_ref.3, ...), custom_call_target="tpu_custom_call" | custom-call | tf_op jit(solution)/shard_map/diffuse/pallas_call | solution.py:172
  9.3 1.9 %collective-permute-start.2 = (bf16[4,8,3200]{2,1,0:T(8,128)(2,1)}, bf16[4,8,3200]{2,1,0:T(8,128)(2,1)S(1)}, u32[]{:S(2)}, u32[]{:S(2)}) collective-permute-start(bf16[4,8,3200]{2,1,0:T(8,128)(2,1)} %get-tuple-element.16), channel_id=1, source_target_pairs={{0,3},{1,0},{2,1},{3,2},{4,7},{5,4},{6,5},{7,6},{8,11},{9,8},{10,9... | collective-permute-start | bytes 614408 | tf_op jit(solution)/shard_map/ppermute | solution.py:351
  11.2 1.6 %collective-permute-start.1 = (bf16[4,8,3200]{2,1,0:T(8,128)(2,1)}, bf16[4,8,3200]{2,1,0:T(8,128)(2,1)}, u32[]{:S(2)}, u32[]{:S(2)}) collective-permute-start(bf16[4,8,3200]{2,1,0:T(8,128)(2,1)} %get-tuple-element.15), channel_id=1, source_target_pairs={{0,2},{1,3},{2,0},{3,1},{4,6},{5,7},{6,4},{7,5},{8,10},{9,11},{10,... | collective-permute-start | bytes 614408 | tf_op jit(solution)/shard_map/ppermute | solution.py:351
  12.8 2.8 %collective-permute-start = (bf16[4,8,3200]{2,1,0:T(8,128)(2,1)}, bf16[4,8,3200]{2,1,0:T(8,128)(2,1)}, u32[]{:S(2)}, u32[]{:S(2)}) collective-permute-start(bf16[4,8,3200]{2,1,0:T(8,128)(2,1)} %get-tuple-element.14), channel_id=1, source_target_pairs={{0,1},{1,2},{2,3},{3,0},{4,5},{5,6},{6,7},{7,4},{8,9},{9,10},{10,1... | collective-permute-start | bytes 614408 | tf_op jit(solution)/shard_map/ppermute | solution.py:351
  15.6 9.3 %diffuse.3 = bf16[16,8,3200]{2,1,0:T(8,128)(2,1)} custom-call(s32[1]{0:T(128)} %bitcast.place_ref, f32[32]{0:T(128)} %scale_ref.3, s32[32]{0:T(128)} %map_ref.3, s32[16]{0:T(128)} %width_ref.7, f32[1,2,384,512]{3,2,1,0:T(8,128)} %alpha_ref.3, f32[384,512]{1,0:T(8,128)} %cx_ref.3, f32[384,512]{1,0:T(8,128)} %cy_ref.3), custom_call_target="tpu_custom_call" | custom-call | tf_op jit(solution)/shard_map/diffuse/pallas_call | solution.py:172
  24.9 0.0 copy-start.3
  25.0 6.4 %all-to-all-start = ((bf16[16,8,3200]{2,1,0:T(8,128)(2,1)}), bf16[16,8,3200]{2,1,0:T(8,128)(2,1)S(1)}, u32[]{:S(2)}, u32[]{:S(2)}) async-start(bf16[16,8,3200]{2,1,0:T(8,128)(2,1)} %diffuse.3), calls=%async_computation | async-start | bytes 1638400 | tf_op jit(solution)/shard_map/all_to_all | solution.py:353
  31.5 0.2 select_reduce_fusion.2
  31.8 0.1 fusion.3.order_ref
  31.8 0.2 select_reduce_fusion.1
  32.0 0.2 select_reduce_fusion
  32.2 0.1 fusion.2
  32.3 0.1 broadcast_in_dim.82
  32.4 0.4 broadcast_in_dim.83
  32.8 0.1 copy.12
  32.9 0.1 broadcast_in_dim.73
  33.0 0.2 broadcast_in_dim.74
  33.2 0.1 copy.11
  33.4 1.4 %copy-done = bf16[1,32,24576]{2,1,0:T(8,128)(2,1)S(1)} copy-done((bf16[1,32,24576]{2,1,0:T(8,128)(2,1)S(1)}, bf16[1,32,24576]{2,1,0:T(8,128)(2,1)}, u32[]{:S(2)}) %copy-start) | copy-done | bytes 1572888
  34.8 1.5 %reorder.1.refs_6_ = bf16[32,24576]{1,0:T(8,128)(2,1)S(1)} custom-call(bf16[32,32]{1,0:T(8,128)(2,1)S(1)} %fusion.3.order_ref, bf16[1,32,24576]{2,1,0:T(8,128)(2,1)S(1)} %copy-done), custom_call_target="tpu_custom_call" | custom-call | tf_op jit(solution)/shard_map/reorder/pallas_call | solution.py:209
  36.3 0.0 copy-start.1
  36.4 0.9 %slice_bitcast_fusion.1 = (bf16[8,3200]{1,0:T(8,128)(2,1)S(1)}, bf16[8,3200]{1,0:T(8,128)(2,1)S(1)}, bf16[8,3200]{1,0:T(8,128)(2,1)S(1)}, bf16[8,3200]{1,0:T(8,128)(2,1)S(1)}) fusion(bf16[4,8,3200]{2,1,0:T(8,128)(2,1)} %collective-permute-done.1), kind=kLoop, calls=%fused_computation.19 | loop fusion | bytes 409600 | tf_op jit(solution)/shard_map/squeeze | solution.py:356
  37.3 0.9 %slice_bitcast_fusion.2 = (bf16[8,3200]{1,0:T(8,128)(2,1)S(1)}, bf16[8,3200]{1,0:T(8,128)(2,1)S(1)}, bf16[8,3200]{1,0:T(8,128)(2,1)S(1)}, bf16[8,3200]{1,0:T(8,128)(2,1)S(1)}) fusion(bf16[4,8,3200]{2,1,0:T(8,128)(2,1)} %collective-permute-done), kind=kLoop, calls=%fused_computation.20 | loop fusion | bytes 409600 | tf_op jit(solution)/shard_map/squeeze | solution.py:356
  38.2 1.5 %collective-permute-start.3 = (bf16[32,3200]{1,0:T(8,128)(2,1)S(1)}, bf16[32,3200]{1,0:T(8,128)(2,1)S(1)}, u32[]{:S(2)}, u32[]{:S(2)}) collective-permute-start(bf16[32,3200]{1,0:T(8,128)(2,1)S(1)} %pad_maximum_fusion.1), channel_id=1, source_target_pairs={{0,4},{1,5},{2,6},{3,7},{4,8},{5,9},{6,10},{7,11},{8,12},{9,13},{1... | collective-permute-start | bytes 614408 | tf_op jit(solution)/shard_map/ppermute | solution.py:358
  39.8 2.8 %collective-permute-start.4 = (bf16[32,3200]{1,0:T(8,128)(2,1)S(1)}, bf16[32,3200]{1,0:T(8,128)(2,1)S(1)}, u32[]{:S(2)}, u32[]{:S(2)}) collective-permute-start(bf16[32,3200]{1,0:T(8,128)(2,1)S(1)} %pad_maximum_fusion.2), channel_id=1, source_target_pairs={{0,8},{1,9},{2,10},{3,11},{4,12},{5,13},{6,14},{7,15},{8,0},{9,1},... | collective-permute-start | bytes 614408 | tf_op jit(solution)/shard_map/ppermute | solution.py:358
  42.5 1.5 %collective-permute-start.5 = (bf16[32,3200]{1,0:T(8,128)(2,1)S(1)}, bf16[32,3200]{1,0:T(8,128)(2,1)S(1)}, u32[]{:S(2)}, u32[]{:S(2)}) collective-permute-start(bf16[32,3200]{1,0:T(8,128)(2,1)S(1)} %pad_maximum_fusion.3), channel_id=1, source_target_pairs={{0,12},{1,13},{2,14},{3,15},{4,0},{5,1},{6,2},{7,3},{8,4},{9,5},{1... | collective-permute-start | bytes 614408 | tf_op jit(solution)/shard_map/ppermute | solution.py:358
  44.1 6.1 %collective-permute-done.3.refs_1_ = bf16[32,3200]{1,0:T(8,128)(2,1)S(1)} collective-permute-done((bf16[32,3200]{1,0:T(8,128)(2,1)S(1)}, bf16[32,3200]{1,0:T(8,128)(2,1)S(1)}, u32[]{:S(2)}, u32[]{:S(2)}) %collective-permute-start.3) | collective-permute-done | bytes 204832 | tf_op jit(solution)/shard_map/ppermute | solution.py:358
  50.2 4.6 %collective-permute-done.4.refs_2_ = bf16[32,3200]{1,0:T(8,128)(2,1)S(1)} collective-permute-done((bf16[32,3200]{1,0:T(8,128)(2,1)S(1)}, bf16[32,3200]{1,0:T(8,128)(2,1)S(1)}, u32[]{:S(2)}, u32[]{:S(2)}) %collective-permute-start.4) | collective-permute-done | bytes 204832 | tf_op jit(solution)/shard_map/ppermute | solution.py:358
  54.8 2.0 %localize.3 = (bf16[16,8192]{1,0:T(8,128)(2,1)S(1)}, bf16[16,8192]{1,0:T(8,128)(2,1)S(1)}) custom-call(s32[1]{0:T(128)} %bitcast.place_ref, s32[16]{0:T(128)S(1)} %copy-done.1, bf16[32,3200]{1,0:T(8,128)(2,1)S(1)} %pad_maximum_fusion.refs_0_, bf16[32,3200]{1,0:T(8,128)(2,1)S(1)} %collective-permute-done.3.refs_1_, ...), custom_call_target="tpu_custom_call" | custom-call | tf_op jit(solution)/shard_map/localize/pallas_call | solution.py:304
  56.8 0.3 collective-permute-start.10
  57.1 3.3 %localize.2 = (bf16[16,16384]{1,0:T(8,128)(2,1)S(1)}, bf16[16,16384]{1,0:T(8,128)(2,1)S(1)}) custom-call(s32[1]{0:T(128)} %bitcast.place_ref, s32[16]{0:T(128)S(1)} %copy-done.1, bf16[32,3200]{1,0:T(8,128)(2,1)S(1)} %pad_maximum_fusion.refs_0_, bf16[32,3200]{1,0:T(8,128)(2,1)S(1)} %collective-permute-done.3.refs_1_, ...), custom_call_target="tpu_custom_call" | custom-call | tf_op jit(solution)/shard_map/localize/pallas_call | solution.py:304
  60.4 0.6 collective-permute-start.6
  61.0 1.6 %collective-permute-start.11 = (bf16[8,8192]{1,0:T(8,128)(2,1)S(1)}, bf16[8,8192]{1,0:T(8,128)(2,1)S(1)}, u32[]{:S(2)}, u32[]{:S(2)}) collective-permute-start(bf16[8,8192]{1,0:T(8,128)(2,1)S(1)} %add_convert_fusion.1), channel_id=1, source_target_pairs={{0,32},{16,112},{32,0},{48,80},{64,96},{80,48},{96,64},{112,16},{1... | collective-permute-start | bytes 393224 | tf_op jit(solution)/shard_map/ppermute | solution.py:415
  62.6 0.1 add_convert_fusion
  62.6 1.5 %collective-permute-start.7 = (bf16[8,16384]{1,0:T(8,128)(2,1)S(1)}, bf16[8,16384]{1,0:T(8,128)(2,1)S(1)}, u32[]{:S(2)}, u32[]{:S(2)}) collective-permute-start(bf16[8,16384]{1,0:T(8,128)(2,1)S(1)} %add_convert_fusion), channel_id=1, source_target_pairs={{0,32},{16,112},{32,0},{48,80},{64,96},{80,48},{96,64},{112,16},{1... | collective-permute-start | bytes 786440 | tf_op jit(solution)/shard_map/ppermute | solution.py:415
  64.1 1.9 %collective-permute-done.11 = bf16[8,8192]{1,0:T(8,128)(2,1)S(1)} collective-permute-done((bf16[8,8192]{1,0:T(8,128)(2,1)S(1)}, bf16[8,8192]{1,0:T(8,128)(2,1)S(1)}, u32[]{:S(2)}, u32[]{:S(2)}) %collective-permute-start.11) | collective-permute-done | bytes 131104 | tf_op jit(solution)/shard_map/ppermute | solution.py:415
  66.1 2.8 %collective-permute-start.12 = (bf16[4,8192]{1,0:T(4,128)(2,1)S(1)}, bf16[4,8192]{1,0:T(4,128)(2,1)S(1)}, u32[]{:S(2)}, u32[]{:S(2)}) collective-permute-start(bf16[4,8192]{1,0:T(4,128)(2,1)S(1)} %slice.189), channel_id=1, source_target_pairs={{0,96},{16,48},{32,64},{48,16},{64,32},{80,112},{96,0},{112,80},{1... | collective-permute-start | bytes 196616 | tf_op jit(solution)/shard_map/ppermute | solution.py:419
  69.0 0.3 collective-permute-done.7
  69.3 0.1 convert_add_fusion
  69.4 0.1 slice.188
  69.4 2.7 %collective-permute-start.8 = (bf16[4,16384]{1,0:T(4,128)(2,1)S(1)}, bf16[4,16384]{1,0:T(4,128)(2,1)S(1)}, u32[]{:S(2)}, u32[]{:S(2)}) collective-permute-start(bf16[4,16384]{1,0:T(4,128)(2,1)S(1)} %slice.188), channel_id=1, source_target_pairs={{0,96},{16,48},{32,64},{48,16},{64,32},{80,112},{96,0},{112,80},{1... | collective-permute-start | bytes 393224 | tf_op jit(solution)/shard_map/ppermute | solution.py:419
  72.2 4.9 %collective-permute-start.13 = (bf16[2,8192]{1,0:T(2,128)(2,1)S(1)}, bf16[2,8192]{1,0:T(2,128)(2,1)S(1)}, u32[]{:S(2)}, u32[]{:S(2)}) collective-permute-start(bf16[2,8192]{1,0:T(2,128)(2,1)S(1)} %slice.191), channel_id=1, source_target_pairs={{0,128},{16,144},{32,160},{48,176},{64,192},{80,208},{96,224},{112... | collective-permute-start | bytes 98312 | tf_op jit(solution)/shard_map/ppermute | solution.py:423
  77.1 0.1 slice_add_fusion
  77.2 0.1 slice.190
  77.2 3.5 %collective-permute-start.9 = (bf16[2,16384]{1,0:T(2,128)(2,1)S(1)}, bf16[2,16384]{1,0:T(2,128)(2,1)S(1)}, u32[]{:S(2)}, u32[]{:S(2)}) collective-permute-start(bf16[2,16384]{1,0:T(2,128)(2,1)S(1)} %slice.190), channel_id=1, source_target_pairs={{0,128},{16,144},{32,160},{48,176},{64,192},{80,208},{96,224},{112... | collective-permute-start | bytes 196616 | tf_op jit(solution)/shard_map/ppermute | solution.py:423
  80.8 5.4 %collective-permute-done.9 = bf16[2,16384]{1,0:T(2,128)(2,1)S(1)} collective-permute-done((bf16[2,16384]{1,0:T(2,128)(2,1)S(1)}, bf16[2,16384]{1,0:T(2,128)(2,1)S(1)}, u32[]{:S(2)}, u32[]{:S(2)}) %collective-permute-start.9) | collective-permute-done | bytes 65568 | tf_op jit(solution)/shard_map/ppermute | solution.py:423
  86.2 0.1 slice_add_fusion.2
  86.3 0.8 pad_maximum_fusion.4
  (35 shorter events, 0.5 us)
Async XLA Ops:
  9.3 27.0 %collective-permute-start.2 = (bf16[4,8,3200]{2,1,0:T(8,128)(2,1)}, bf16[4,8,3200]{2,1,0:T(8,128)(2,1)S(1)}, u32[]{:S(2)}, u32[]{:S(2)}) collective-permute-start(bf16[4,8,3200]{2,1,0:T(8,128)(2,1)} %get-tuple-element.16), channel_id=1, source_target_pairs={{0,3},{1,0},{2,1},{3,2},{4,7},{5,4},{6,5},{7,6},{8,11},{9,8},{10,9... | collective-permute-start | bytes 614408 | tf_op jit(solution)/shard_map/ppermute | solution.py:351
  11.2 25.1 %collective-permute-start.1 = (bf16[4,8,3200]{2,1,0:T(8,128)(2,1)}, bf16[4,8,3200]{2,1,0:T(8,128)(2,1)}, u32[]{:S(2)}, u32[]{:S(2)}) collective-permute-start(bf16[4,8,3200]{2,1,0:T(8,128)(2,1)} %get-tuple-element.15), channel_id=1, source_target_pairs={{0,2},{1,3},{2,0},{3,1},{4,6},{5,7},{6,4},{7,5},{8,10},{9,11},{10,... | collective-permute-start | bytes 614408 | tf_op jit(solution)/shard_map/ppermute | solution.py:351
  12.8 24.5 %collective-permute-start = (bf16[4,8,3200]{2,1,0:T(8,128)(2,1)}, bf16[4,8,3200]{2,1,0:T(8,128)(2,1)}, u32[]{:S(2)}, u32[]{:S(2)}) collective-permute-start(bf16[4,8,3200]{2,1,0:T(8,128)(2,1)} %get-tuple-element.14), channel_id=1, source_target_pairs={{0,1},{1,2},{2,3},{3,0},{4,5},{5,6},{6,7},{7,4},{8,9},{9,10},{10,1... | collective-permute-start | bytes 614408 | tf_op jit(solution)/shard_map/ppermute | solution.py:351
  24.9 6.5 %copy-start.2 = (bf16[4,8,3200]{2,1,0:T(8,128)(2,1)S(1)}, bf16[4,8,3200]{2,1,0:T(8,128)(2,1)}, u32[]{:S(2)}) copy-start(bf16[4,8,3200]{2,1,0:T(8,128)(2,1)} %get-tuple-element.13) | copy-start | bytes 614404
  24.9 6.6 %copy-start.3 = (s32[32]{0:T(128)S(1)}, s32[32]{0:T(128)}, u32[]{:S(2)}) copy-start(s32[32]{0:T(128)} %map_ref.3) | copy-start | bytes 388
  25.0 6.9 %copy-start.4 = (s32[32]{0:T(128)S(1)}, s32[32]{0:T(128)}, u32[]{:S(2)}) copy-start(s32[32]{0:T(128)} %param.15) | copy-start | bytes 388
  25.0 29.9 %all-to-all-start = ((bf16[16,8,3200]{2,1,0:T(8,128)(2,1)}), bf16[16,8,3200]{2,1,0:T(8,128)(2,1)S(1)}, u32[]{:S(2)}, u32[]{:S(2)}) async-start(bf16[16,8,3200]{2,1,0:T(8,128)(2,1)} %diffuse.3), calls=%async_computation | async-start | bytes 1638400 | tf_op jit(solution)/shard_map/all_to_all | solution.py:353
  33.4 1.4 %copy-start = (bf16[1,32,24576]{2,1,0:T(8,128)(2,1)S(1)}, bf16[1,32,24576]{2,1,0:T(8,128)(2,1)}, u32[]{:S(2)}) copy-start(bf16[1,32,24576]{2,1,0:T(8,128)(2,1)} %pert_ref.1) | copy-start | bytes 4718596
  36.3 18.6 %copy-start.1 = (s32[16]{0:T(128)S(1)}, s32[16]{0:T(128)}, u32[]{:S(2)}) copy-start(s32[16]{0:T(128)} %width_ref.7) | copy-start | bytes 196
  38.2 12.0 %collective-permute-start.3 = (bf16[32,3200]{1,0:T(8,128)(2,1)S(1)}, bf16[32,3200]{1,0:T(8,128)(2,1)S(1)}, u32[]{:S(2)}, u32[]{:S(2)}) collective-permute-start(bf16[32,3200]{1,0:T(8,128)(2,1)S(1)} %pad_maximum_fusion.1), channel_id=1, source_target_pairs={{0,4},{1,5},{2,6},{3,7},{4,8},{5,9},{6,10},{7,11},{8,12},{9,13},{1... | collective-permute-start | bytes 614408 | tf_op jit(solution)/shard_map/ppermute | solution.py:358
  39.8 15.1 %collective-permute-start.4 = (bf16[32,3200]{1,0:T(8,128)(2,1)S(1)}, bf16[32,3200]{1,0:T(8,128)(2,1)S(1)}, u32[]{:S(2)}, u32[]{:S(2)}) collective-permute-start(bf16[32,3200]{1,0:T(8,128)(2,1)S(1)} %pad_maximum_fusion.2), channel_id=1, source_target_pairs={{0,8},{1,9},{2,10},{3,11},{4,12},{5,13},{6,14},{7,15},{8,0},{9,1},... | collective-permute-start | bytes 614408 | tf_op jit(solution)/shard_map/ppermute | solution.py:358
  42.5 12.3 %collective-permute-start.5 = (bf16[32,3200]{1,0:T(8,128)(2,1)S(1)}, bf16[32,3200]{1,0:T(8,128)(2,1)S(1)}, u32[]{:S(2)}, u32[]{:S(2)}) collective-permute-start(bf16[32,3200]{1,0:T(8,128)(2,1)S(1)} %pad_maximum_fusion.3), channel_id=1, source_target_pairs={{0,12},{1,13},{2,14},{3,15},{4,0},{5,1},{6,2},{7,3},{8,4},{9,5},{1... | collective-permute-start | bytes 614408 | tf_op jit(solution)/shard_map/ppermute | solution.py:358
  56.8 4.1 %collective-permute-start.10 = (bf16[16,8192]{1,0:T(8,128)(2,1)S(1)}, bf16[16,8192]{1,0:T(8,128)(2,1)S(1)}, u32[]{:S(2)}, u32[]{:S(2)}) collective-permute-start(bf16[16,8192]{1,0:T(8,128)(2,1)S(1)} %get-tuple-element.20), channel_id=1, source_target_pairs={{0,16},{16,0},{32,48},{48,32},{64,80},{80,64},{96,112},{112,96},{1... | collective-permute-start | bytes 786440 | tf_op jit(solution)/shard_map/ppermute | solution.py:412
  60.4 2.2 %collective-permute-start.6 = (bf16[16,16384]{1,0:T(8,128)(2,1)S(1)}, bf16[16,16384]{1,0:T(8,128)(2,1)S(1)}, u32[]{:S(2)}, u32[]{:S(2)}) collective-permute-start(bf16[16,16384]{1,0:T(8,128)(2,1)S(1)} %get-tuple-element.18), channel_id=1, source_target_pairs={{0,16},{16,0},{32,48},{48,32},{64,80},{80,64},{96,112},{112,96},{1... | collective-permute-start | bytes 1572872 | tf_op jit(solution)/shard_map/ppermute | solution.py:412
  61.0 5.1 %collective-permute-start.11 = (bf16[8,8192]{1,0:T(8,128)(2,1)S(1)}, bf16[8,8192]{1,0:T(8,128)(2,1)S(1)}, u32[]{:S(2)}, u32[]{:S(2)}) collective-permute-start(bf16[8,8192]{1,0:T(8,128)(2,1)S(1)} %add_convert_fusion.1), channel_id=1, source_target_pairs={{0,32},{16,112},{32,0},{48,80},{64,96},{80,48},{96,64},{112,16},{1... | collective-permute-start | bytes 393224 | tf_op jit(solution)/shard_map/ppermute | solution.py:415
  62.6 6.6 %collective-permute-start.7 = (bf16[8,16384]{1,0:T(8,128)(2,1)S(1)}, bf16[8,16384]{1,0:T(8,128)(2,1)S(1)}, u32[]{:S(2)}, u32[]{:S(2)}) collective-permute-start(bf16[8,16384]{1,0:T(8,128)(2,1)S(1)} %add_convert_fusion), channel_id=1, source_target_pairs={{0,32},{16,112},{32,0},{48,80},{64,96},{80,48},{96,64},{112,16},{1... | collective-permute-start | bytes 786440 | tf_op jit(solution)/shard_map/ppermute | solution.py:415
  66.1 6.0 %collective-permute-start.12 = (bf16[4,8192]{1,0:T(4,128)(2,1)S(1)}, bf16[4,8192]{1,0:T(4,128)(2,1)S(1)}, u32[]{:S(2)}, u32[]{:S(2)}) collective-permute-start(bf16[4,8192]{1,0:T(4,128)(2,1)S(1)} %slice.189), channel_id=1, source_target_pairs={{0,96},{16,48},{32,64},{48,16},{64,32},{80,112},{96,0},{112,80},{1... | collective-permute-start | bytes 196616 | tf_op jit(solution)/shard_map/ppermute | solution.py:419
  69.4 7.7 %collective-permute-start.8 = (bf16[4,16384]{1,0:T(4,128)(2,1)S(1)}, bf16[4,16384]{1,0:T(4,128)(2,1)S(1)}, u32[]{:S(2)}, u32[]{:S(2)}) collective-permute-start(bf16[4,16384]{1,0:T(4,128)(2,1)S(1)} %slice.188), channel_id=1, source_target_pairs={{0,96},{16,48},{32,64},{48,16},{64,32},{80,112},{96,0},{112,80},{1... | collective-permute-start | bytes 393224 | tf_op jit(solution)/shard_map/ppermute | solution.py:419
  72.2 8.6 %collective-permute-start.13 = (bf16[2,8192]{1,0:T(2,128)(2,1)S(1)}, bf16[2,8192]{1,0:T(2,128)(2,1)S(1)}, u32[]{:S(2)}, u32[]{:S(2)}) collective-permute-start(bf16[2,8192]{1,0:T(2,128)(2,1)S(1)} %slice.191), channel_id=1, source_target_pairs={{0,128},{16,144},{32,160},{48,176},{64,192},{80,208},{96,224},{112... | collective-permute-start | bytes 98312 | tf_op jit(solution)/shard_map/ppermute | solution.py:423
  77.2 9.0 %collective-permute-start.9 = (bf16[2,16384]{1,0:T(2,128)(2,1)S(1)}, bf16[2,16384]{1,0:T(2,128)(2,1)S(1)}, u32[]{:S(2)}, u32[]{:S(2)}) collective-permute-start(bf16[2,16384]{1,0:T(2,128)(2,1)S(1)} %slice.190), channel_id=1, source_target_pairs={{0,128},{16,144},{32,160},{48,176},{64,192},{80,208},{96,224},{112... | collective-permute-start | bytes 196616 | tf_op jit(solution)/shard_map/ppermute | solution.py:423
